TPU v7x, 256 devices: a whole 4x4x8 slice. The times are simulated.
256 devices in a mesh: region: 8 (over y_hi, x), blk: 32 (over z, y_lo, core).
Axes of the slice: x: 4, y: 4 (y_hi: 2, y_lo: 2; y = y_hi * 2 + y_lo), z: 8, core: 2. Of those that a mesh axis runs over, the one named last changes fastest.
Arguments:
- probes: bfloat16 [2, 16, 131072], P(None, None, ('region', 'blk')), may hold values from -6 to 6
- near_blocks: bfloat16 [3, 2, 131072, 512], P(None, None, ('region', 'blk')), may hold values from -0.078125 to 0.078125
- inner_basis: bfloat16 [2, 64, 131072], P(None, None, ('region', 'blk')), may hold values from -0.1875 to 0.1875
- coupling: bfloat16 [2, 16384, 2048], P(None, ('region', 'blk')), may hold values from -0.09375 to 0.09375
- inner_expand: bfloat16 [2, 64, 131072], P(None, None, ('region', 'blk')), may hold values from -0.25 to 0.25
- outer_basis: bfloat16 [2, 256, 131072], P(None, None, ('region', 'blk')), may hold values from -0.1875 to 0.1875
- group_coupling: bfloat16 [2, 2048, 2048], P(None, 'region'), may hold values from -0.015625 to 0.015625
- outer_expand: bfloat16 [2, 256, 131072], P(None, None, ('region', 'blk')), may hold values from -0.125 to 0.125
- ranks: int32 [256], P(('region', 'blk')), may hold values from 8 to 64, as said below
Outputs:
- first: float32 [2, 16, 131072], P(None, None, ('region', 'blk'))
- second: float32 [2, 16, 131072], P(None, None, ('region', 'blk'))
Inputs may be any that keep to these rules, and one draw needn't show every extreme that they name: `ranks`: some cluster has rank 64.
All inputs are finite; a program needn't handle non-finite values.
Results may differ from a plain program's by a relative error of at most 0.004.
Values may be sent and summed in bfloat16 or wider, within the bound.
No kernel may reach another device: no remote copies, remote signals or barrier semaphores. Data moves between devices by JAX's collectives and lax.ppermute only.
A program may use at most 64 MiB of HBM per device.

v0:
```python
import jax
import jax.numpy as jnp
from jax import lax
from jax.sharding import PartitionSpec as P


def padded_2(value, sides, width):
    for axis, dim in sides:
        devices, length = (lax.axis_size(axis), value.shape[dim])
        up = [(i, (i + 1) % devices) for i in range(devices - 1)]
        down = [(j, i) for i, j in up]
        last = lax.slice_in_dim(value, length - width, length, axis=dim)
        leading = lax.slice_in_dim(value, 0, width, axis=dim)
        before = lax.ppermute(last, axis, up)
        after = lax.ppermute(leading, axis, down)
        value = jnp.concatenate([before, value, after], axis=dim)
    return value


def in_order(tiles, dim):
    dims = list(tiles.shape[1:])
    dims[dim] *= tiles.shape[0]
    return jnp.moveaxis(tiles, 0, dim).reshape(dims)


def copy_for_each(value, axis):
    copies = jnp.broadcast_to(value, (lax.axis_size(axis), *value.shape))
    return lax.all_to_all(copies, axis, split_axis=0, concat_axis=0, tiled=True)


def gathered_copies(value, axis, dim):
    return in_order(copy_for_each(value, axis), dim)


def of_everyone(value, axis):
    everything = copy_for_each(value, axis)
    return jnp.sum(everything, axis=0)


def dots(vec, mat):
    return jnp.dot(vec, mat.T, preferred_element_type=jnp.float32)


def cmul(mat, vec):
    real = dots(vec[0], mat[0]) - dots(vec[1], mat[1])
    imag = dots(vec[1], mat[0]) + dots(vec[0], mat[1])
    return jnp.stack([real, imag])


def cexpand(vec, mat):
    real = jnp.dot(vec[0], mat[0], preferred_element_type=jnp.float32) - jnp.dot(
        vec[1], mat[1], preferred_element_type=jnp.float32
    )
    imag = jnp.dot(vec[1], mat[0], preferred_element_type=jnp.float32) + jnp.dot(
        vec[0], mat[1], preferred_element_type=jnp.float32
    )
    return jnp.stack([real, imag])


def cmul_high(mat, vec):
    high = lax.Precision.HIGHEST
    real = jnp.dot(vec[0], mat[0].T, precision=high) - jnp.dot(vec[1], mat[1].T, precision=high)
    imag = jnp.dot(vec[1], mat[0].T, precision=high) + jnp.dot(vec[0], mat[1].T, precision=high)
    return jnp.stack([real, imag])


def apply_operator(
    vec,
    near_blocks,
    inner_basis,
    coupling,
    inner_expand,
    outer_basis,
    group_coupling,
    outer_expand,
    ranks,
):
    width = vec.shape[2]
    rank_cap = inner_basis.shape[1]
    group_rank = outer_basis.shape[1]
    position = lax.axis_index("blk")
    region_index = lax.axis_index("region")
    padded = padded_2(vec, (("blk", 2),), width)
    near = (
        cmul(near_blocks[0], padded[:, :, :width])
        + cmul(near_blocks[1], vec)
        + cmul(near_blocks[2], padded[:, :, 2 * width :])
    )
    keep = jnp.arange(rank_cap, dtype=jnp.int32) < ranks[0]
    coeff = cmul(inner_basis, vec)
    coeff = jnp.where(keep[None, None, :], coeff, jnp.zeros_like(coeff)).astype(jnp.bfloat16)
    piece = gathered_copies(coeff, "blk", 2)
    columns = piece.shape[2]
    owners = jnp.arange(columns, dtype=jnp.int32) // rank_cap
    distant = jnp.abs(owners - position) > 1
    piece = jnp.where(distant[None, None, :], piece, jnp.zeros_like(piece))
    rows = coupling
    inner = cmul(rows, piece).astype(jnp.bfloat16)
    wide = cmul(outer_basis, vec)
    group_total = of_everyone(wide, "blk")
    piece = gathered_copies(group_total, "region", 2)
    columns = piece.shape[2]
    owners = jnp.arange(columns, dtype=jnp.int32) // group_rank
    others = owners != region_index
    piece = jnp.where(others[None, None, :], piece, jnp.zeros_like(piece))
    rows = group_coupling.astype(jnp.float32)
    field = cmul_high(rows, piece)
    field = field.astype(jnp.bfloat16)
    return near + cexpand(inner, inner_expand) + cexpand(field, outer_expand)


def local(
    probes,
    near_blocks,
    inner_basis,
    coupling,
    inner_expand,
    outer_basis,
    group_coupling,
    outer_expand,
    ranks,
):
    first = apply_operator(
        probes,
        near_blocks,
        inner_basis,
        coupling,
        inner_expand,
        outer_basis,
        group_coupling,
        outer_expand,
        ranks,
    )
    second = apply_operator(
        first.astype(jnp.bfloat16),
        near_blocks,
        inner_basis,
        coupling,
        inner_expand,
        outer_basis,
        group_coupling,
        outer_expand,
        ranks,
    )
    return (first, second)


def solution(mesh):
    placed = (
        P(None, None, ("region", "blk")),
        P(None, None, ("region", "blk"), None),
        P(None, None, ("region", "blk")),
        P(None, ("region", "blk"), None),
        P(None, None, ("region", "blk")),
        P(None, None, ("region", "blk")),
        P(None, "region", None),
        P(None, None, ("region", "blk")),
        P(("region", "blk")),
    )
    return jax.shard_map(
        local,
        mesh=mesh,
        in_specs=placed,
        out_specs=(P(None, None, ("region", "blk")), P(None, None, ("region", "blk"))),
        check_vma=False,
    )
```

profile of v0, /device:TPU:32, one launch (start us, length us, event | category | flops | bytes accessed | tf_op | source)
XLA Modules:
  0.0 178.8 jit_solution(4971559892409348065)
XLA Ops:
  0.7 2.7 %collective-permute-start.1 = (bf16[2,16,512]{2,1,0:T(8,128)(2,1)}, bf16[2,16,512]{2,1,0:T(8,128)(2,1)S(1)}, u32[]{:S(2)}, u32[]{:S(2)}) collective-permute-start(bf16[2,16,512]{2,1,0:T(8,128)(2,1)} %param.9), channel_id=1, source_target_pairs={{1,0},{2,1},{3,2},{4,3},{5,4},{6,5},{7,6},{8,7},{9,8},{10,9},{11,1... | collective-permute-start | bytes 98312 | tf_op jit(solution)/shard_map/ppermute | solution.py:15
  3.4 1.9 %collective-permute-start = (bf16[2,16,512]{2,1,0:T(8,128)(2,1)}, bf16[2,16,512]{2,1,0:T(8,128)(2,1)S(1)}, u32[]{:S(2)}, u32[]{:S(2)}) collective-permute-start(bf16[2,16,512]{2,1,0:T(8,128)(2,1)} %param.9), channel_id=1, source_target_pairs={{0,1},{1,2},{2,3},{3,4},{4,5},{5,6},{6,7},{7,8},{8,9},{9,10},{10,1... | collective-permute-start | bytes 98312 | tf_op jit(solution)/shard_map/ppermute | solution.py:14
  10.9 11.3 %all-to-all-start = ((bf16[32,2,1024]{2,1,0:T(2,128)(2,1)}), bf16[32,2,1024]{2,1,0:T(2,128)(2,1)S(1)}, u32[]{:S(2)}, u32[]{:S(2)}) async-start(bf16[32,2,1024]{2,1,0:T(2,128)(2,1)} %reshape.73), calls=%async_computation | async-start | bytes 262144 | tf_op jit(solution)/shard_map/all_to_all | solution.py:28
  23.3 1.2 fusion.138
  24.4 1.3 fusion.76
  25.7 1.3 fusion.78
  35.0 8.3 %all-to-all-start.1 = ((f32[32,2,16,256]{3,2,1,0:T(8,128)}), f32[32,2,16,256]{3,2,1,0:T(8,128)}, u32[]{:S(2)}, u32[]{:S(2)}) async-start(f32[32,2,16,256]{3,2,1,0:T(8,128)} %broadcast_in_dim.61), calls=%async_computation.1 | async-start | bytes 2097152 | tf_op jit(solution)/shard_map/all_to_all | solution.py:28
  47.0 1.2 reshape.69
  49.4 1.1 fusion.32
  54.3 17.1 %all-to-all-done.1 = f32[32,2,16,256]{3,2,1,0:T(8,128)} async-done(((f32[32,2,16,256]{3,2,1,0:T(8,128)}), f32[32,2,16,256]{3,2,1,0:T(8,128)}, u32[]{:S(2)}, u32[]{:S(2)}) %all-to-all-start.1) | async-done | bytes 1048608 | tf_op jit(solution)/shard_map/all_to_all | solution.py:28
  71.4 1.3 reduce_sum.18
  73.4 6.6 %all-to-all-start.2 = ((f32[8,2,16,256]{3,2,1,0:T(8,128)}), f32[8,2,16,256]{3,2,1,0:T(8,128)S(1)}, u32[]{:S(2)}, u32[]{:S(2)}) async-start(f32[8,2,16,256]{3,2,1,0:T(8,128)} %broadcast_in_dim.62), calls=%async_computation.2 | async-start | bytes 524288 | tf_op jit(solution)/shard_map/all_to_all | solution.py:28
  80.1 1.5 fusion.7
  81.6 1.5 fusion.6
  83.1 5.8 %all-to-all-done.2 = f32[8,2,16,256]{3,2,1,0:T(8,128)S(1)} async-done(((f32[8,2,16,256]{3,2,1,0:T(8,128)}), f32[8,2,16,256]{3,2,1,0:T(8,128)S(1)}, u32[]{:S(2)}, u32[]{:S(2)}) %all-to-all-start.2) | async-done | bytes 262176 | tf_op jit(solution)/shard_map/all_to_all | solution.py:28
  89.0 2.3 %fusion.46 = f32[16,256]{1,0:T(8,128)S(1)} fusion(bf16[2,256,2048]{2,1,0:T(8,128)(2,1)} %param.15, f32[2,16,2048]{2,1,0:T(8,128)S(1)} %broadcast_select_fusion.1), kind=kOutput, calls=%fused_computation.82 | convolution fusion | flops 100663296 | bytes 1196032 | tf_op jit(solution)/shard_map/dot_general | solution.py:62
  91.3 2.2 %fusion.44 = f32[16,256]{1,0:T(8,128)S(1)} fusion(bf16[2,256,2048]{2,1,0:T(8,128)(2,1)} %param.15, f32[2,16,2048]{2,1,0:T(8,128)S(1)} %broadcast_select_fusion.1), kind=kOutput, calls=%fused_computation.80 | convolution fusion | flops 100663296 | bytes 1196032 | tf_op jit(solution)/shard_map/dot_general | solution.py:63
  97.4 1.9 %collective-permute-start.3 = (bf16[2,16,512]{2,1,0:T(8,128)(2,1)S(1)}, bf16[2,16,512]{2,1,0:T(8,128)(2,1)S(1)}, u32[]{:S(2)}, u32[]{:S(2)}) collective-permute-start(bf16[2,16,512]{2,1,0:T(8,128)(2,1)S(1)} %get-tuple-element.2), channel_id=1, source_target_pairs={{1,0},{2,1},{3,2},{4,3},{5,4},{6,5},{7,6},{8,7},{9,8},{10,9},{11,1... | collective-permute-start | bytes 98312 | tf_op jit(solution)/shard_map/ppermute | solution.py:15
  100.4 2.4 %collective-permute-start.2 = (bf16[2,16,512]{2,1,0:T(8,128)(2,1)S(1)}, bf16[2,16,512]{2,1,0:T(8,128)(2,1)}, u32[]{:S(2)}, u32[]{:S(2)}) collective-permute-start(bf16[2,16,512]{2,1,0:T(8,128)(2,1)S(1)} %get-tuple-element.2), channel_id=1, source_target_pairs={{0,1},{1,2},{2,3},{3,4},{4,5},{5,6},{6,7},{7,8},{8,9},{9,10},{10,1... | collective-permute-start | bytes 98312 | tf_op jit(solution)/shard_map/ppermute | solution.py:14
  104.8 1.8 %reshape.75 = bf16[32,2,1024]{2,1,0:T(2,128)(2,1)} reshape(bf16[32,2,16,64]{3,2,1,0:T(8,128)(2,1)} %broadcast_in_dim.63) | data formatting | bytes 262144
  106.6 6.1 %all-to-all-start.3 = ((bf16[32,2,1024]{2,1,0:T(2,128)(2,1)}), bf16[32,2,1024]{2,1,0:T(2,128)(2,1)S(1)}, u32[]{:S(2)}, u32[]{:S(2)}) async-start(bf16[32,2,1024]{2,1,0:T(2,128)(2,1)} %reshape.75), calls=%async_computation.3 | async-start | bytes 262144 | tf_op jit(solution)/shard_map/all_to_all | solution.py:28
  113.9 1.3 pad_maximum_fusion.1
  117.1 1.6 fusion.82
  119.7 1.6 fusion.80
  121.6 1.9 %broadcast_in_dim.64 = f32[32,2,16,256]{3,2,1,0:T(8,128)} broadcast(f32[2,16,256]{2,1,0:T(8,128)} %pad_maximum_fusion.1), dimensions={1,2,3} | broadcast | bytes 1081344 | tf_op jit(solution)/shard_map/broadcast_in_dim | solution.py:27
  123.5 8.0 %all-to-all-start.4 = ((f32[32,2,16,256]{3,2,1,0:T(8,128)}), f32[32,2,16,256]{3,2,1,0:T(8,128)}, u32[]{:S(2)}, u32[]{:S(2)}) async-start(f32[32,2,16,256]{3,2,1,0:T(8,128)} %broadcast_in_dim.64), calls=%async_computation.4 | async-start | bytes 2097152 | tf_op jit(solution)/shard_map/all_to_all | solution.py:28
  131.4 1.6 fusion.13
  133.1 1.6 fusion.12
  140.2 19.3 %all-to-all-done.4 = f32[32,2,16,256]{3,2,1,0:T(8,128)} async-done(((f32[32,2,16,256]{3,2,1,0:T(8,128)}), f32[32,2,16,256]{3,2,1,0:T(8,128)}, u32[]{:S(2)}, u32[]{:S(2)}) %all-to-all-start.4) | async-done | bytes 1048608 | tf_op jit(solution)/shard_map/all_to_all | solution.py:28
  159.5 1.3 reduce_sum.19
  161.5 3.6 %all-to-all-start.5 = ((f32[8,2,16,256]{3,2,1,0:T(8,128)}), f32[8,2,16,256]{3,2,1,0:T(8,128)S(1)}, u32[]{:S(2)}, u32[]{:S(2)}) async-start(f32[8,2,16,256]{3,2,1,0:T(8,128)} %broadcast_in_dim.65), calls=%async_computation.5 | async-start | bytes 524288 | tf_op jit(solution)/shard_map/all_to_all | solution.py:28
  165.4 8.3 %all-to-all-done.5 = f32[8,2,16,256]{3,2,1,0:T(8,128)S(1)} async-done(((f32[8,2,16,256]{3,2,1,0:T(8,128)}), f32[8,2,16,256]{3,2,1,0:T(8,128)S(1)}, u32[]{:S(2)}, u32[]{:S(2)}) %all-to-all-start.5) | async-done | bytes 262176 | tf_op jit(solution)/shard_map/all_to_all | solution.py:28
  (145 shorter events, 46.0 us)
Async XLA Ops:
  0.6 27.6 %copy-start.8 = (bf16[2,16,512]{2,1,0:T(8,128)(2,1)S(1)}, bf16[2,16,512]{2,1,0:T(8,128)(2,1)}, u32[]{:S(2)}) copy-start(bf16[2,16,512]{2,1,0:T(8,128)(2,1)} %param.9) | copy-start | bytes 98308
  0.6 28.7 %copy-start = (bf16[3,2,512,512]{3,2,1,0:T(8,128)(2,1)S(1)}, bf16[3,2,512,512]{3,2,1,0:T(8,128)(2,1)}, u32[]{:S(2)}) copy-start(bf16[3,2,512,512]{3,2,1,0:T(8,128)(2,1)} %param.10) | copy-start | bytes 9437188
  0.7 30.5 %collective-permute-start.1 = (bf16[2,16,512]{2,1,0:T(8,128)(2,1)}, bf16[2,16,512]{2,1,0:T(8,128)(2,1)S(1)}, u32[]{:S(2)}, u32[]{:S(2)}) collective-permute-start(bf16[2,16,512]{2,1,0:T(8,128)(2,1)} %param.9), channel_id=1, source_target_pairs={{1,0},{2,1},{3,2},{4,3},{5,4},{6,5},{7,6},{8,7},{9,8},{10,9},{11,1... | collective-permute-start | bytes 98312 | tf_op jit(solution)/shard_map/ppermute | solution.py:15
  3.4 29.1 %collective-permute-start = (bf16[2,16,512]{2,1,0:T(8,128)(2,1)}, bf16[2,16,512]{2,1,0:T(8,128)(2,1)S(1)}, u32[]{:S(2)}, u32[]{:S(2)}) collective-permute-start(bf16[2,16,512]{2,1,0:T(8,128)(2,1)} %param.9), channel_id=1, source_target_pairs={{0,1},{1,2},{2,3},{3,4},{4,5},{5,6},{6,7},{7,8},{8,9},{9,10},{10,1... | collective-permute-start | bytes 98312 | tf_op jit(solution)/shard_map/ppermute | solution.py:14
  10.9 23.0 %all-to-all-start = ((bf16[32,2,1024]{2,1,0:T(2,128)(2,1)}), bf16[32,2,1024]{2,1,0:T(2,128)(2,1)S(1)}, u32[]{:S(2)}, u32[]{:S(2)}) async-start(bf16[32,2,1024]{2,1,0:T(2,128)(2,1)} %reshape.73), calls=%async_computation | async-start | bytes 262144 | tf_op jit(solution)/shard_map/all_to_all | solution.py:28
  27.1 21.1 %copy-start.23 = (pred[2048]{0:T(1024)(128)(4,1)}, pred[2048]{0:T(1024)(128)(4,1)S(1)}, u32[]{:S(2)}) copy-start(pred[2048]{0:T(1024)(128)(4,1)S(1)} %fusion.238) | copy-start | bytes 6148
  31.1 57.8 %copy-start.21 = (pred[2048]{0:T(1024)(128)(4,1)}, pred[2048]{0:T(1024)(128)(4,1)S(1)}, u32[]{:S(2)}) copy-start(pred[2048]{0:T(1024)(128)(4,1)S(1)} %fusion.240) | copy-start | bytes 6148
  33.9 16.7 %copy-start.7 = (bf16[2,64,512]{2,1,0:T(8,128)(2,1)S(1)}, bf16[2,64,512]{2,1,0:T(8,128)(2,1)}, u32[]{:S(2)}) copy-start(bf16[2,64,512]{2,1,0:T(8,128)(2,1)} %param.13) | copy-start | bytes 393220
  33.9 10.3 %copy-start.9 = (bf16[32,2,1024]{2,1,0:T(2,128)(2,1)}, bf16[32,2,1024]{2,1,0:T(2,128)(2,1)S(1)}, u32[]{:S(2)}) copy-start(bf16[32,2,1024]{2,1,0:T(2,128)(2,1)S(1)} %all-to-all-done) | copy-start | bytes 393220
  35.0 36.4 %all-to-all-start.1 = ((f32[32,2,16,256]{3,2,1,0:T(8,128)}), f32[32,2,16,256]{3,2,1,0:T(8,128)}, u32[]{:S(2)}, u32[]{:S(2)}) async-start(f32[32,2,16,256]{3,2,1,0:T(8,128)} %broadcast_in_dim.61), calls=%async_computation.1 | async-start | bytes 2097152 | tf_op jit(solution)/shard_map/all_to_all | solution.py:28
  73.4 15.4 %all-to-all-start.2 = ((f32[8,2,16,256]{3,2,1,0:T(8,128)}), f32[8,2,16,256]{3,2,1,0:T(8,128)S(1)}, u32[]{:S(2)}, u32[]{:S(2)}) async-start(f32[8,2,16,256]{3,2,1,0:T(8,128)} %broadcast_in_dim.62), calls=%async_computation.2 | async-start | bytes 524288 | tf_op jit(solution)/shard_map/all_to_all | solution.py:28
  88.9 6.6 %copy-start.4 = (bf16[2,256,512]{2,1,0:T(8,128)(2,1)S(1)}, bf16[2,256,512]{2,1,0:T(8,128)(2,1)}, u32[]{:S(2)}) copy-start(bf16[2,256,512]{2,1,0:T(8,128)(2,1)} %param.16) | copy-start | bytes 1572868
  88.9 7.1 %copy-start.13 = (f32[1,16,512]{2,1,0:T(8,128)S(1)}, f32[1,16,512]{2,1,0:T(8,128)}, u32[]{:S(2)}) copy-start(f32[1,16,512]{2,1,0:T(8,128)} %fusion.16) | copy-start | bytes 98308
  88.9 7.1 %copy-start.14 = (f32[1,16,512]{2,1,0:T(8,128)S(1)}, f32[1,16,512]{2,1,0:T(8,128)}, u32[]{:S(2)}) copy-start(f32[1,16,512]{2,1,0:T(8,128)} %fusion.17) | copy-start | bytes 98308
  88.9 7.1 %copy-start.15 = (f32[1,16,512]{2,1,0:T(8,128)S(1)}, f32[1,16,512]{2,1,0:T(8,128)}, u32[]{:S(2)}) copy-start(f32[1,16,512]{2,1,0:T(8,128)} %fusion.14) | copy-start | bytes 98308
  89.0 7.1 %copy-start.16 = (f32[1,16,512]{2,1,0:T(8,128)S(1)}, f32[1,16,512]{2,1,0:T(8,128)}, u32[]{:S(2)}) copy-start(f32[1,16,512]{2,1,0:T(8,128)} %fusion.15) | copy-start | bytes 98308
  89.0 7.1 %copy-start.17 = (f32[1,16,512]{2,1,0:T(8,128)S(1)}, f32[1,16,512]{2,1,0:T(8,128)}, u32[]{:S(2)}) copy-start(f32[1,16,512]{2,1,0:T(8,128)} %fusion.18) | copy-start | bytes 98308
  89.0 7.1 %copy-start.18 = (f32[1,16,512]{2,1,0:T(8,128)S(1)}, f32[1,16,512]{2,1,0:T(8,128)}, u32[]{:S(2)}) copy-start(f32[1,16,512]{2,1,0:T(8,128)} %fusion.19) | copy-start | bytes 98308
  89.0 7.1 %copy-start.19 = (f32[1,16,512]{2,1,0:T(8,128)S(1)}, f32[1,16,512]{2,1,0:T(8,128)}, u32[]{:S(2)}) copy-start(f32[1,16,512]{2,1,0:T(8,128)} %fusion.7) | copy-start | bytes 98308
  89.0 7.1 %copy-start.20 = (f32[1,16,512]{2,1,0:T(8,128)S(1)}, f32[1,16,512]{2,1,0:T(8,128)}, u32[]{:S(2)}) copy-start(f32[1,16,512]{2,1,0:T(8,128)} %fusion.6) | copy-start | bytes 98308
  89.0 7.7 %copy-start.3 = (bf16[2,256,512]{2,1,0:T(8,128)(2,1)S(1)}, bf16[2,256,512]{2,1,0:T(8,128)(2,1)}, u32[]{:S(2)}) copy-start(bf16[2,256,512]{2,1,0:T(8,128)(2,1)} %param.14) | copy-start | bytes 1572868
  91.3 5.8 %copy-start.6 = (bf16[2,64,512]{2,1,0:T(8,128)(2,1)S(1)}, bf16[2,64,512]{2,1,0:T(8,128)(2,1)}, u32[]{:S(2)}) copy-start(bf16[2,64,512]{2,1,0:T(8,128)(2,1)} %param.11) | copy-start | bytes 393220
  93.5 10.5 %copy-start.26 = (pred[64]{0:T(512)(128)(4,1)S(1)}, pred[64]{0:T(512)(128)(4,1)}, u32[]{:S(2)}) copy-start(pred[64]{0:T(512)(128)(4,1)} %copy-done.25) | copy-start | bytes 196
  97.4 17.9 %collective-permute-start.3 = (bf16[2,16,512]{2,1,0:T(8,128)(2,1)S(1)}, bf16[2,16,512]{2,1,0:T(8,128)(2,1)S(1)}, u32[]{:S(2)}, u32[]{:S(2)}) collective-permute-start(bf16[2,16,512]{2,1,0:T(8,128)(2,1)S(1)} %get-tuple-element.2), channel_id=1, source_target_pairs={{1,0},{2,1},{3,2},{4,3},{5,4},{6,5},{7,6},{8,7},{9,8},{10,9},{11,1... | collective-permute-start | bytes 98312 | tf_op jit(solution)/shard_map/ppermute | solution.py:15
  100.4 16.7 %collective-permute-start.2 = (bf16[2,16,512]{2,1,0:T(8,128)(2,1)S(1)}, bf16[2,16,512]{2,1,0:T(8,128)(2,1)}, u32[]{:S(2)}, u32[]{:S(2)}) collective-permute-start(bf16[2,16,512]{2,1,0:T(8,128)(2,1)S(1)} %get-tuple-element.2), channel_id=1, source_target_pairs={{0,1},{1,2},{2,3},{3,4},{4,5},{5,6},{6,7},{7,8},{8,9},{9,10},{10,1... | collective-permute-start | bytes 98312 | tf_op jit(solution)/shard_map/ppermute | solution.py:14
  106.6 15.0 %all-to-all-start.3 = ((bf16[32,2,1024]{2,1,0:T(2,128)(2,1)}), bf16[32,2,1024]{2,1,0:T(2,128)(2,1)S(1)}, u32[]{:S(2)}, u32[]{:S(2)}) async-start(bf16[32,2,1024]{2,1,0:T(2,128)(2,1)} %reshape.75), calls=%async_computation.3 | async-start | bytes 262144 | tf_op jit(solution)/shard_map/all_to_all | solution.py:28
  119.6 15.7 %copy-start.24 = (pred[2048]{0:T(1024)(128)(4,1)S(1)}, pred[2048]{0:T(1024)(128)(4,1)}, u32[]{:S(2)}) copy-start(pred[2048]{0:T(1024)(128)(4,1)} %copy-done.23) | copy-start | bytes 6148
  123.5 36.0 %all-to-all-start.4 = ((f32[32,2,16,256]{3,2,1,0:T(8,128)}), f32[32,2,16,256]{3,2,1,0:T(8,128)}, u32[]{:S(2)}, u32[]{:S(2)}) async-start(f32[32,2,16,256]{3,2,1,0:T(8,128)} %broadcast_in_dim.64), calls=%async_computation.4 | async-start | bytes 2097152 | tf_op jit(solution)/shard_map/all_to_all | solution.py:28
  133.1 40.6 %copy-start.22 = (pred[2048]{0:T(1024)(128)(4,1)S(1)}, pred[2048]{0:T(1024)(128)(4,1)}, u32[]{:S(2)}) copy-start(pred[2048]{0:T(1024)(128)(4,1)} %copy-done.21) | copy-start | bytes 6148
  134.7 39.0 %copy-start.2 = (bf16[2,256,2048]{2,1,0:T(8,128)(2,1)S(1)}, bf16[2,256,2048]{2,1,0:T(8,128)(2,1)}, u32[]{:S(2)}) copy-start(bf16[2,256,2048]{2,1,0:T(8,128)(2,1)} %param.15) | copy-start | bytes 6291460
  140.2 36.4 %copy-start.5 = (bf16[2,256,512]{2,1,0:T(8,128)(2,1)S(1)}, bf16[2,256,512]{2,1,0:T(8,128)(2,1)}, u32[]{:S(2)}) copy-start(bf16[2,256,512]{2,1,0:T(8,128)(2,1)} %param.16) | copy-start | bytes 1572868
  161.5 12.1 %all-to-all-start.5 = ((f32[8,2,16,256]{3,2,1,0:T(8,128)}), f32[8,2,16,256]{3,2,1,0:T(8,128)S(1)}, u32[]{:S(2)}, u32[]{:S(2)}) async-start(f32[8,2,16,256]{3,2,1,0:T(8,128)} %broadcast_in_dim.65), calls=%async_computation.5 | async-start | bytes 524288 | tf_op jit(solution)/shard_map/all_to_all | solution.py:28
  (5 other events, 16.0 us)
where the time goes:
time: 182 us; the launch traced here: 179 us
  matrix products  55.7 us (31%)
  starting transfers between devices  52.8 us (29%)
  waiting for transfers between devices  50.9 us (28%)
  local copies, waits for them, and re-layouts  12.2 us (7%)
  other arithmetic  5.42 us (3%)
    all_to_all x6, waiting for transfers between devices, copy_for_each(): return lax.all_to_all(copies, axis, split_axis=0, concat_axis=0, tiled=True)  50.9 us
    all_to_all x6, starting transfers between devices, copy_for_each(): return lax.all_to_all(copies, axis, split_axis=0, concat_axis=0, tiled=True)  43.8 us
    dot_general x48, matrix products, dots(): return jnp.dot(vec, mat.T, preferred_element_type=jnp.float32)  39.4 us
    broadcast_in_dim x6, local copies, waits for them, and re-layouts, copy_for_each(): copies = jnp.broadcast_to(value, (lax.axis_size(axis), *value.shape))  5.19 us
    ppermute x2, starting transfers between devices, padded_2(): after = lax.ppermute(leading, axis, down)  4.66 us
    unnamed x58, local copies, waits for them, and re-layouts  4.55 us
    ppermute x2, starting transfers between devices, padded_2(): before = lax.ppermute(last, axis, up)  4.32 us
  transfers between devices with their start and end apart: 10, of which 5 were waited for; matrix products, arithmetic and copies ran while one was open for 29% of the time, Pallas kernels for 0%

commit v1 on v0

v1 whole, which is shorter than its diff:
```python
import functools

import jax
import jax.numpy as jnp
from jax import lax
from jax.experimental import pallas as pl
from jax.experimental.pallas import tpu as pltpu
from jax.sharding import Mesh
from jax.sharding import PartitionSpec as P

REGION = ("yh", "x")
BLK = ("z", "yl", "c")
PLANE = ("yh", "x", "yl", "c")
ALL = REGION + BLK
NT = (((1,), (1,)), ((), ()))
f32 = jnp.float32
bf16 = jnp.bfloat16


def vmem(n):
    return [pl.BlockSpec(memory_space=pltpu.VMEM)] * n


def nt(rows, mat):
    return lax.dot_general(rows, mat, NT, preferred_element_type=f32)


def nn(rows, mat):
    return jnp.dot(rows, mat, preferred_element_type=f32)


def halves(acc, width):
    real = acc[:16, :width] - acc[16:, width:]
    imag = acc[:16, width:] + acc[16:, :width]
    return real, imag


def paired(acc):
    lane = lax.broadcasted_iota(jnp.int32, (16, 128), 1)
    crossed = pltpu.roll(acc[16:], 64, 1)
    return acc[:16] + jnp.where(lane < 64, -crossed, crossed)


def fill_sends(vec, ranks, inner_basis, outer_basis, send):
    coeff = paired(nt(vec, inner_basis[...].reshape(128, 512)))
    lane = lax.broadcasted_iota(jnp.int32, (16, 128), 1)
    rank = jnp.where(lane < 64, lane, lane - 64)
    coeff = jnp.where(rank < ranks[0], coeff, 0.0).astype(bf16)
    real, imag = halves(nt(vec, outer_basis[...].reshape(512, 512)), 256)
    quarters = (real[:, :128], real[:, 128:], imag[:, :128], imag[:, 128:])
    quarters = [q.astype(bf16) for q in quarters]
    for d in range(32):
        send[d, :16] = coeff
        send[d, 16:] = quarters[d % 4]


def start_kernel(probes, ranks, inner_basis, outer_basis, send):
    fill_sends(probes[...].reshape(32, 512), ranks, inner_basis, outer_basis, send)


def sum_kernel(recv, send):
    total = recv[0, 16:].astype(f32)
    for j in range(1, 32):
        total = total + recv[j, 16:].astype(f32)
    total = total.astype(bf16)
    for d in range(32):
        send[d] = total


def local_kernel(index, before, vec, after, near_blocks, recv, coupling, inner_expand, out):
    acc = None
    for b, part in enumerate((before, vec, after)):
        term = nt(part[...].reshape(32, 512), near_blocks[b].reshape(1024, 512))
        acc = term if acc is None else acc + term
    real, imag = halves(acc, 512)
    lane = lax.broadcasted_iota(jnp.int32, (16, 128), 1)
    position = index[0]
    res, ims = [], []
    for j in range(0, 32, 2):
        first, second = (
            jnp.where(jnp.abs(k - position) > 1, recv[k, :16].astype(f32), 0.0) for k in (j, j + 1)
        )
        res.append(jnp.where(lane < 64, first, pltpu.roll(second, 64, 1)))
        ims.append(jnp.where(lane < 64, pltpu.roll(first, 64, 1), second))
    rows = jnp.concatenate([jnp.concatenate(res, 1), jnp.concatenate(ims, 1)], 0).astype(bf16)
    inner = paired(nt(rows, coupling[...].reshape(128, 2048)))
    rows = jnp.concatenate([inner[:, :64], pltpu.roll(inner, 64, 1)[:, :64]], 0).astype(bf16)
    a, b = nn(rows, inner_expand[0]), nn(rows, inner_expand[1])
    out[0] = real + (a[:16] - b[16:])
    out[1] = imag + (a[16:] + b[:16])


def field_part(index, recv, coupling, expand):
    region = index[1]
    res, ims = [], []
    for s in range(8):
        tiles = [jnp.where(s != region, recv[4 * s + q], jnp.zeros((16, 128), bf16)) for q in range(4)]
        res += tiles[:2]
        ims += tiles[2:]
    rows = jnp.concatenate([jnp.concatenate(res, 1), jnp.concatenate(ims, 1)], 0)
    real, imag = halves(nt(rows, coupling[...].reshape(512, 2048)), 256)
    rows = jnp.concatenate([real, imag], 0).astype(bf16)
    a, b = nn(rows, expand[0]), nn(rows, expand[1])
    return a[:16] - b[16:], a[16:] + b[:16]


def middle_kernel(index, recv, coupling, expand, local, ranks, inner_basis, outer_basis, first, vec, send):
    real, imag = field_part(index, recv, coupling, expand)
    real, imag = local[0] + real, local[1] + imag
    first[0] = real
    first[1] = imag
    rows = jnp.concatenate([real, imag], 0).astype(bf16)
    vec[0] = rows[:16]
    vec[1] = rows[16:]
    fill_sends(rows, ranks, inner_basis, outer_basis, send)


def last_kernel(index, recv, coupling, expand, local, second):
    real, imag = field_part(index, recv, coupling, expand)
    second[0] = local[0] + real
    second[1] = local[1] + imag


def shape(dims, dtype):
    return jax.ShapeDtypeStruct(dims, dtype)


SMEM = pl.BlockSpec(memory_space=pltpu.SMEM)
UP = [(i, i + 1) for i in range(31)]
DOWN = [(i + 1, i) for i in range(31)]


def exchange(value, axes):
    return lax.all_to_all(value, axes, split_axis=0, concat_axis=0, tiled=True)


def local_terms(index, vec, near_blocks, recv, coupling, inner_expand):
    before = lax.ppermute(vec, BLK, UP)
    after = lax.ppermute(vec, BLK, DOWN)
    return pl.pallas_call(
        local_kernel,
        in_specs=[SMEM] + vmem(7),
        out_specs=vmem(1)[0],
        out_shape=shape((2, 16, 512), f32),
        name="local_terms",
    )(index, before, vec, after, near_blocks, recv, coupling, inner_expand)


def group_sums(recv):
    send = pl.pallas_call(
        sum_kernel,
        in_specs=vmem(1),
        out_specs=vmem(1)[0],
        out_shape=shape((32, 16, 128), bf16),
        name="group_sums",
    )(recv)
    return exchange(send, PLANE)


def local(probes, near_blocks, inner_basis, coupling, inner_expand, outer_basis, group_coupling, outer_expand, ranks):
    index = jnp.stack([lax.axis_index(BLK), lax.axis_index(REGION)]).astype(jnp.int32)
    send = pl.pallas_call(
        start_kernel,
        in_specs=[vmem(1)[0], SMEM] + vmem(2),
        out_specs=vmem(1)[0],
        out_shape=shape((32, 32, 128), bf16),
        name="start",
    )(probes, ranks, inner_basis, outer_basis)
    recv = exchange(send, BLK)
    sums = group_sums(recv)
    near = local_terms(index, probes, near_blocks, recv, coupling, inner_expand)
    first, vec, send = pl.pallas_call(
        middle_kernel,
        in_specs=[SMEM] + vmem(4) + [SMEM] + vmem(2),
        out_specs=vmem(3),
        out_shape=[shape((2, 16, 512), f32), shape((2, 16, 512), bf16), shape((32, 32, 128), bf16)],
        name="middle",
    )(index, sums, group_coupling, outer_expand, near, ranks, inner_basis, outer_basis)
    recv = exchange(send, BLK)
    sums = group_sums(recv)
    near = local_terms(index, vec, near_blocks, recv, coupling, inner_expand)
    second = pl.pallas_call(
        last_kernel,
        in_specs=[SMEM] + vmem(4),
        out_specs=vmem(1)[0],
        out_shape=shape((2, 16, 512), f32),
        name="last",
    )(index, sums, group_coupling, outer_expand, near)
    return first, second


def solution(mesh):
    fine = Mesh(mesh.devices.reshape(2, 4, 8, 2, 2), ALL)
    placed = (
        P(None, None, ALL),
        P(None, None, ALL, None),
        P(None, None, ALL),
        P(None, ALL, None),
        P(None, None, ALL),
        P(None, None, ALL),
        P(None, REGION, None),
        P(None, None, ALL),
        P(ALL),
    )
    return jax.shard_map(
        local,
        mesh=fine,
        in_specs=placed,
        out_specs=(P(None, None, ALL), P(None, None, ALL)),
        check_vma=False,
    )
```

time: 182 us -> 98.1 us (0.54); the launches traced: 179 us -> 97.5 us
  matrix products: 55.7 us -> 0 us
  waiting for transfers between devices: 50.9 us -> 5.72 us
  blocking collectives: 0 us -> 39 us
  starting transfers between devices: 52.8 us -> 26.9 us
  Pallas kernels: 0 us -> 21.5 us
  local copies, waits for them, and re-layouts: 12.2 us -> 2.53 us
  other arithmetic: 5.42 us -> 0.56 us
    dot_general x72 -> x0, matrix products: 55.7 us -> none  [the longest x48 39.4 us: dots(): return jnp.dot(vec, mat.T, preferred_element_type=jnp.float32)]
    all_to_all x6 -> x2, waiting for transfers between devices: 50.9 us -> 0.01 us  [exchange(): return lax.all_to_all(value, axes, split_axis=0, concat_axis=0, tiled=True)]
    all_to_all x0 -> x2, blocking collectives: none -> 39 us  [exchange(): return lax.all_to_all(value, axes, split_axis=0, concat_axis=0, tiled=True)]
    all_to_all x6 -> x2, starting transfers between devices: 43.8 us -> 14.4 us  [exchange(): return lax.all_to_all(value, axes, split_axis=0, concat_axis=0, tiled=True)]
    pallas_call x0 -> x7, Pallas kernels: none -> 21.5 us  [the longest x2 8.45 us: local_terms(): pl.pallas_call(local_kernel, in_specs=[SMEM] + vmem(7), out_specs=vmem(1)...]
    ppermute x4, waiting for transfers between devices: 0.01 us -> 5.72 us  [the longest x2 4.4 us: local_terms(): before = lax.ppermute(vec, BLK, UP)]
    broadcast_in_dim x6 -> x0, local copies, waits for them, and re-layouts: 5.19 us -> none  [copy_for_each(): copies = jnp.broadcast_to(value, (lax.axis_size(axis), *value.shape))]
    ppermute x4, starting transfers between devices: 8.98 us -> 12.4 us  [the longest x2 8.32 us: local_terms(): after = lax.ppermute(vec, BLK, DOWN)]
  transfers between devices with their start and end apart: 10 -> 6, of which waited for: 5 -> 2; matrix products, arithmetic and copies ran while one was open for 29% -> 1% of each run, Pallas kernels for 0% -> 9%
where the time goes in v1:
time: 98.1 us; the launch traced here: 97.5 us
  blocking collectives  39 us (40%)
  starting transfers between devices  26.9 us (27%)
  Pallas kernels  21.5 us (22%)
  waiting for transfers between devices  5.72 us (6%)
  local copies, waits for them, and re-layouts  2.53 us (3%)
  between operations  1.36 us (1%)
    all_to_all x2, blocking collectives, exchange(): return lax.all_to_all(value, axes, split_axis=0, concat_axis=0, tiled=True)  39 us
    all_to_all x2, starting transfers between devices, exchange(): return lax.all_to_all(value, axes, split_axis=0, concat_axis=0, tiled=True)  14.4 us
    pallas_call x2, Pallas kernels, local_terms(): pl.pallas_call(local_kernel, in_specs=[SMEM] + vmem(7), out_specs=vmem(1)...  8.45 us
    ppermute x2, starting transfers between devices, local_terms(): after = lax.ppermute(vec, BLK, DOWN)  8.32 us
    ppermute x2, waiting for transfers between devices, local_terms(): before = lax.ppermute(vec, BLK, UP)  4.4 us
    pallas_call x1, Pallas kernels, local(): pl.pallas_call(middle_kernel, in_specs=[SMEM] + vmem(4) + [SMEM] + vmem(2...  4.23 us
    ppermute x2, starting transfers between devices, local_terms(): before = lax.ppermute(vec, BLK, UP)  4.1 us
    pallas_call x1, Pallas kernels, local(): pl.pallas_call(last_kernel, in_specs=[SMEM] + vmem(4), out_specs=vmem(1)[...  3.35 us
  transfers between devices with their start and end apart: 6, of which 2 were waited for; matrix products, arithmetic and copies ran while one was open for 1% of the time, Pallas kernels for 9%

profile of v1, /device:TPU:32, one launch (start us, length us, event | category | flops | bytes accessed | tf_op | source)
XLA Modules:
  0.0 97.5 jit_solution(14655831690281537317)
XLA Ops:
  1.3 2.2 %start.1 = bf16[32,32,128]{2,1,0:T(8,128)(2,1)} custom-call(bf16[2,16,512]{2,1,0:T(8,128)(2,1)} %vec.1, s32[1]{0:T(128)S(6)} %copy.11.ranks, bf16[2,64,512]{2,1,0:T(8,128)(2,1)} %inner_basis.3, bf16[2,256,512]{2,1,0:T(8,128)(2,1)} %outer_basis.3), custom_call_target="tpu_custom_call" | custom-call | tf_op jit(solution)/shard_map/start/pallas_call | solution.py:162
  3.5 21.3 %all_to_all.20.recv = bf16[32,32,128]{2,1,0:T(8,128)(2,1)} all-to-all(bf16[32,32,128]{2,1,0:T(8,128)(2,1)} %start.1), channel_id=1, replica_groups=mesh['yh'=2,'x'=4,'z'=8,'yl'=2,'c'=2] {'z','yl','c'}, dimensions={0} | all-to-all | bytes 524288 | tf_op jit(solution)/shard_map/all_to_all | solution.py:134
  24.8 1.6 %group_sums.2 = bf16[32,16,128]{2,1,0:T(8,128)(2,1)} custom-call(bf16[32,32,128]{2,1,0:T(8,128)(2,1)} %all_to_all.20.recv), custom_call_target="tpu_custom_call" | custom-call | tf_op jit(solution)/shard_map/group_sums/pallas_call | solution.py:150
  26.4 7.0 %all-to-all-start.1 = ((bf16[32,16,128]{2,1,0:T(8,128)(2,1)}), bf16[32,16,128]{2,1,0:T(8,128)(2,1)S(1)}, u32[]{:S(2)}, u32[]{:S(2)}) async-start(bf16[32,16,128]{2,1,0:T(8,128)(2,1)} %group_sums.2), calls=%async_computation.1 | async-start | bytes 262144 | tf_op jit(solution)/shard_map/all_to_all | solution.py:134
  33.4 2.2 %collective-permute-start = (bf16[2,16,512]{2,1,0:T(8,128)(2,1)}, bf16[2,16,512]{2,1,0:T(8,128)(2,1)S(1)}, u32[]{:S(2)}, u32[]{:S(2)}) collective-permute-start(bf16[2,16,512]{2,1,0:T(8,128)(2,1)} %vec.1), channel_id=1, source_target_pairs={{0,1},{1,2},{2,3},{3,4},{4,5},{5,6},{6,7},{7,8},{8,9},{9,10},{10,1... | collective-permute-start | bytes 98312 | tf_op jit(solution)/shard_map/ppermute | solution.py:138
  35.6 4.3 %collective-permute-start.1 = (bf16[2,16,512]{2,1,0:T(8,128)(2,1)}, bf16[2,16,512]{2,1,0:T(8,128)(2,1)S(1)}, u32[]{:S(2)}, u32[]{:S(2)}) collective-permute-start(bf16[2,16,512]{2,1,0:T(8,128)(2,1)} %vec.1), channel_id=1, source_target_pairs={{1,0},{2,1},{3,2},{4,3},{5,4},{6,5},{7,6},{8,7},{9,8},{10,9},{11,1... | collective-permute-start | bytes 98312 | tf_op jit(solution)/shard_map/ppermute | solution.py:139
  39.9 0.6 pad_add_fusion.index
  40.5 0.0 collective-permute-done.before
  40.5 0.0 copy-start.2
  40.5 1.3 %collective-permute-done.1.after = bf16[2,16,512]{2,1,0:T(8,128)(2,1)S(1)} collective-permute-done((bf16[2,16,512]{2,1,0:T(8,128)(2,1)}, bf16[2,16,512]{2,1,0:T(8,128)(2,1)S(1)}, u32[]{:S(2)}, u32[]{:S(2)}) %collective-permute-start.1) | collective-permute-done | bytes 32800 | tf_op jit(solution)/shard_map/ppermute | solution.py:139
  41.8 0.0 copy-done.2
  41.8 0.6 copy-done.3
  42.4 4.2 %local_terms.2.local = f32[2,16,512]{2,1,0:T(8,128)} custom-call(s32[2]{0:T(128)} %pad_add_fusion.index, bf16[2,16,512]{2,1,0:T(8,128)(2,1)} %copy-done.2, bf16[2,16,512]{2,1,0:T(8,128)(2,1)} %vec.1, bf16[2,16,512]{2,1,0:T(8,128)(2,1)} %copy-done.3, bf16[3,2,512,512]{3,2,1,0:T(8,128)(2,1)} %near_blocks.3, bf16[32,32,128]{2,1,0:T(8,128)(2,1)} %all_to_all.20.recv, ...), custom_call_target="tpu_custom_call" | custom-call | tf_op jit(solution)/shard_map/local_terms/pallas_call | solution.py:140
  46.6 0.0 all-to-all-done.1.recv
  46.6 0.0 copy-start
  46.6 0.6 copy-done
  47.3 4.2 %middle.1 = (f32[2,16,512]{2,1,0:T(8,128)}, bf16[2,16,512]{2,1,0:T(8,128)(2,1)}, bf16[32,32,128]{2,1,0:T(8,128)(2,1)}) custom-call(s32[2]{0:T(128)} %pad_add_fusion.index, bf16[32,16,128]{2,1,0:T(8,128)(2,1)} %copy-done, bf16[2,256,2048]{2,1,0:T(8,128)(2,1)} %coupling.7, bf16[2,256,512]{2,1,0:T(8,128)(2,1)} %expand.3, f32[2,16,512]{2,1,0:T(8,128)} %local_terms.2.local, ...), custom_call_target="tpu_custom_call" | custom-call | tf_op jit(solution)/shard_map/middle/pallas_call | solution.py:172
  51.5 17.7 %all_to_all.21.recv = bf16[32,32,128]{2,1,0:T(8,128)(2,1)} all-to-all(bf16[32,32,128]{2,1,0:T(8,128)(2,1)} %get-tuple-element.6), channel_id=1, replica_groups=mesh['yh'=2,'x'=4,'z'=8,'yl'=2,'c'=2] {'z','yl','c'}, dimensions={0} | all-to-all | bytes 524288 | tf_op jit(solution)/shard_map/all_to_all | solution.py:134
  69.2 1.6 %group_sums.3 = bf16[32,16,128]{2,1,0:T(8,128)(2,1)} custom-call(bf16[32,32,128]{2,1,0:T(8,128)(2,1)} %all_to_all.21.recv), custom_call_target="tpu_custom_call" | custom-call | tf_op jit(solution)/shard_map/group_sums/pallas_call | solution.py:150
  70.9 7.4 %all-to-all-start.3 = ((bf16[32,16,128]{2,1,0:T(8,128)(2,1)}), bf16[32,16,128]{2,1,0:T(8,128)(2,1)S(1)}, u32[]{:S(2)}, u32[]{:S(2)}) async-start(bf16[32,16,128]{2,1,0:T(8,128)(2,1)} %group_sums.3), calls=%async_computation.3 | async-start | bytes 262144 | tf_op jit(solution)/shard_map/all_to_all | solution.py:134
  78.3 4.0 %collective-permute-start.3 = (bf16[2,16,512]{2,1,0:T(8,128)(2,1)}, bf16[2,16,512]{2,1,0:T(8,128)(2,1)S(1)}, u32[]{:S(2)}, u32[]{:S(2)}) collective-permute-start(bf16[2,16,512]{2,1,0:T(8,128)(2,1)} %get-tuple-element.7.vec), channel_id=1, source_target_pairs={{1,0},{2,1},{3,2},{4,3},{5,4},{6,5},{7,6},{8,7},{9,8},{10,9},{11,1... | collective-permute-start | bytes 98312 | tf_op jit(solution)/shard_map/ppermute | solution.py:139
  82.3 1.9 %collective-permute-start.2 = (bf16[2,16,512]{2,1,0:T(8,128)(2,1)}, bf16[2,16,512]{2,1,0:T(8,128)(2,1)S(1)}, u32[]{:S(2)}, u32[]{:S(2)}) collective-permute-start(bf16[2,16,512]{2,1,0:T(8,128)(2,1)} %get-tuple-element.7.vec), channel_id=1, source_target_pairs={{0,1},{1,2},{2,3},{3,4},{4,5},{5,6},{6,7},{7,8},{8,9},{9,10},{10,1... | collective-permute-start | bytes 98312 | tf_op jit(solution)/shard_map/ppermute | solution.py:138
  84.2 0.0 collective-permute-done.3.after
  84.3 0.0 copy-start.4
  84.3 4.4 %collective-permute-done.2.before = bf16[2,16,512]{2,1,0:T(8,128)(2,1)S(1)} collective-permute-done((bf16[2,16,512]{2,1,0:T(8,128)(2,1)}, bf16[2,16,512]{2,1,0:T(8,128)(2,1)S(1)}, u32[]{:S(2)}, u32[]{:S(2)}) %collective-permute-start.2) | collective-permute-done | bytes 32800 | tf_op jit(solution)/shard_map/ppermute | solution.py:138
  88.7 0.0 copy-done.4
  88.7 0.0 copy-start.5
  88.7 0.6 copy-done.5
  89.3 4.2 %local_terms.3.local = f32[2,16,512]{2,1,0:T(8,128)} custom-call(s32[2]{0:T(128)} %pad_add_fusion.index, bf16[2,16,512]{2,1,0:T(8,128)(2,1)} %copy-done.5, bf16[2,16,512]{2,1,0:T(8,128)(2,1)} %get-tuple-element.7.vec, bf16[2,16,512]{2,1,0:T(8,128)(2,1)} %copy-done.4, bf16[3,2,512,512]{3,2,1,0:T(8,128)(2,1)} %near_blocks.3, ...), custom_call_target="tpu_custom_call" | custom-call | tf_op jit(solution)/shard_map/local_terms/pallas_call | solution.py:140
  93.5 0.0 all-to-all-done.3.recv
  93.5 0.6 copy-done.1
  94.2 3.4 %last.1 = f32[2,16,512]{2,1,0:T(8,128)} custom-call(s32[2]{0:T(128)} %pad_add_fusion.index, bf16[32,16,128]{2,1,0:T(8,128)(2,1)} %copy-done.1, bf16[2,256,2048]{2,1,0:T(8,128)(2,1)} %coupling.7, bf16[2,256,512]{2,1,0:T(8,128)(2,1)} %expand.3, f32[2,16,512]{2,1,0:T(8,128)} %local_terms.3.local), custom_call_target="tpu_custom_call" | custom-call | tf_op jit(solution)/shard_map/last/pallas_call | solution.py:182
  (2 shorter events, 0.0 us)
Async XLA Ops:
  26.4 20.3 %all-to-all-start.1 = ((bf16[32,16,128]{2,1,0:T(8,128)(2,1)}), bf16[32,16,128]{2,1,0:T(8,128)(2,1)S(1)}, u32[]{:S(2)}, u32[]{:S(2)}) async-start(bf16[32,16,128]{2,1,0:T(8,128)(2,1)} %group_sums.2), calls=%async_computation.1 | async-start | bytes 262144 | tf_op jit(solution)/shard_map/all_to_all | solution.py:134
  33.4 7.1 %collective-permute-start = (bf16[2,16,512]{2,1,0:T(8,128)(2,1)}, bf16[2,16,512]{2,1,0:T(8,128)(2,1)S(1)}, u32[]{:S(2)}, u32[]{:S(2)}) collective-permute-start(bf16[2,16,512]{2,1,0:T(8,128)(2,1)} %vec.1), channel_id=1, source_target_pairs={{0,1},{1,2},{2,3},{3,4},{4,5},{5,6},{6,7},{7,8},{8,9},{9,10},{10,1... | collective-permute-start | bytes 98312 | tf_op jit(solution)/shard_map/ppermute | solution.py:138
  35.6 6.2 %collective-permute-start.1 = (bf16[2,16,512]{2,1,0:T(8,128)(2,1)}, bf16[2,16,512]{2,1,0:T(8,128)(2,1)S(1)}, u32[]{:S(2)}, u32[]{:S(2)}) collective-permute-start(bf16[2,16,512]{2,1,0:T(8,128)(2,1)} %vec.1), channel_id=1, source_target_pairs={{1,0},{2,1},{3,2},{4,3},{5,4},{6,5},{7,6},{8,7},{9,8},{10,9},{11,1... | collective-permute-start | bytes 98312 | tf_op jit(solution)/shard_map/ppermute | solution.py:139
  40.5 1.3 %copy-start.2 = (bf16[2,16,512]{2,1,0:T(8,128)(2,1)}, bf16[2,16,512]{2,1,0:T(8,128)(2,1)S(1)}, u32[]{:S(2)}) copy-start(bf16[2,16,512]{2,1,0:T(8,128)(2,1)S(1)} %collective-permute-done.before) | copy-start | bytes 98308
  41.8 0.6 copy-start.3
  46.6 0.7 copy-start
  70.9 22.6 %all-to-all-start.3 = ((bf16[32,16,128]{2,1,0:T(8,128)(2,1)}), bf16[32,16,128]{2,1,0:T(8,128)(2,1)S(1)}, u32[]{:S(2)}, u32[]{:S(2)}) async-start(bf16[32,16,128]{2,1,0:T(8,128)(2,1)} %group_sums.3), calls=%async_computation.3 | async-start | bytes 262144 | tf_op jit(solution)/shard_map/all_to_all | solution.py:134
  78.3 6.0 %collective-permute-start.3 = (bf16[2,16,512]{2,1,0:T(8,128)(2,1)}, bf16[2,16,512]{2,1,0:T(8,128)(2,1)S(1)}, u32[]{:S(2)}, u32[]{:S(2)}) collective-permute-start(bf16[2,16,512]{2,1,0:T(8,128)(2,1)} %get-tuple-element.7.vec), channel_id=1, source_target_pairs={{1,0},{2,1},{3,2},{4,3},{5,4},{6,5},{7,6},{8,7},{9,8},{10,9},{11,1... | collective-permute-start | bytes 98312 | tf_op jit(solution)/shard_map/ppermute | solution.py:139
  82.3 6.3 %collective-permute-start.2 = (bf16[2,16,512]{2,1,0:T(8,128)(2,1)}, bf16[2,16,512]{2,1,0:T(8,128)(2,1)S(1)}, u32[]{:S(2)}, u32[]{:S(2)}) collective-permute-start(bf16[2,16,512]{2,1,0:T(8,128)(2,1)} %get-tuple-element.7.vec), channel_id=1, source_target_pairs={{0,1},{1,2},{2,3},{3,4},{4,5},{5,6},{6,7},{7,8},{8,9},{9,10},{10,1... | collective-permute-start | bytes 98312 | tf_op jit(solution)/shard_map/ppermute | solution.py:138
  84.3 4.4 %copy-start.4 = (bf16[2,16,512]{2,1,0:T(8,128)(2,1)}, bf16[2,16,512]{2,1,0:T(8,128)(2,1)S(1)}, u32[]{:S(2)}) copy-start(bf16[2,16,512]{2,1,0:T(8,128)(2,1)S(1)} %collective-permute-done.3.after) | copy-start | bytes 98308
  88.7 0.6 copy-start.5
  93.5 0.7 copy-start.1

commit v2 on v1

--- a/solution.py
+++ b/solution.py
@@ -1,5 +1,3 @@
-import functools
-
 import jax
 import jax.numpy as jnp
 from jax import lax
@@ -54,11 +52,11 @@
         send[d, 16:] = quarters[d % 4]
 
 
-def start_kernel(probes, ranks, inner_basis, outer_basis, send):
+def start_kernel(probes, inner_basis, outer_basis, ranks, send):
     fill_sends(probes[...].reshape(32, 512), ranks, inner_basis, outer_basis, send)
 
 
-def sum_kernel(recv, send):
+def sum_kernel(recv, before, after, send):
     total = recv[0, 16:].astype(f32)
     for j in range(1, 32):
         total = total + recv[j, 16:].astype(f32)
@@ -67,14 +65,14 @@
         send[d] = total
 
 
-def local_kernel(index, before, vec, after, near_blocks, recv, coupling, inner_expand, out):
+def local_kernel(before, vec, after, recv, near_blocks, coupling, inner_expand, out):
     acc = None
     for b, part in enumerate((before, vec, after)):
         term = nt(part[...].reshape(32, 512), near_blocks[b].reshape(1024, 512))
         acc = term if acc is None else acc + term
     real, imag = halves(acc, 512)
     lane = lax.broadcasted_iota(jnp.int32, (16, 128), 1)
-    position = index[0]
+    position = lax.axis_index(BLK)
     res, ims = [], []
     for j in range(0, 32, 2):
         first, second = (
@@ -90,8 +88,8 @@
     out[1] = imag + (a[16:] + b[:16])
 
 
-def field_part(index, recv, coupling, expand):
-    region = index[1]
+def field_part(recv, coupling, expand):
+    region = lax.axis_index(REGION)
     res, ims = [], []
     for s in range(8):
         tiles = [jnp.where(s != region, recv[4 * s + q], jnp.zeros((16, 128), bf16)) for q in range(4)]
@@ -104,88 +102,112 @@
     return a[:16] - b[16:], a[16:] + b[:16]
 
 
-def middle_kernel(index, recv, coupling, expand, local, ranks, inner_basis, outer_basis, first, vec, send):
-    real, imag = field_part(index, recv, coupling, expand)
+def middle_kernel(recv, coupling, expand, local, inner_hbm, outer_hbm, ranks, first, vec, send, *scratch):
+    inner_basis, outer_basis, sems = scratch
+    copies = [
+        pltpu.make_async_copy(inner_hbm, inner_basis, sems.at[0]),
+        pltpu.make_async_copy(outer_hbm, outer_basis, sems.at[1]),
+    ]
+    for copy in copies:
+        copy.start()
+    real, imag = field_part(recv, coupling, expand)
     real, imag = local[0] + real, local[1] + imag
     first[0] = real
     first[1] = imag
     rows = jnp.concatenate([real, imag], 0).astype(bf16)
     vec[0] = rows[:16]
     vec[1] = rows[16:]
+    for copy in copies:
+        copy.wait()
     fill_sends(rows, ranks, inner_basis, outer_basis, send)
 
 
-def last_kernel(index, recv, coupling, expand, local, second):
-    real, imag = field_part(index, recv, coupling, expand)
+def last_kernel(recv, coupling, expand, local, second):
+    real, imag = field_part(recv, coupling, expand)
     second[0] = local[0] + real
     second[1] = local[1] + imag
 
 
-def shape(dims, dtype):
-    return jax.ShapeDtypeStruct(dims, dtype)
-
-
-SMEM = pl.BlockSpec(memory_space=pltpu.SMEM)
 UP = [(i, i + 1) for i in range(31)]
 DOWN = [(i + 1, i) for i in range(31)]
+ANY = pl.BlockSpec(memory_space=pl.ANY)
+RANKS = pl.BlockSpec(memory_space=pltpu.SMEM)
+PARAMS = pltpu.CompilerParams(vmem_limit_bytes=16 * 1024 * 1024)
+
+
+def in_vmem(*arrays):
+    return [pltpu.with_memory_space_constraint(a, pltpu.VMEM) for a in arrays]
+
+
+def in_hbm(*arrays):
+    return [pltpu.with_memory_space_constraint(a, pltpu.HBM) for a in arrays]
+
+
+def call(kernel, outs, *args):
+    return pl.pallas_call(
+        kernel,
+        in_specs=[RANKS if a.dtype == jnp.int32 else vmem(1)[0] for a in args],
+        out_specs=vmem(len(outs)),
+        out_shape=outs,
+        compiler_params=PARAMS,
+    )(*args)
 
 
 def exchange(value, axes):
     return lax.all_to_all(value, axes, split_axis=0, concat_axis=0, tiled=True)
 
 
-def local_terms(index, vec, near_blocks, recv, coupling, inner_expand):
-    before = lax.ppermute(vec, BLK, UP)
-    after = lax.ppermute(vec, BLK, DOWN)
-    return pl.pallas_call(
-        local_kernel,
-        in_specs=[SMEM] + vmem(7),
-        out_specs=vmem(1)[0],
-        out_shape=shape((2, 16, 512), f32),
-        name="local_terms",
-    )(index, before, vec, after, near_blocks, recv, coupling, inner_expand)
-
-
-def group_sums(recv):
+def neighbours(vec):
+    return lax.ppermute(vec, BLK, UP), lax.ppermute(vec, BLK, DOWN)
+
+
+def local_terms(before, vec, after, recv, near_blocks, coupling, inner_expand):
+    args = in_vmem(before) + [vec] + in_vmem(after, recv) + in_hbm(near_blocks, coupling, inner_expand)
+    return call(local_kernel, [pltpu.VMEM((2, 16, 512), f32)], *args)[0]
+
+
+def group_sums(recv, before, after):
     send = pl.pallas_call(
         sum_kernel,
-        in_specs=vmem(1),
+        in_specs=vmem(1) + [ANY] * 2,
         out_specs=vmem(1)[0],
-        out_shape=shape((32, 16, 128), bf16),
+        out_shape=pltpu.VMEM((32, 16, 128), bf16),
+        compiler_params=PARAMS,
         name="group_sums",
-    )(recv)
+    )(*in_vmem(recv), before, after)
     return exchange(send, PLANE)
 
 
 def local(probes, near_blocks, inner_basis, coupling, inner_expand, outer_basis, group_coupling, outer_expand, ranks):
-    index = jnp.stack([lax.axis_index(BLK), lax.axis_index(REGION)]).astype(jnp.int32)
-    send = pl.pallas_call(
-        start_kernel,
-        in_specs=[vmem(1)[0], SMEM] + vmem(2),
-        out_specs=vmem(1)[0],
-        out_shape=shape((32, 32, 128), bf16),
-        name="start",
-    )(probes, ranks, inner_basis, outer_basis)
+    sends = pltpu.VMEM((32, 32, 128), bf16)
+    send = call(start_kernel, [sends], *in_hbm(probes, inner_basis, outer_basis), ranks)[0]
     recv = exchange(send, BLK)
-    sums = group_sums(recv)
-    near = local_terms(index, probes, near_blocks, recv, coupling, inner_expand)
+    before, after = neighbours(probes)
+    probes = in_hbm(probes)[0]
+    sums = group_sums(recv, before, after)
+    near = local_terms(before, probes, after, recv, near_blocks, coupling, inner_expand)
+    outs = [pltpu.VMEM((2, 16, 512), f32), pltpu.VMEM((2, 16, 512), bf16), sends]
+    weights = in_vmem(group_coupling, outer_expand)
     first, vec, send = pl.pallas_call(
         middle_kernel,
-        in_specs=[SMEM] + vmem(4) + [SMEM] + vmem(2),
+        in_specs=vmem(4) + [ANY] * 2 + [RANKS],
         out_specs=vmem(3),
-        out_shape=[shape((2, 16, 512), f32), shape((2, 16, 512), bf16), shape((32, 32, 128), bf16)],
+        out_shape=outs,
+        scratch_shapes=[
+            pltpu.VMEM(inner_basis.shape, bf16),
+            pltpu.VMEM(outer_basis.shape, bf16),
+            pltpu.SemaphoreType.DMA((2,)),
+        ],
+        compiler_params=PARAMS,
         name="middle",
-    )(index, sums, group_coupling, outer_expand, near, ranks, inner_basis, outer_basis)
+    )(*in_vmem(sums), *weights, *in_vmem(near), *in_hbm(inner_basis, outer_basis), ranks)
     recv = exchange(send, BLK)
-    sums = group_sums(recv)
-    near = local_terms(index, vec, near_blocks, recv, coupling, inner_expand)
-    second = pl.pallas_call(
-        last_kernel,
-        in_specs=[SMEM] + vmem(4),
-        out_specs=vmem(1)[0],
-        out_shape=shape((2, 16, 512), f32),
-        name="last",
-    )(index, sums, group_coupling, outer_expand, near)
+    before, after = neighbours(vec)
+    sums = group_sums(recv, before, after)
+    vec = in_vmem(vec)[0]
+    near = local_terms(before, vec, after, recv, near_blocks, coupling, inner_expand)
+    args = in_vmem(sums) + weights + in_vmem(near)
+    second = call(last_kernel, [jax.ShapeDtypeStruct((2, 16, 512), f32)], *args)[0]
     return first, second
 
 

time: 98.1 us -> 78.1 us (0.80)
  the two profiles are of different devices: /device:TPU:32 before, /device:TPU:1 now
where the time goes in v2:
time: 78.1 us; the launch traced here: 77.5 us
  starting transfers between devices  40.4 us (52%)
  waiting for transfers between devices  19.5 us (25%)
  Pallas kernels  15.7 us (20%)
  between operations  1.4 us (2%)
    all_to_all x4, starting transfers between devices, exchange(): return lax.all_to_all(value, axes, split_axis=0, concat_axis=0, tiled=True)  29.3 us
    all_to_all x4, waiting for transfers between devices, exchange(): return lax.all_to_all(value, axes, split_axis=0, concat_axis=0, tiled=True)  14.4 us
    ppermute x4, starting transfers between devices, neighbours(): return (lax.ppermute(vec, BLK, UP), lax.ppermute(vec, BLK, DOWN))  11 us
    pallas_call x4, Pallas kernels, call(): pl.pallas_call(kernel, in_specs=[RANKS if a.dtype == jnp.int32 else vmem(...  10.9 us
    ppermute x4, waiting for transfers between devices, neighbours(): return (lax.ppermute(vec, BLK, UP), lax.ppermute(vec, BLK, DOWN))  5.05 us
    pallas_call x1, Pallas kernels, local(): pl.pallas_call(middle_kernel, in_specs=vmem(4) + [ANY] * 2 + [RANKS], out...  3.34 us
  transfers between devices with their start and end apart: 8, of which 6 were waited for; matrix products, arithmetic and copies ran while one was open for 1% of the time, Pallas kernels for 9%

profile of v2, /device:TPU:1, one launch (start us, length us, event | category | flops | bytes accessed | tf_op | source)
XLA Modules:
  0.0 77.5 jit_solution(16860909348138369025)
XLA Ops:
  1.3 0.0 copy-start
  1.3 0.0 copy-start.1
  1.3 2.3 %shard_map.104 = bf16[32,32,128]{2,1,0:T(8,128)(2,1)} custom-call(bf16[2,16,512]{2,1,0:T(8,128)(2,1)} %vec.1, bf16[2,64,512]{2,1,0:T(8,128)(2,1)} %inner_hbm.1, bf16[2,256,512]{2,1,0:T(8,128)(2,1)} %outer_hbm.1, s32[1]{0:T(128)S(6)} %copy.12.ranks), custom_call_target="tpu_custom_call" | custom-call | tf_op jit(solution)/shard_map/pallas_call | solution.py:147
  3.6 11.1 %all-to-all-start = ((bf16[32,32,128]{2,1,0:T(8,128)(2,1)}), bf16[32,32,128]{2,1,0:T(8,128)(2,1)S(1)}, u32[]{:S(2)}, u32[]{:S(2)}) async-start(bf16[32,32,128]{2,1,0:T(8,128)(2,1)} %shard_map.104), calls=%async_computation | async-start | bytes 524288 | tf_op jit(solution)/shard_map/all_to_all | solution.py:157
  14.8 3.5 %collective-permute-start = (bf16[2,16,512]{2,1,0:T(8,128)(2,1)}, bf16[2,16,512]{2,1,0:T(8,128)(2,1)S(1)}, u32[]{:S(2)}, u32[]{:S(2)}) collective-permute-start(bf16[2,16,512]{2,1,0:T(8,128)(2,1)} %vec.1), channel_id=1, source_target_pairs={{0,1},{1,2},{2,3},{3,4},{4,5},{5,6},{6,7},{7,8},{8,9},{9,10},{10,1... | collective-permute-start | bytes 98312 | tf_op jit(solution)/shard_map/ppermute | solution.py:161
  18.3 1.9 %collective-permute-start.1 = (bf16[2,16,512]{2,1,0:T(8,128)(2,1)}, bf16[2,16,512]{2,1,0:T(8,128)(2,1)S(1)}, u32[]{:S(2)}, u32[]{:S(2)}) collective-permute-start(bf16[2,16,512]{2,1,0:T(8,128)(2,1)} %vec.1), channel_id=1, source_target_pairs={{1,0},{2,1},{3,2},{4,3},{5,4},{6,5},{7,6},{8,7},{9,8},{10,9},{11,1... | collective-permute-start | bytes 98312 | tf_op jit(solution)/shard_map/ppermute | solution.py:161
  20.2 0.0 collective-permute-done.before
  20.2 4.1 %collective-permute-done.1.after = bf16[2,16,512]{2,1,0:T(8,128)(2,1)S(1)} collective-permute-done((bf16[2,16,512]{2,1,0:T(8,128)(2,1)}, bf16[2,16,512]{2,1,0:T(8,128)(2,1)S(1)}, u32[]{:S(2)}, u32[]{:S(2)}) %collective-permute-start.1) | collective-permute-done | bytes 32800 | tf_op jit(solution)/shard_map/ppermute | solution.py:161
  24.3 1.9 %all-to-all-done.recv = bf16[32,32,128]{2,1,0:T(8,128)(2,1)S(1)} async-done(((bf16[32,32,128]{2,1,0:T(8,128)(2,1)}), bf16[32,32,128]{2,1,0:T(8,128)(2,1)S(1)}, u32[]{:S(2)}, u32[]{:S(2)}) %all-to-all-start) | async-done | bytes 262176 | tf_op jit(solution)/shard_map/all_to_all | solution.py:157
  26.2 0.7 group_sums.2
  26.9 8.3 %all-to-all-start.1 = ((bf16[32,16,128]{2,1,0:T(8,128)(2,1)}), bf16[32,16,128]{2,1,0:T(8,128)(2,1)S(1)}, u32[]{:S(2)}, u32[]{:S(2)}) async-start(bf16[32,16,128]{2,1,0:T(8,128)(2,1)} %group_sums.2), calls=%async_computation.1 | async-start | bytes 262144 | tf_op jit(solution)/shard_map/all_to_all | solution.py:157
  35.1 3.5 %shard_map.105.local = f32[2,16,512]{2,1,0:T(8,128)S(1)} custom-call(bf16[2,16,512]{2,1,0:T(8,128)(2,1)S(1)} %collective-permute-done.before, bf16[2,16,512]{2,1,0:T(8,128)(2,1)} %vec.1, bf16[2,16,512]{2,1,0:T(8,128)(2,1)S(1)} %collective-permute-done.1.after, bf16[32,32,128]{2,1,0:T(8,128)(2,1)S(1)} %all-to-all-done.recv, ...), custom_call_target="tpu_custom_call" | custom-call | tf_op jit(solution)/shard_map/pallas_call | solution.py:147
  38.6 4.2 %all-to-all-done.1.recv = bf16[32,16,128]{2,1,0:T(8,128)(2,1)S(1)} async-done(((bf16[32,16,128]{2,1,0:T(8,128)(2,1)}), bf16[32,16,128]{2,1,0:T(8,128)(2,1)S(1)}, u32[]{:S(2)}, u32[]{:S(2)}) %all-to-all-start.1) | async-done | bytes 131104 | tf_op jit(solution)/shard_map/all_to_all | solution.py:157
  42.8 0.0 copy-done
  42.8 0.0 copy-done.1
  42.8 3.3 %middle.1 = (f32[2,16,512]{2,1,0:T(8,128)S(1)}, bf16[2,16,512]{2,1,0:T(8,128)(2,1)S(1)}, bf16[32,32,128]{2,1,0:T(8,128)(2,1)}) custom-call(bf16[32,16,128]{2,1,0:T(8,128)(2,1)S(1)} %all-to-all-done.1.recv, bf16[2,256,2048]{2,1,0:T(8,128)(2,1)S(1)} %copy-done, bf16[2,256,512]{2,1,0:T(8,128)(2,1)S(1)} %copy-done.1, f32[2,16,512]{2,1,0:T(8,128)S(1)} %shard_map.105.local, ...), custom_call_target="tpu_custom_call" | custom-call | tf_op jit(solution)/shard_map/middle/pallas_call | solution.py:191
  46.1 5.0 %all-to-all-start.2 = ((bf16[32,32,128]{2,1,0:T(8,128)(2,1)}), bf16[32,32,128]{2,1,0:T(8,128)(2,1)S(1)}, u32[]{:S(2)}, u32[]{:S(2)}) async-start(bf16[32,32,128]{2,1,0:T(8,128)(2,1)} %get-tuple-element.6), calls=%async_computation.2 | async-start | bytes 524288 | tf_op jit(solution)/shard_map/all_to_all | solution.py:157
  51.2 2.1 %collective-permute-start.3 = (bf16[2,16,512]{2,1,0:T(8,128)(2,1)S(1)}, bf16[2,16,512]{2,1,0:T(8,128)(2,1)S(1)}, u32[]{:S(2)}, u32[]{:S(2)}) collective-permute-start(bf16[2,16,512]{2,1,0:T(8,128)(2,1)S(1)} %get-tuple-element.7.vec), channel_id=1, source_target_pairs={{1,0},{2,1},{3,2},{4,3},{5,4},{6,5},{7,6},{8,7},{9,8},{10,9},{11,1... | collective-permute-start | bytes 98312 | tf_op jit(solution)/shard_map/ppermute | solution.py:161
  53.3 3.4 %collective-permute-start.2 = (bf16[2,16,512]{2,1,0:T(8,128)(2,1)S(1)}, bf16[2,16,512]{2,1,0:T(8,128)(2,1)S(1)}, u32[]{:S(2)}, u32[]{:S(2)}) collective-permute-start(bf16[2,16,512]{2,1,0:T(8,128)(2,1)S(1)} %get-tuple-element.7.vec), channel_id=1, source_target_pairs={{0,1},{1,2},{2,3},{3,4},{4,5},{5,6},{6,7},{7,8},{8,9},{9,10},{10,1... | collective-permute-start | bytes 98312 | tf_op jit(solution)/shard_map/ppermute | solution.py:161
  56.7 0.0 collective-permute-done.3.after
  56.7 1.0 %collective-permute-done.2.before = bf16[2,16,512]{2,1,0:T(8,128)(2,1)S(1)} collective-permute-done((bf16[2,16,512]{2,1,0:T(8,128)(2,1)S(1)}, bf16[2,16,512]{2,1,0:T(8,128)(2,1)S(1)}, u32[]{:S(2)}, u32[]{:S(2)}) %collective-permute-start.2) | collective-permute-done | bytes 32800 | tf_op jit(solution)/shard_map/ppermute | solution.py:161
  57.7 4.8 %all-to-all-done.2.recv = bf16[32,32,128]{2,1,0:T(8,128)(2,1)S(1)} async-done(((bf16[32,32,128]{2,1,0:T(8,128)(2,1)}), bf16[32,32,128]{2,1,0:T(8,128)(2,1)S(1)}, u32[]{:S(2)}, u32[]{:S(2)}) %all-to-all-start.2) | async-done | bytes 262176 | tf_op jit(solution)/shard_map/all_to_all | solution.py:157
  62.6 0.7 group_sums.3
  63.3 4.9 %all-to-all-start.3 = ((bf16[32,16,128]{2,1,0:T(8,128)(2,1)}), bf16[32,16,128]{2,1,0:T(8,128)(2,1)S(1)}, u32[]{:S(2)}, u32[]{:S(2)}) async-start(bf16[32,16,128]{2,1,0:T(8,128)(2,1)} %group_sums.3), calls=%async_computation.3 | async-start | bytes 262144 | tf_op jit(solution)/shard_map/all_to_all | solution.py:157
  68.2 0.6 copy.11
  68.9 3.5 %shard_map.106.local = f32[2,16,512]{2,1,0:T(8,128)S(1)} custom-call(bf16[2,16,512]{2,1,0:T(8,128)(2,1)S(1)} %collective-permute-done.2.before, bf16[2,16,512]{2,1,0:T(8,128)(2,1)S(1)} %get-tuple-element.7.vec, bf16[2,16,512]{2,1,0:T(8,128)(2,1)S(1)} %collective-permute-done.3.after, bf16[32,32,128]{2,1,0:T(8,128)(2,1)S(1)} %all-to-all-done.2.recv, ...), custom_call_target="tpu_custom_call" | custom-call | tf_op jit(solution)/shard_map/pallas_call | solution.py:147
  72.4 3.5 %all-to-all-done.3.recv = bf16[32,16,128]{2,1,0:T(8,128)(2,1)S(1)} async-done(((bf16[32,16,128]{2,1,0:T(8,128)(2,1)}), bf16[32,16,128]{2,1,0:T(8,128)(2,1)S(1)}, u32[]{:S(2)}, u32[]{:S(2)}) %all-to-all-start.3) | async-done | bytes 131104 | tf_op jit(solution)/shard_map/all_to_all | solution.py:157
  75.9 1.6 %shard_map.107 = f32[2,16,512]{2,1,0:T(8,128)} custom-call(bf16[32,16,128]{2,1,0:T(8,128)(2,1)S(1)} %all-to-all-done.3.recv, bf16[2,256,2048]{2,1,0:T(8,128)(2,1)S(1)} %copy-done, bf16[2,256,512]{2,1,0:T(8,128)(2,1)S(1)} %copy-done.1, f32[2,16,512]{2,1,0:T(8,128)S(1)} %shard_map.106.local), custom_call_target="tpu_custom_call" | custom-call | tf_op jit(solution)/shard_map/pallas_call | solution.py:147
Async XLA Ops:
  1.3 41.5 %copy-start = (bf16[2,256,2048]{2,1,0:T(8,128)(2,1)S(1)}, bf16[2,256,2048]{2,1,0:T(8,128)(2,1)}, u32[]{:S(2)}) copy-start(bf16[2,256,2048]{2,1,0:T(8,128)(2,1)} %coupling.7) | copy-start | bytes 6291460
  1.3 41.5 %copy-start.1 = (bf16[2,256,512]{2,1,0:T(8,128)(2,1)S(1)}, bf16[2,256,512]{2,1,0:T(8,128)(2,1)}, u32[]{:S(2)}) copy-start(bf16[2,256,512]{2,1,0:T(8,128)(2,1)} %expand.3) | copy-start | bytes 1572868
  3.6 22.5 %all-to-all-start = ((bf16[32,32,128]{2,1,0:T(8,128)(2,1)}), bf16[32,32,128]{2,1,0:T(8,128)(2,1)S(1)}, u32[]{:S(2)}, u32[]{:S(2)}) async-start(bf16[32,32,128]{2,1,0:T(8,128)(2,1)} %shard_map.104), calls=%async_computation | async-start | bytes 524288 | tf_op jit(solution)/shard_map/all_to_all | solution.py:157
  14.8 5.5 %collective-permute-start = (bf16[2,16,512]{2,1,0:T(8,128)(2,1)}, bf16[2,16,512]{2,1,0:T(8,128)(2,1)S(1)}, u32[]{:S(2)}, u32[]{:S(2)}) collective-permute-start(bf16[2,16,512]{2,1,0:T(8,128)(2,1)} %vec.1), channel_id=1, source_target_pairs={{0,1},{1,2},{2,3},{3,4},{4,5},{5,6},{6,7},{7,8},{8,9},{9,10},{10,1... | collective-permute-start | bytes 98312 | tf_op jit(solution)/shard_map/ppermute | solution.py:161
  18.3 6.0 %collective-permute-start.1 = (bf16[2,16,512]{2,1,0:T(8,128)(2,1)}, bf16[2,16,512]{2,1,0:T(8,128)(2,1)S(1)}, u32[]{:S(2)}, u32[]{:S(2)}) collective-permute-start(bf16[2,16,512]{2,1,0:T(8,128)(2,1)} %vec.1), channel_id=1, source_target_pairs={{1,0},{2,1},{3,2},{4,3},{5,4},{6,5},{7,6},{8,7},{9,8},{10,9},{11,1... | collective-permute-start | bytes 98312 | tf_op jit(solution)/shard_map/ppermute | solution.py:161
  26.9 15.9 %all-to-all-start.1 = ((bf16[32,16,128]{2,1,0:T(8,128)(2,1)}), bf16[32,16,128]{2,1,0:T(8,128)(2,1)S(1)}, u32[]{:S(2)}, u32[]{:S(2)}) async-start(bf16[32,16,128]{2,1,0:T(8,128)(2,1)} %group_sums.2), calls=%async_computation.1 | async-start | bytes 262144 | tf_op jit(solution)/shard_map/all_to_all | solution.py:157
  46.1 16.4 %all-to-all-start.2 = ((bf16[32,32,128]{2,1,0:T(8,128)(2,1)}), bf16[32,32,128]{2,1,0:T(8,128)(2,1)S(1)}, u32[]{:S(2)}, u32[]{:S(2)}) async-start(bf16[32,32,128]{2,1,0:T(8,128)(2,1)} %get-tuple-element.6), calls=%async_computation.2 | async-start | bytes 524288 | tf_op jit(solution)/shard_map/all_to_all | solution.py:157
  51.2 5.6 %collective-permute-start.3 = (bf16[2,16,512]{2,1,0:T(8,128)(2,1)S(1)}, bf16[2,16,512]{2,1,0:T(8,128)(2,1)S(1)}, u32[]{:S(2)}, u32[]{:S(2)}) collective-permute-start(bf16[2,16,512]{2,1,0:T(8,128)(2,1)S(1)} %get-tuple-element.7.vec), channel_id=1, source_target_pairs={{1,0},{2,1},{3,2},{4,3},{5,4},{6,5},{7,6},{8,7},{9,8},{10,9},{11,1... | collective-permute-start | bytes 98312 | tf_op jit(solution)/shard_map/ppermute | solution.py:161
  53.3 4.4 %collective-permute-start.2 = (bf16[2,16,512]{2,1,0:T(8,128)(2,1)S(1)}, bf16[2,16,512]{2,1,0:T(8,128)(2,1)S(1)}, u32[]{:S(2)}, u32[]{:S(2)}) collective-permute-start(bf16[2,16,512]{2,1,0:T(8,128)(2,1)S(1)} %get-tuple-element.7.vec), channel_id=1, source_target_pairs={{0,1},{1,2},{2,3},{3,4},{4,5},{5,6},{6,7},{7,8},{8,9},{9,10},{10,1... | collective-permute-start | bytes 98312 | tf_op jit(solution)/shard_map/ppermute | solution.py:161
  63.3 12.6 %all-to-all-start.3 = ((bf16[32,16,128]{2,1,0:T(8,128)(2,1)}), bf16[32,16,128]{2,1,0:T(8,128)(2,1)S(1)}, u32[]{:S(2)}, u32[]{:S(2)}) async-start(bf16[32,16,128]{2,1,0:T(8,128)(2,1)} %group_sums.3), calls=%async_computation.3 | async-start | bytes 262144 | tf_op jit(solution)/shard_map/all_to_all | solution.py:157

commit v3 on v2

--- a/solution.py
+++ b/solution.py
@@ -8,6 +8,7 @@
 
 REGION = ("yh", "x")
 BLK = ("z", "yl", "c")
+CHIPS = ("z", "yl")
 PLANE = ("yh", "x", "yl", "c")
 ALL = REGION + BLK
 NT = (((1,), (1,)), ((), ()))
@@ -39,44 +40,65 @@
     return acc[:16] + jnp.where(lane < 64, -crossed, crossed)
 
 
-def fill_sends(vec, ranks, inner_basis, outer_basis, send):
+def fill_pair(vec, ranks, inner_basis, outer_basis, give, keep):
     coeff = paired(nt(vec, inner_basis[...].reshape(128, 512)))
     lane = lax.broadcasted_iota(jnp.int32, (16, 128), 1)
     rank = jnp.where(lane < 64, lane, lane - 64)
-    coeff = jnp.where(rank < ranks[0], coeff, 0.0).astype(bf16)
+    coeff = jnp.where(rank < ranks[0], coeff, 0.0)
     real, imag = halves(nt(vec, outer_basis[...].reshape(512, 512)), 256)
-    quarters = (real[:, :128], real[:, 128:], imag[:, :128], imag[:, 128:])
-    quarters = [q.astype(bf16) for q in quarters]
-    for d in range(32):
-        send[d, :16] = coeff
-        send[d, 16:] = quarters[d % 4]
-
-
-def start_kernel(probes, inner_basis, outer_basis, ranks, send):
-    fill_sends(probes[...].reshape(32, 512), ranks, inner_basis, outer_basis, send)
-
-
-def sum_kernel(recv, before, after, send):
-    total = recv[0, 16:].astype(f32)
-    for j in range(1, 32):
-        total = total + recv[j, 16:].astype(f32)
+    core = lax.axis_index("c")
+    wide = jnp.concatenate([real, imag], 0)
+    low, high = wide[:, :128], wide[:, 128:]
+    keep[:16] = coeff.astype(bf16).astype(f32)
+    keep[16:] = jnp.where(core == 0, low, high)
+    give[:16] = coeff.astype(bf16)
+    give[16:48] = jnp.where(core == 0, high, low).astype(bf16)
+    for k in range(4):
+        give[48 + 32 * k : 80 + 32 * k] = vec[:, 128 * k : 128 * k + 128]
+
+
+def start_kernel(probes, inner_basis, outer_basis, ranks, give, keep):
+    fill_pair(probes[...].reshape(32, 512), ranks, inner_basis, outer_basis, give, keep)
+
+
+def pair_kernel(got, keep, send):
+    core = lax.axis_index("c")
+    mine, other = keep[:16].astype(bf16), got[:16]
+    even, odd = jnp.where(core == 0, mine, other), jnp.where(core == 0, other, mine)
+    quarters = (keep[16:] + got[16:48].astype(f32)).astype(bf16)
+    for d in range(16):
+        part = d % 2
+        send[d, :16] = even
+        send[d, 16:32] = odd
+        send[d, 32:] = quarters[16 * part : 16 * part + 16]
+
+
+def sum_kernel(recv, cross, send):
+    total = recv[0, 32:].astype(f32)
+    for j in range(1, 16):
+        total = total + recv[j, 32:].astype(f32)
     total = total.astype(bf16)
     for d in range(32):
         send[d] = total
 
 
-def local_kernel(before, vec, after, recv, near_blocks, coupling, inner_expand, out):
+def local_kernel(got, cross, vec, recv, near_blocks, coupling, inner_expand, out):
+    core = lax.axis_index("c")
+    partner = jnp.concatenate([got[48 + 32 * k : 80 + 32 * k] for k in range(4)], 1)
+    cross = cross[...].reshape(32, 512)
+    before, after = jnp.where(core == 0, cross, partner), jnp.where(core == 0, partner, cross)
     acc = None
-    for b, part in enumerate((before, vec, after)):
-        term = nt(part[...].reshape(32, 512), near_blocks[b].reshape(1024, 512))
+    for b, part in enumerate((before, vec[...].reshape(32, 512), after)):
+        term = nt(part, near_blocks[b].reshape(1024, 512))
         acc = term if acc is None else acc + term
     real, imag = halves(acc, 512)
     lane = lax.broadcasted_iota(jnp.int32, (16, 128), 1)
     position = lax.axis_index(BLK)
     res, ims = [], []
-    for j in range(0, 32, 2):
+    for j in range(16):
         first, second = (
-            jnp.where(jnp.abs(k - position) > 1, recv[k, :16].astype(f32), 0.0) for k in (j, j + 1)
+            jnp.where(jnp.abs(2 * j + k - position) > 1, recv[j, 16 * k : 16 * k + 16].astype(f32), 0.0)
+            for k in range(2)
         )
         res.append(jnp.where(lane < 64, first, pltpu.roll(second, 64, 1)))
         ims.append(jnp.where(lane < 64, pltpu.roll(first, 64, 1), second))
@@ -102,7 +124,7 @@
     return a[:16] - b[16:], a[16:] + b[:16]
 
 
-def middle_kernel(recv, coupling, expand, local, inner_hbm, outer_hbm, ranks, first, vec, send, *scratch):
+def middle_kernel(recv, coupling, expand, local, inner_hbm, outer_hbm, ranks, first, vec, give, keep, *scratch):
     inner_basis, outer_basis, sems = scratch
     copies = [
         pltpu.make_async_copy(inner_hbm, inner_basis, sems.at[0]),
@@ -119,7 +141,7 @@
     vec[1] = rows[16:]
     for copy in copies:
         copy.wait()
-    fill_sends(rows, ranks, inner_basis, outer_basis, send)
+    fill_pair(rows, ranks, inner_basis, outer_basis, give, keep)
 
 
 def last_kernel(recv, coupling, expand, local, second):
@@ -128,8 +150,8 @@
     second[1] = local[1] + imag
 
 
-UP = [(i, i + 1) for i in range(31)]
-DOWN = [(i + 1, i) for i in range(31)]
+PARTNER = [(i, i ^ 1) for i in range(32)]
+CROSS = [(i, i + 1) for i in range(1, 31, 2)] + [(i, i - 1) for i in range(2, 32, 2)]
 ANY = pl.BlockSpec(memory_space=pl.ANY)
 RANKS = pl.BlockSpec(memory_space=pltpu.SMEM)
 PARAMS = pltpu.CompilerParams(vmem_limit_bytes=16 * 1024 * 1024)
@@ -157,41 +179,47 @@
     return lax.all_to_all(value, axes, split_axis=0, concat_axis=0, tiled=True)
 
 
-def neighbours(vec):
-    return lax.ppermute(vec, BLK, UP), lax.ppermute(vec, BLK, DOWN)
-
-
-def local_terms(before, vec, after, recv, near_blocks, coupling, inner_expand):
-    args = in_vmem(before) + [vec] + in_vmem(after, recv) + in_hbm(near_blocks, coupling, inner_expand)
+def swapped(give, keep):
+    got = lax.ppermute(give, BLK, PARTNER)
+    args = in_vmem(got, keep)
+    return got, call(pair_kernel, [pltpu.VMEM((16, 48, 128), bf16)], *args)[0]
+
+
+def crossed(vec):
+    return lax.ppermute(vec, BLK, CROSS)
+
+
+def local_terms(got, cross, vec, recv, near_blocks, coupling, inner_expand):
+    args = in_vmem(got, cross) + [vec] + in_vmem(recv) + in_hbm(near_blocks, coupling, inner_expand)
     return call(local_kernel, [pltpu.VMEM((2, 16, 512), f32)], *args)[0]
 
 
-def group_sums(recv, before, after):
+def group_sums(recv, cross):
     send = pl.pallas_call(
         sum_kernel,
-        in_specs=vmem(1) + [ANY] * 2,
+        in_specs=vmem(1) + [ANY],
         out_specs=vmem(1)[0],
         out_shape=pltpu.VMEM((32, 16, 128), bf16),
         compiler_params=PARAMS,
         name="group_sums",
-    )(*in_vmem(recv), before, after)
+    )(*in_vmem(recv), cross)
     return exchange(send, PLANE)
 
 
 def local(probes, near_blocks, inner_basis, coupling, inner_expand, outer_basis, group_coupling, outer_expand, ranks):
-    sends = pltpu.VMEM((32, 32, 128), bf16)
-    send = call(start_kernel, [sends], *in_hbm(probes, inner_basis, outer_basis), ranks)[0]
-    recv = exchange(send, BLK)
-    before, after = neighbours(probes)
-    probes = in_hbm(probes)[0]
-    sums = group_sums(recv, before, after)
-    near = local_terms(before, probes, after, recv, near_blocks, coupling, inner_expand)
-    outs = [pltpu.VMEM((2, 16, 512), f32), pltpu.VMEM((2, 16, 512), bf16), sends]
+    pair = [pltpu.VMEM((176, 128), bf16), pltpu.VMEM((48, 128), f32)]
+    give, keep = call(start_kernel, pair, *in_hbm(probes, inner_basis, outer_basis), ranks)
+    got, send = swapped(give, keep)
+    recv = exchange(send, CHIPS)
+    cross = crossed(probes)
+    sums = group_sums(recv, cross)
+    near = local_terms(got, cross, *in_hbm(probes), recv, near_blocks, coupling, inner_expand)
+    outs = [pltpu.VMEM((2, 16, 512), f32), pltpu.VMEM((2, 16, 512), bf16)] + pair
     weights = in_vmem(group_coupling, outer_expand)
-    first, vec, send = pl.pallas_call(
+    first, vec, give, keep = pl.pallas_call(
         middle_kernel,
         in_specs=vmem(4) + [ANY] * 2 + [RANKS],
-        out_specs=vmem(3),
+        out_specs=vmem(4),
         out_shape=outs,
         scratch_shapes=[
             pltpu.VMEM(inner_basis.shape, bf16),
@@ -201,11 +229,11 @@
         compiler_params=PARAMS,
         name="middle",
     )(*in_vmem(sums), *weights, *in_vmem(near), *in_hbm(inner_basis, outer_basis), ranks)
-    recv = exchange(send, BLK)
-    before, after = neighbours(vec)
-    sums = group_sums(recv, before, after)
-    vec = in_vmem(vec)[0]
-    near = local_terms(before, vec, after, recv, near_blocks, coupling, inner_expand)
+    got, send = swapped(give, keep)
+    recv = exchange(send, CHIPS)
+    cross = crossed(vec)
+    sums = group_sums(recv, cross)
+    near = local_terms(got, cross, *in_vmem(vec), recv, near_blocks, coupling, inner_expand)
     args = in_vmem(sums) + weights + in_vmem(near)
     second = call(last_kernel, [jax.ShapeDtypeStruct((2, 16, 512), f32)], *args)[0]
     return first, second

time: 78.1 us -> 78 us (level)
  starting transfers between devices: 40.4 us -> 38.4 us
  waiting for transfers between devices: 19.5 us -> 21.4 us
    all_to_all x4, starting transfers between devices: 29.3 us -> 26.6 us  [exchange(): return lax.all_to_all(value, axes, split_axis=0, concat_axis=0, tiled=True)]
    all_to_all x4, waiting for transfers between devices: 14.4 us -> 15.5 us  [exchange(): return lax.all_to_all(value, axes, split_axis=0, concat_axis=0, tiled=True)]
    ppermute x4, waiting for transfers between devices: 5.05 us -> 5.91 us  [the longest x2 4.16 us: crossed(): return lax.ppermute(vec, BLK, CROSS)]
    pallas_call x4 -> x6, Pallas kernels: 10.9 us -> 11.4 us  [call(): pl.pallas_call(kernel, in_specs=[RANKS if a.dtype == jnp.int32 else vmem(...]
  transfers between devices with their start and end apart: 8 -> 8, of which waited for: 6 -> 8; matrix products, arithmetic and copies ran while one was open for 1% -> 1% of each run, Pallas kernels for 9% -> 9%
where the time goes in v3:
time: 78 us; the launch traced here: 77.4 us
  starting transfers between devices  38.4 us (49%)
  waiting for transfers between devices  21.4 us (27%)
  Pallas kernels  15.4 us (20%)
  between operations  1.56 us (2%)
    all_to_all x4, starting transfers between devices, exchange(): return lax.all_to_all(value, axes, split_axis=0, concat_axis=0, tiled=True)  26.6 us
    all_to_all x4, waiting for transfers between devices, exchange(): return lax.all_to_all(value, axes, split_axis=0, concat_axis=0, tiled=True)  15.5 us
    pallas_call x6, Pallas kernels, call(): pl.pallas_call(kernel, in_specs=[RANKS if a.dtype == jnp.int32 else vmem(...  11.4 us
    ppermute x2, starting transfers between devices, crossed(): return lax.ppermute(vec, BLK, CROSS)  7.72 us
    ppermute x2, waiting for transfers between devices, crossed(): return lax.ppermute(vec, BLK, CROSS)  4.16 us
    ppermute x2, starting transfers between devices, swapped(): got = lax.ppermute(give, BLK, PARTNER)  4.08 us
    pallas_call x1, Pallas kernels, local(): pl.pallas_call(middle_kernel, in_specs=vmem(4) + [ANY] * 2 + [RANKS], out...  2.63 us
    ppermute x2, waiting for transfers between devices, swapped(): got = lax.ppermute(give, BLK, PARTNER)  1.75 us
  transfers between devices with their start and end apart: 8, of which 8 were waited for; matrix products, arithmetic and copies ran while one was open for 1% of the time, Pallas kernels for 9%

profile of v3, /device:TPU:1, one launch (start us, length us, event | category | flops | bytes accessed | tf_op | source)
XLA Modules:
  0.0 77.4 jit_solution(11483905754884218899)
XLA Ops:
  0.6 0.0 copy-start
  0.6 0.0 copy-start.1
  1.4 1.5 %shard_map.104 = (bf16[176,128]{1,0:T(8,128)(2,1)S(1)}, f32[48,128]{1,0:T(8,128)S(1)}) custom-call(bf16[2,16,512]{2,1,0:T(8,128)(2,1)} %vec.1, bf16[2,64,512]{2,1,0:T(8,128)(2,1)} %inner_hbm.1, bf16[2,256,512]{2,1,0:T(8,128)(2,1)} %outer_hbm.1, s32[1]{0:T(128)S(6)} %copy.12.ranks), custom_call_target="tpu_custom_call" | custom-call | tf_op jit(solution)/shard_map/pallas_call | solution.py:169
  2.9 3.3 %collective-permute-start = (bf16[176,128]{1,0:T(8,128)(2,1)S(1)}, bf16[176,128]{1,0:T(8,128)(2,1)S(1)}, u32[]{:S(2)}, u32[]{:S(2)}) collective-permute-start(bf16[176,128]{1,0:T(8,128)(2,1)S(1)} %get-tuple-element.8), channel_id=1, source_target_pairs={{0,1},{1,0},{2,3},{3,2},{4,5},{5,4},{6,7},{7,6},{8,9},{9,8},{10,11... | collective-permute-start | bytes 135176 | tf_op jit(solution)/shard_map/ppermute | solution.py:183
  6.2 0.9 %collective-permute-done.got = bf16[176,128]{1,0:T(8,128)(2,1)S(1)} collective-permute-done((bf16[176,128]{1,0:T(8,128)(2,1)S(1)}, bf16[176,128]{1,0:T(8,128)(2,1)S(1)}, u32[]{:S(2)}, u32[]{:S(2)}) %collective-permute-start) | collective-permute-done | bytes 45088 | tf_op jit(solution)/shard_map/ppermute | solution.py:183
  7.0 0.7 shard_map.105
  7.7 7.6 %all-to-all-start = ((bf16[16,48,128]{2,1,0:T(8,128)(2,1)}), bf16[16,48,128]{2,1,0:T(8,128)(2,1)S(1)}, u32[]{:S(2)}, u32[]{:S(2)}) async-start(bf16[16,48,128]{2,1,0:T(8,128)(2,1)} %shard_map.105), calls=%async_computation | async-start | bytes 393216 | tf_op jit(solution)/shard_map/all_to_all | solution.py:179
  15.3 4.1 %collective-permute-start.1 = (bf16[2,16,512]{2,1,0:T(8,128)(2,1)}, bf16[2,16,512]{2,1,0:T(8,128)(2,1)S(1)}, u32[]{:S(2)}, u32[]{:S(2)}) collective-permute-start(bf16[2,16,512]{2,1,0:T(8,128)(2,1)} %vec.1), channel_id=1, source_target_pairs={{1,2},{3,4},{5,6},{7,8},{9,10},{11,12},{13,14},{15,16},{17,18},{19... | collective-permute-start | bytes 98312 | tf_op jit(solution)/shard_map/ppermute | solution.py:189
  19.4 2.1 %collective-permute-done.1.cross = bf16[2,16,512]{2,1,0:T(8,128)(2,1)S(1)} collective-permute-done((bf16[2,16,512]{2,1,0:T(8,128)(2,1)}, bf16[2,16,512]{2,1,0:T(8,128)(2,1)S(1)}, u32[]{:S(2)}, u32[]{:S(2)}) %collective-permute-start.1) | collective-permute-done | bytes 32800 | tf_op jit(solution)/shard_map/ppermute | solution.py:189
  21.5 3.5 %all-to-all-done.recv = bf16[16,48,128]{2,1,0:T(8,128)(2,1)S(1)} async-done(((bf16[16,48,128]{2,1,0:T(8,128)(2,1)}), bf16[16,48,128]{2,1,0:T(8,128)(2,1)S(1)}, u32[]{:S(2)}, u32[]{:S(2)}) %all-to-all-start) | async-done | bytes 196640 | tf_op jit(solution)/shard_map/all_to_all | solution.py:179
  25.0 0.7 group_sums.2
  25.7 9.6 %all-to-all-start.1 = ((bf16[32,16,128]{2,1,0:T(8,128)(2,1)}), bf16[32,16,128]{2,1,0:T(8,128)(2,1)S(1)}, u32[]{:S(2)}, u32[]{:S(2)}) async-start(bf16[32,16,128]{2,1,0:T(8,128)(2,1)} %group_sums.2), calls=%async_computation.1 | async-start | bytes 262144 | tf_op jit(solution)/shard_map/all_to_all | solution.py:179
  35.3 3.5 %shard_map.106.local = f32[2,16,512]{2,1,0:T(8,128)S(1)} custom-call(bf16[176,128]{1,0:T(8,128)(2,1)S(1)} %collective-permute-done.got, bf16[2,16,512]{2,1,0:T(8,128)(2,1)S(1)} %collective-permute-done.1.cross, bf16[2,16,512]{2,1,0:T(8,128)(2,1)} %vec.1, bf16[16,48,128]{2,1,0:T(8,128)(2,1)S(1)} %all-to-all-done.recv, bf16[3,2,512,512]{3,2,1,0:T(8,128)(2,1)} %near_blocks.3, ...), custom_call_target="tpu_custom_call" | custom-call | tf_op jit(solution)/shard_map/pallas_call | solution.py:169
  38.8 4.2 %all-to-all-done.1.recv = bf16[32,16,128]{2,1,0:T(8,128)(2,1)S(1)} async-done(((bf16[32,16,128]{2,1,0:T(8,128)(2,1)}), bf16[32,16,128]{2,1,0:T(8,128)(2,1)S(1)}, u32[]{:S(2)}, u32[]{:S(2)}) %all-to-all-start.1) | async-done | bytes 131104 | tf_op jit(solution)/shard_map/all_to_all | solution.py:179
  42.9 0.0 copy-done
  42.9 0.0 copy-done.1
  42.9 2.6 %middle.1 = (f32[2,16,512]{2,1,0:T(8,128)S(1)}, bf16[2,16,512]{2,1,0:T(8,128)(2,1)S(1)}, bf16[176,128]{1,0:T(8,128)(2,1)S(1)}, f32[48,128]{1,0:T(8,128)S(1)}) custom-call(bf16[32,16,128]{2,1,0:T(8,128)(2,1)S(1)} %all-to-all-done.1.recv, bf16[2,256,2048]{2,1,0:T(8,128)(2,1)S(1)} %copy-done, bf16[2,256,512]{2,1,0:T(8,128)(2,1)S(1)} %copy-done.1, ...), custom_call_target="tpu_custom_call" | custom-call | tf_op jit(solution)/shard_map/middle/pallas_call | solution.py:219
  45.6 0.8 %collective-permute-start.2 = (bf16[176,128]{1,0:T(8,128)(2,1)S(1)}, bf16[176,128]{1,0:T(8,128)(2,1)S(1)}, u32[]{:S(2)}, u32[]{:S(2)}) collective-permute-start(bf16[176,128]{1,0:T(8,128)(2,1)S(1)} %get-tuple-element.11), channel_id=1, source_target_pairs={{0,1},{1,0},{2,3},{3,2},{4,5},{5,4},{6,7},{7,6},{8,9},{9,8},{10,11... | collective-permute-start | bytes 135176 | tf_op jit(solution)/shard_map/ppermute | solution.py:183
  46.4 0.9 %collective-permute-done.2.got = bf16[176,128]{1,0:T(8,128)(2,1)S(1)} collective-permute-done((bf16[176,128]{1,0:T(8,128)(2,1)S(1)}, bf16[176,128]{1,0:T(8,128)(2,1)S(1)}, u32[]{:S(2)}, u32[]{:S(2)}) %collective-permute-start.2) | collective-permute-done | bytes 45088 | tf_op jit(solution)/shard_map/ppermute | solution.py:183
  47.3 0.7 shard_map.107
  48.0 3.5 %all-to-all-start.2 = ((bf16[16,48,128]{2,1,0:T(8,128)(2,1)}), bf16[16,48,128]{2,1,0:T(8,128)(2,1)S(1)}, u32[]{:S(2)}, u32[]{:S(2)}) async-start(bf16[16,48,128]{2,1,0:T(8,128)(2,1)} %shard_map.107), calls=%async_computation.2 | async-start | bytes 393216 | tf_op jit(solution)/shard_map/all_to_all | solution.py:179
  51.5 3.7 %collective-permute-start.3 = (bf16[2,16,512]{2,1,0:T(8,128)(2,1)S(1)}, bf16[2,16,512]{2,1,0:T(8,128)(2,1)S(1)}, u32[]{:S(2)}, u32[]{:S(2)}) collective-permute-start(bf16[2,16,512]{2,1,0:T(8,128)(2,1)S(1)} %get-tuple-element.13.vec), channel_id=1, source_target_pairs={{1,2},{3,4},{5,6},{7,8},{9,10},{11,12},{13,14},{15,16},{17,18},{19... | collective-permute-start | bytes 98312 | tf_op jit(solution)/shard_map/ppermute | solution.py:189
  55.2 2.1 %collective-permute-done.3.cross = bf16[2,16,512]{2,1,0:T(8,128)(2,1)S(1)} collective-permute-done((bf16[2,16,512]{2,1,0:T(8,128)(2,1)S(1)}, bf16[2,16,512]{2,1,0:T(8,128)(2,1)S(1)}, u32[]{:S(2)}, u32[]{:S(2)}) %collective-permute-start.3) | collective-permute-done | bytes 32800 | tf_op jit(solution)/shard_map/ppermute | solution.py:189
  57.3 4.2 %all-to-all-done.2.recv = bf16[16,48,128]{2,1,0:T(8,128)(2,1)S(1)} async-done(((bf16[16,48,128]{2,1,0:T(8,128)(2,1)}), bf16[16,48,128]{2,1,0:T(8,128)(2,1)S(1)}, u32[]{:S(2)}, u32[]{:S(2)}) %all-to-all-start.2) | async-done | bytes 196640 | tf_op jit(solution)/shard_map/all_to_all | solution.py:179
  61.5 0.7 group_sums.3
  62.1 5.9 %all-to-all-start.3 = ((bf16[32,16,128]{2,1,0:T(8,128)(2,1)}), bf16[32,16,128]{2,1,0:T(8,128)(2,1)S(1)}, u32[]{:S(2)}, u32[]{:S(2)}) async-start(bf16[32,16,128]{2,1,0:T(8,128)(2,1)} %group_sums.3), calls=%async_computation.3 | async-start | bytes 262144 | tf_op jit(solution)/shard_map/all_to_all | solution.py:179
  68.0 0.6 copy.11
  68.7 3.5 %shard_map.108.local = f32[2,16,512]{2,1,0:T(8,128)S(1)} custom-call(bf16[176,128]{1,0:T(8,128)(2,1)S(1)} %collective-permute-done.2.got, bf16[2,16,512]{2,1,0:T(8,128)(2,1)S(1)} %collective-permute-done.3.cross, bf16[2,16,512]{2,1,0:T(8,128)(2,1)S(1)} %get-tuple-element.13.vec, bf16[16,48,128]{2,1,0:T(8,128)(2,1)S(1)} %all-to-all-done.2.recv, ...), custom_call_target="tpu_custom_call" | custom-call | tf_op jit(solution)/shard_map/pallas_call | solution.py:169
  72.2 3.6 %all-to-all-done.3.recv = bf16[32,16,128]{2,1,0:T(8,128)(2,1)S(1)} async-done(((bf16[32,16,128]{2,1,0:T(8,128)(2,1)}), bf16[32,16,128]{2,1,0:T(8,128)(2,1)S(1)}, u32[]{:S(2)}, u32[]{:S(2)}) %all-to-all-start.3) | async-done | bytes 131104 | tf_op jit(solution)/shard_map/all_to_all | solution.py:179
  75.8 1.6 %shard_map.109 = f32[2,16,512]{2,1,0:T(8,128)} custom-call(bf16[32,16,128]{2,1,0:T(8,128)(2,1)S(1)} %all-to-all-done.3.recv, bf16[2,256,2048]{2,1,0:T(8,128)(2,1)S(1)} %copy-done, bf16[2,256,512]{2,1,0:T(8,128)(2,1)S(1)} %copy-done.1, f32[2,16,512]{2,1,0:T(8,128)S(1)} %shard_map.108.local), custom_call_target="tpu_custom_call" | custom-call | tf_op jit(solution)/shard_map/pallas_call | solution.py:169
Async XLA Ops:
  0.6 42.3 %copy-start = (bf16[2,256,2048]{2,1,0:T(8,128)(2,1)S(1)}, bf16[2,256,2048]{2,1,0:T(8,128)(2,1)}, u32[]{:S(2)}) copy-start(bf16[2,256,2048]{2,1,0:T(8,128)(2,1)} %coupling.7) | copy-start | bytes 6291460
  0.6 42.3 %copy-start.1 = (bf16[2,256,512]{2,1,0:T(8,128)(2,1)S(1)}, bf16[2,256,512]{2,1,0:T(8,128)(2,1)}, u32[]{:S(2)}) copy-start(bf16[2,256,512]{2,1,0:T(8,128)(2,1)} %expand.3) | copy-start | bytes 1572868
  2.9 4.1 %collective-permute-start = (bf16[176,128]{1,0:T(8,128)(2,1)S(1)}, bf16[176,128]{1,0:T(8,128)(2,1)S(1)}, u32[]{:S(2)}, u32[]{:S(2)}) collective-permute-start(bf16[176,128]{1,0:T(8,128)(2,1)S(1)} %get-tuple-element.8), channel_id=1, source_target_pairs={{0,1},{1,0},{2,3},{3,2},{4,5},{5,4},{6,7},{7,6},{8,9},{9,8},{10,11... | collective-permute-start | bytes 135176 | tf_op jit(solution)/shard_map/ppermute | solution.py:183
  7.7 17.2 %all-to-all-start = ((bf16[16,48,128]{2,1,0:T(8,128)(2,1)}), bf16[16,48,128]{2,1,0:T(8,128)(2,1)S(1)}, u32[]{:S(2)}, u32[]{:S(2)}) async-start(bf16[16,48,128]{2,1,0:T(8,128)(2,1)} %shard_map.105), calls=%async_computation | async-start | bytes 393216 | tf_op jit(solution)/shard_map/all_to_all | solution.py:179
  15.3 6.2 %collective-permute-start.1 = (bf16[2,16,512]{2,1,0:T(8,128)(2,1)}, bf16[2,16,512]{2,1,0:T(8,128)(2,1)S(1)}, u32[]{:S(2)}, u32[]{:S(2)}) collective-permute-start(bf16[2,16,512]{2,1,0:T(8,128)(2,1)} %vec.1), channel_id=1, source_target_pairs={{1,2},{3,4},{5,6},{7,8},{9,10},{11,12},{13,14},{15,16},{17,18},{19... | collective-permute-start | bytes 98312 | tf_op jit(solution)/shard_map/ppermute | solution.py:189
  25.7 17.3 %all-to-all-start.1 = ((bf16[32,16,128]{2,1,0:T(8,128)(2,1)}), bf16[32,16,128]{2,1,0:T(8,128)(2,1)S(1)}, u32[]{:S(2)}, u32[]{:S(2)}) async-start(bf16[32,16,128]{2,1,0:T(8,128)(2,1)} %group_sums.2), calls=%async_computation.1 | async-start | bytes 262144 | tf_op jit(solution)/shard_map/all_to_all | solution.py:179
  45.6 1.7 %collective-permute-start.2 = (bf16[176,128]{1,0:T(8,128)(2,1)S(1)}, bf16[176,128]{1,0:T(8,128)(2,1)S(1)}, u32[]{:S(2)}, u32[]{:S(2)}) collective-permute-start(bf16[176,128]{1,0:T(8,128)(2,1)S(1)} %get-tuple-element.11), channel_id=1, source_target_pairs={{0,1},{1,0},{2,3},{3,2},{4,5},{5,4},{6,7},{7,6},{8,9},{9,8},{10,11... | collective-permute-start | bytes 135176 | tf_op jit(solution)/shard_map/ppermute | solution.py:183
  48.0 13.5 %all-to-all-start.2 = ((bf16[16,48,128]{2,1,0:T(8,128)(2,1)}), bf16[16,48,128]{2,1,0:T(8,128)(2,1)S(1)}, u32[]{:S(2)}, u32[]{:S(2)}) async-start(bf16[16,48,128]{2,1,0:T(8,128)(2,1)} %shard_map.107), calls=%async_computation.2 | async-start | bytes 393216 | tf_op jit(solution)/shard_map/all_to_all | solution.py:179
  51.5 5.7 %collective-permute-start.3 = (bf16[2,16,512]{2,1,0:T(8,128)(2,1)S(1)}, bf16[2,16,512]{2,1,0:T(8,128)(2,1)S(1)}, u32[]{:S(2)}, u32[]{:S(2)}) collective-permute-start(bf16[2,16,512]{2,1,0:T(8,128)(2,1)S(1)} %get-tuple-element.13.vec), channel_id=1, source_target_pairs={{1,2},{3,4},{5,6},{7,8},{9,10},{11,12},{13,14},{15,16},{17,18},{19... | collective-permute-start | bytes 98312 | tf_op jit(solution)/shard_map/ppermute | solution.py:189
  62.1 13.7 %all-to-all-start.3 = ((bf16[32,16,128]{2,1,0:T(8,128)(2,1)}), bf16[32,16,128]{2,1,0:T(8,128)(2,1)S(1)}, u32[]{:S(2)}, u32[]{:S(2)}) async-start(bf16[32,16,128]{2,1,0:T(8,128)(2,1)} %group_sums.3), calls=%async_computation.3 | async-start | bytes 262144 | tf_op jit(solution)/shard_map/all_to_all | solution.py:179

commit v4 on v3

v4 whole, which is shorter than its diff:
```python
import jax
import jax.numpy as jnp
from jax import lax
from jax.experimental import pallas as pl
from jax.experimental.pallas import tpu as pltpu
from jax.sharding import Mesh
from jax.sharding import PartitionSpec as P

REGION = ("yh", "x")
BLK = ("z", "yl", "c")
CHIPS = ("z", "yl")
PLANE = ("yh", "x", "yl", "c")
ALL = REGION + BLK
NT = (((1,), (1,)), ((), ()))
f32 = jnp.float32
bf16 = jnp.bfloat16


def vmem(n):
    return [pl.BlockSpec(memory_space=pltpu.VMEM)] * n


def nt(rows, mat):
    return lax.dot_general(rows, mat, NT, preferred_element_type=f32)


def nn(rows, mat):
    return jnp.dot(rows, mat, preferred_element_type=f32)


def halves(acc, width):
    real = acc[:16, :width] - acc[16:, width:]
    imag = acc[:16, width:] + acc[16:, :width]
    return real, imag


def paired(acc):
    lane = lax.broadcasted_iota(jnp.int32, (16, 128), 1)
    crossed = pltpu.roll(acc[16:], 64, 1)
    return acc[:16] + jnp.where(lane < 64, -crossed, crossed)


def fill_pair(vec, inner_basis, outer_basis, give, keep):
    real, imag = halves(nt(vec, outer_basis[...].reshape(512, 512)), 256)
    core = lax.axis_index("c")
    wide = jnp.concatenate([real, imag], 0)
    low, high = wide[:, :128], wide[:, 128:]
    keep[:16] = paired(nt(vec, inner_basis[...].reshape(128, 512)))
    keep[16:] = jnp.where(core == 0, low, high)
    give[:32] = jnp.where(core == 0, high, low).astype(bf16)
    for k in range(4):
        give[32 + 32 * k : 64 + 32 * k] = vec[:, 128 * k : 128 * k + 128]


def start_kernel(probes, inner_basis, outer_basis, give, keep):
    fill_pair(probes[...].reshape(32, 512), inner_basis, outer_basis, give, keep)


def pair_kernel(got, keep, ranks, send):
    lane = lax.broadcasted_iota(jnp.int32, (16, 128), 1)
    rank = jnp.where(lane < 64, lane, lane - 64)
    coeff = jnp.where(rank < ranks[0], keep[:16], 0.0).astype(bf16)
    quarters = (keep[16:] + got[:32].astype(f32)).astype(bf16)
    for d in range(16):
        part = d % 2
        send[d, :16] = coeff
        send[d, 16:] = quarters[16 * part : 16 * part + 16]


def sum_kernel(recv, send):
    total = recv[0, 16:].astype(f32)
    for j in range(1, 16):
        total = total + recv[j, 16:].astype(f32)
    total = total.astype(bf16)
    for d in range(32):
        send[d] = total


def near_kernel(got, vec, blocks_hbm, out, blocks, sems):
    other = 2 - 2 * lax.axis_index("c")
    copies = [
        pltpu.make_async_copy(blocks_hbm.at[source], blocks.at[slot], sems.at[slot])
        for slot, source in enumerate((1, other))
    ]
    for copy in copies:
        copy.start()
    partner = jnp.concatenate([got[32 + 32 * k : 64 + 32 * k] for k in range(4)], 1)
    copies[0].wait()
    acc = nt(vec[...].reshape(32, 512), blocks[0].reshape(1024, 512))
    copies[1].wait()
    acc = acc + nt(partner, blocks[1].reshape(1024, 512))
    out[0], out[1] = halves(acc, 512)


def terms_kernel(near, cross, recv, other, blocks_hbm, coupling_hbm, expand_hbm, out, block, coupling, expand, sems):
    core = lax.axis_index("c")
    copies = [
        pltpu.make_async_copy(coupling_hbm, coupling, sems.at[0]),
        pltpu.make_async_copy(expand_hbm, expand, sems.at[1]),
        pltpu.make_async_copy(blocks_hbm.at[2 * core], block, sems.at[2]),
    ]
    for copy in copies:
        copy.start()
    lane = lax.broadcasted_iota(jnp.int32, (16, 128), 1)
    position = lax.axis_index(BLK)
    res, ims = [], []
    for j in range(16):
        mine, theirs = (ref[j, :16].astype(f32) for ref in (recv, other))
        first, second = jnp.where(core == 0, mine, theirs), jnp.where(core == 0, theirs, mine)
        first = jnp.where(jnp.abs(2 * j - position) > 1, first, 0.0)
        second = jnp.where(jnp.abs(2 * j + 1 - position) > 1, second, 0.0)
        res.append(jnp.where(lane < 64, first, pltpu.roll(second, 64, 1)))
        ims.append(jnp.where(lane < 64, pltpu.roll(first, 64, 1), second))
    rows = jnp.concatenate([jnp.concatenate(res, 1), jnp.concatenate(ims, 1)], 0).astype(bf16)
    copies[0].wait()
    inner = paired(nt(rows, coupling[...].reshape(128, 2048)))
    rows = jnp.concatenate([inner[:, :64], pltpu.roll(inner, 64, 1)[:, :64]], 0).astype(bf16)
    copies[1].wait()
    a, b = nn(rows, expand[0]), nn(rows, expand[1])
    copies[2].wait()
    real, imag = halves(nt(cross[...].reshape(32, 512), block[...].reshape(1024, 512)), 512)
    out[0] = near[0] + real + (a[:16] - b[16:])
    out[1] = near[1] + imag + (a[16:] + b[:16])


def field_part(recv, coupling, expand):
    region = lax.axis_index(REGION)
    res, ims = [], []
    for s in range(8):
        tiles = [jnp.where(s != region, recv[4 * s + q], jnp.zeros((16, 128), bf16)) for q in range(4)]
        res += tiles[:2]
        ims += tiles[2:]
    rows = jnp.concatenate([jnp.concatenate(res, 1), jnp.concatenate(ims, 1)], 0)
    real, imag = halves(nt(rows, coupling[...].reshape(512, 2048)), 256)
    rows = jnp.concatenate([real, imag], 0).astype(bf16)
    a, b = nn(rows, expand[0]), nn(rows, expand[1])
    return a[:16] - b[16:], a[16:] + b[:16]


def middle_kernel(recv, coupling, expand, local, inner_hbm, outer_hbm, first_hbm, vec, give, keep, *scratch):
    inner_basis, outer_basis, first, sems = scratch
    copies = [
        pltpu.make_async_copy(inner_hbm, inner_basis, sems.at[0]),
        pltpu.make_async_copy(outer_hbm, outer_basis, sems.at[1]),
    ]
    for copy in copies:
        copy.start()
    real, imag = field_part(recv, coupling, expand)
    real, imag = local[0] + real, local[1] + imag
    first[0] = real
    first[1] = imag
    result = pltpu.make_async_copy(first, first_hbm, sems.at[2])
    result.start()
    rows = jnp.concatenate([real, imag], 0).astype(bf16)
    vec[0] = rows[:16]
    vec[1] = rows[16:]
    for copy in copies:
        copy.wait()
    fill_pair(rows, inner_basis, outer_basis, give, keep)
    result.wait()


def last_kernel(recv, coupling, expand, local, second):
    real, imag = field_part(recv, coupling, expand)
    second[0] = local[0] + real
    second[1] = local[1] + imag


PARTNER = [(i, i ^ 1) for i in range(32)]
CROSS = [(i, i + 1) for i in range(1, 31, 2)] + [(i, i - 1) for i in range(2, 32, 2)]
ANY = pl.BlockSpec(memory_space=pl.ANY)
RANKS = pl.BlockSpec(memory_space=pltpu.SMEM)
PARAMS = pltpu.CompilerParams(vmem_limit_bytes=16 * 1024 * 1024)


def in_vmem(*arrays):
    return [pltpu.with_memory_space_constraint(a, pltpu.VMEM) for a in arrays]


def in_hbm(*arrays):
    return [pltpu.with_memory_space_constraint(a, pltpu.HBM) for a in arrays]


def call(kernel, outs, *args):
    return pl.pallas_call(
        kernel,
        in_specs=vmem(len(args)),
        out_specs=vmem(len(outs)),
        out_shape=outs,
        compiler_params=PARAMS,
    )(*args)


def exchange(value, axes):
    return lax.all_to_all(value, axes, split_axis=0, concat_axis=0, tiled=True)


def swapped(give, keep, ranks):
    got = lax.ppermute(give, BLK, PARTNER)
    send = pl.pallas_call(
        pair_kernel,
        in_specs=vmem(2) + [RANKS],
        out_specs=vmem(1)[0],
        out_shape=pltpu.VMEM((16, 32, 128), bf16),
        compiler_params=PARAMS,
        name="pair_sums",
    )(*in_vmem(got, keep), ranks)
    return got, send


def crossed(vec):
    return lax.ppermute(vec, BLK, CROSS)


def near_terms(got, vec, near_blocks):
    return pl.pallas_call(
        near_kernel,
        in_specs=vmem(2) + [ANY],
        out_specs=vmem(1)[0],
        out_shape=pltpu.VMEM((2, 16, 512), f32),
        scratch_shapes=[pltpu.VMEM((2, 2, 512, 512), bf16), pltpu.SemaphoreType.DMA((2,))],
        compiler_params=PARAMS,
        name="near_terms",
    )(*in_vmem(got), vec, *in_hbm(near_blocks))


def local_terms(near, cross, recv, near_blocks, coupling, inner_expand):
    other = lax.ppermute(recv, BLK, PARTNER)
    return pl.pallas_call(
        terms_kernel,
        in_specs=vmem(4) + [ANY] * 3,
        out_specs=vmem(1)[0],
        out_shape=pltpu.VMEM((2, 16, 512), f32),
        scratch_shapes=[
            pltpu.VMEM((2, 512, 512), bf16),
            pltpu.VMEM(coupling.shape, bf16),
            pltpu.VMEM(inner_expand.shape, bf16),
            pltpu.SemaphoreType.DMA((3,)),
        ],
        compiler_params=PARAMS,
        name="local_terms",
    )(*in_vmem(near, cross, recv, other), *in_hbm(near_blocks, coupling, inner_expand))


def group_sums(recv):
    send = call(sum_kernel, [pltpu.VMEM((32, 16, 128), bf16)], *in_vmem(recv))[0]
    return exchange(send, PLANE)


def local(probes, near_blocks, inner_basis, coupling, inner_expand, outer_basis, group_coupling, outer_expand, ranks):
    pair = [pltpu.VMEM((160, 128), bf16), pltpu.VMEM((48, 128), f32)]
    give, keep = pl.pallas_call(
        start_kernel,
        in_specs=vmem(3),
        out_specs=vmem(2),
        out_shape=pair,
        compiler_params=PARAMS,
        name="start",
    )(*in_hbm(probes, inner_basis, outer_basis))
    got, send = swapped(give, keep, ranks)
    recv = exchange(send, CHIPS)
    cross = crossed(probes)
    sums = group_sums(recv)
    near = near_terms(got, *in_hbm(probes), near_blocks)
    near = local_terms(near, cross, recv, near_blocks, coupling, inner_expand)
    outs = [jax.ShapeDtypeStruct((2, 16, 512), f32), pltpu.VMEM((2, 16, 512), bf16)] + pair
    weights = in_vmem(group_coupling, outer_expand)
    first, vec, give, keep = pl.pallas_call(
        middle_kernel,
        in_specs=vmem(4) + [ANY] * 2,
        out_specs=[ANY] + vmem(3),
        out_shape=outs,
        scratch_shapes=[
            pltpu.VMEM(inner_basis.shape, bf16),
            pltpu.VMEM(outer_basis.shape, bf16),
            pltpu.VMEM((2, 16, 512), f32),
            pltpu.SemaphoreType.DMA((3,)),
        ],
        compiler_params=PARAMS,
        name="middle",
    )(*in_vmem(sums), *weights, *in_vmem(near), *in_hbm(inner_basis, outer_basis))
    got, send = swapped(give, keep, ranks)
    recv = exchange(send, CHIPS)
    cross = crossed(vec)
    sums = group_sums(recv)
    near = near_terms(got, *in_vmem(vec), near_blocks)
    near = local_terms(near, cross, recv, near_blocks, coupling, inner_expand)
    args = in_vmem(sums) + weights + in_vmem(near)
    second = call(last_kernel, [jax.ShapeDtypeStruct((2, 16, 512), f32)], *args)[0]
    return first, second


def solution(mesh):
    fine = Mesh(mesh.devices.reshape(2, 4, 8, 2, 2), ALL)
    placed = (
        P(None, None, ALL),
        P(None, None, ALL, None),
        P(None, None, ALL),
        P(None, ALL, None),
        P(None, None, ALL),
        P(None, None, ALL),
        P(None, REGION, None),
        P(None, None, ALL),
        P(ALL),
    )
    return jax.shard_map(
        local,
        mesh=fine,
        in_specs=placed,
        out_specs=(P(None, None, ALL), P(None, None, ALL)),
        check_vma=False,
    )
```

time: 78 us -> 77.2 us (0.990)
  blocking collectives: 0 us -> 28.3 us
  waiting for transfers between devices: 21.4 us -> 1.44 us
  starting transfers between devices: 38.4 us -> 28.1 us
  Pallas kernels: 15.4 us -> 17.2 us
    all_to_all x0 -> x2, blocking collectives: none -> 28.3 us  [exchange(): return lax.all_to_all(value, axes, split_axis=0, concat_axis=0, tiled=True)]
    all_to_all x4 -> x2, waiting for transfers between devices: 15.5 us -> 0.01 us  [exchange(): return lax.all_to_all(value, axes, split_axis=0, concat_axis=0, tiled=True)]
    all_to_all x4 -> x2, starting transfers between devices: 26.6 us -> 13.6 us  [exchange(): return lax.all_to_all(value, axes, split_axis=0, concat_axis=0, tiled=True)]
    ppermute x2, waiting for transfers between devices: 4.16 us -> 0.01 us  [crossed(): return lax.ppermute(vec, BLK, CROSS)]
    ppermute x0 -> x2, starting transfers between devices: none -> 3.94 us  [local_terms(): other = lax.ppermute(recv, BLK, PARTNER)]
    pallas_call x9 -> x11, Pallas kernels: 15.4 us -> 17.2 us  [the longest x2 5.33 us: near_terms(): pl.pallas_call(near_kernel, in_specs=vmem(2) + [ANY], out_specs=vmem(1)[0...]
  transfers between devices with their start and end apart: 8 -> 8, of which waited for: 8 -> 2; matrix products, arithmetic and copies ran while one was open for 1% -> 0% of each run, Pallas kernels for 9% -> 15%
where the time goes in v4:
time: 77.2 us; the launch traced here: 76.6 us
  blocking collectives  28.3 us (37%)
  starting transfers between devices  28.1 us (36%)
  Pallas kernels  17.2 us (22%)
  between operations  1.46 us (2%)
  waiting for transfers between devices  1.44 us (2%)
    all_to_all x2, blocking collectives, exchange(): return lax.all_to_all(value, axes, split_axis=0, concat_axis=0, tiled=True)  28.3 us
    all_to_all x2, starting transfers between devices, exchange(): return lax.all_to_all(value, axes, split_axis=0, concat_axis=0, tiled=True)  13.6 us
    ppermute x2, starting transfers between devices, crossed(): return lax.ppermute(vec, BLK, CROSS)  7.21 us
    pallas_call x2, Pallas kernels, near_terms(): pl.pallas_call(near_kernel, in_specs=vmem(2) + [ANY], out_specs=vmem(1)[0...  5.33 us
    pallas_call x2, Pallas kernels, local_terms(): pl.pallas_call(terms_kernel, in_specs=vmem(4) + [ANY] * 3, out_specs=vmem...  4.7 us
    ppermute x2, starting transfers between devices, local_terms(): other = lax.ppermute(recv, BLK, PARTNER)  3.94 us
    ppermute x2, starting transfers between devices, swapped(): got = lax.ppermute(give, BLK, PARTNER)  3.38 us
    pallas_call x3, Pallas kernels, call(): pl.pallas_call(kernel, in_specs=vmem(len(args)), out_specs=vmem(len(outs)...  2.99 us
  transfers between devices with their start and end apart: 8, of which 2 were waited for; matrix products, arithmetic and copies ran while one was open for 0% of the time, Pallas kernels for 15%

profile of v4, /device:TPU:1, one launch (start us, length us, event | category | flops | bytes accessed | tf_op | source)
XLA Modules:
  0.0 76.6 jit_solution(13671707661993485691)
XLA Ops:
  0.6 1.5 %start.1 = (bf16[160,128]{1,0:T(8,128)(2,1)S(1)}, f32[48,128]{1,0:T(8,128)S(1)}) custom-call(bf16[2,16,512]{2,1,0:T(8,128)(2,1)} %vec.1, bf16[2,64,512]{2,1,0:T(8,128)(2,1)} %inner_hbm.1, bf16[2,256,512]{2,1,0:T(8,128)(2,1)} %outer_hbm.1), custom_call_target="tpu_custom_call" | custom-call | tf_op jit(solution)/shard_map/start/pallas_call | solution.py:252
  2.1 3.3 %collective-permute-start = (bf16[160,128]{1,0:T(8,128)(2,1)S(1)}, bf16[160,128]{1,0:T(8,128)(2,1)S(1)}, u32[]{:S(2)}, u32[]{:S(2)}) collective-permute-start(bf16[160,128]{1,0:T(8,128)(2,1)S(1)} %get-tuple-element.8), channel_id=1, source_target_pairs={{0,1},{1,0},{2,3},{3,2},{4,5},{5,4},{6,7},{7,6},{8,9},{9,8},{10,11... | collective-permute-start | bytes 122888 | tf_op jit(solution)/shard_map/ppermute | solution.py:199
  6.0 0.2 collective-permute-done.got
  6.3 15.9 %all_to_all.20.recv = bf16[16,32,128]{2,1,0:T(8,128)(2,1)S(1)} all-to-all(bf16[16,32,128]{2,1,0:T(8,128)(2,1)S(1)} %pair_sums.2), channel_id=1, replica_groups=mesh['yh'=2,'x'=4,'z'=8,'yl'=2,'c'=2] {'z','yl'}, dimensions={0} | all-to-all | bytes 262144 | tf_op jit(solution)/shard_map/all_to_all | solution.py:195
  22.2 2.0 %collective-permute-start.2 = (bf16[16,32,128]{2,1,0:T(8,128)(2,1)S(1)}, bf16[16,32,128]{2,1,0:T(8,128)(2,1)S(1)}, u32[]{:S(2)}, u32[]{:S(2)}) collective-permute-start(bf16[16,32,128]{2,1,0:T(8,128)(2,1)S(1)} %all_to_all.20.recv), channel_id=1, source_target_pairs={{0,1},{1,0},{2,3},{3,2},{4,5},{5,4},{6,7},{7,6},{8,9},{9,8},{10,11... | collective-permute-start | bytes 393224 | tf_op jit(solution)/shard_map/ppermute | solution.py:228
  24.2 0.7 shard_map.104
  24.9 6.9 %all-to-all-start.1 = ((bf16[32,16,128]{2,1,0:T(8,128)(2,1)}), bf16[32,16,128]{2,1,0:T(8,128)(2,1)S(1)}, u32[]{:S(2)}, u32[]{:S(2)}) async-start(bf16[32,16,128]{2,1,0:T(8,128)(2,1)} %shard_map.104), calls=%async_computation.1 | async-start | bytes 262144 | tf_op jit(solution)/shard_map/all_to_all | solution.py:195
  31.8 0.0 copy-start
  31.8 0.0 copy-start.1
  31.9 3.7 %collective-permute-start.1 = (bf16[2,16,512]{2,1,0:T(8,128)(2,1)}, bf16[2,16,512]{2,1,0:T(8,128)(2,1)S(1)}, u32[]{:S(2)}, u32[]{:S(2)}) collective-permute-start(bf16[2,16,512]{2,1,0:T(8,128)(2,1)} %vec.1), channel_id=1, source_target_pairs={{1,2},{3,4},{5,6},{7,8},{9,10},{11,12},{13,14},{15,16},{17,18},{19... | collective-permute-start | bytes 98312 | tf_op jit(solution)/shard_map/ppermute | solution.py:212
  35.5 3.0 %near_terms.2.near = f32[2,16,512]{2,1,0:T(8,128)S(1)} custom-call(bf16[160,128]{1,0:T(8,128)(2,1)S(1)} %collective-permute-done.got, bf16[2,16,512]{2,1,0:T(8,128)(2,1)} %vec.1, bf16[3,2,512,512]{3,2,1,0:T(8,128)(2,1)} %blocks_hbm.7), custom_call_target="tpu_custom_call" | custom-call | tf_op jit(solution)/shard_map/near_terms/pallas_call | solution.py:216
  38.6 0.0 collective-permute-done.1.cross
  38.6 0.0 collective-permute-done.2.other
  38.6 2.3 %local_terms.2.local = f32[2,16,512]{2,1,0:T(8,128)S(1)} custom-call(f32[2,16,512]{2,1,0:T(8,128)S(1)} %near_terms.2.near, bf16[2,16,512]{2,1,0:T(8,128)(2,1)S(1)} %collective-permute-done.1.cross, bf16[16,32,128]{2,1,0:T(8,128)(2,1)S(1)} %all_to_all.20.recv, bf16[16,32,128]{2,1,0:T(8,128)(2,1)S(1)} %collective-permute-done.2.other, ...), custom_call_target="tpu_custom_call" | custom-call | tf_op jit(solution)/shard_map/local_terms/pallas_call | solution.py:229
  41.0 0.0 all-to-all-done.1.recv
  41.0 0.0 copy-done
  41.0 0.0 copy-done.1
  41.0 2.7 %middle.1 = (f32[2,16,512]{2,1,0:T(8,128)}, bf16[2,16,512]{2,1,0:T(8,128)(2,1)S(1)}, bf16[160,128]{1,0:T(8,128)(2,1)S(1)}, f32[48,128]{1,0:T(8,128)S(1)}) custom-call(bf16[32,16,128]{2,1,0:T(8,128)(2,1)S(1)} %all-to-all-done.1.recv, bf16[2,256,2048]{2,1,0:T(8,128)(2,1)S(1)} %copy-done, bf16[2,256,512]{2,1,0:T(8,128)(2,1)S(1)} %copy-done.1, ...), custom_call_target="tpu_custom_call" | custom-call | tf_op jit(solution)/shard_map/middle/pallas_call | solution.py:268
  43.7 0.1 collective-permute-start.3
  43.8 1.2 %collective-permute-done.3.got = bf16[160,128]{1,0:T(8,128)(2,1)S(1)} collective-permute-done((bf16[160,128]{1,0:T(8,128)(2,1)S(1)}, bf16[160,128]{1,0:T(8,128)(2,1)S(1)}, u32[]{:S(2)}, u32[]{:S(2)}) %collective-permute-start.3) | collective-permute-done | bytes 40992 | tf_op jit(solution)/shard_map/ppermute | solution.py:199
  45.1 12.4 %all_to_all.21.recv = bf16[16,32,128]{2,1,0:T(8,128)(2,1)S(1)} all-to-all(bf16[16,32,128]{2,1,0:T(8,128)(2,1)S(1)} %pair_sums.3), channel_id=1, replica_groups=mesh['yh'=2,'x'=4,'z'=8,'yl'=2,'c'=2] {'z','yl'}, dimensions={0} | all-to-all | bytes 262144 | tf_op jit(solution)/shard_map/all_to_all | solution.py:195
  57.4 1.9 %collective-permute-start.5 = (bf16[16,32,128]{2,1,0:T(8,128)(2,1)S(1)}, bf16[16,32,128]{2,1,0:T(8,128)(2,1)S(1)}, u32[]{:S(2)}, u32[]{:S(2)}) collective-permute-start(bf16[16,32,128]{2,1,0:T(8,128)(2,1)S(1)} %all_to_all.21.recv), channel_id=1, source_target_pairs={{0,1},{1,0},{2,3},{3,2},{4,5},{5,4},{6,7},{7,6},{8,9},{9,8},{10,11... | collective-permute-start | bytes 393224 | tf_op jit(solution)/shard_map/ppermute | solution.py:228
  59.4 0.7 shard_map.105
  60.0 6.7 %all-to-all-start.3 = ((bf16[32,16,128]{2,1,0:T(8,128)(2,1)}), bf16[32,16,128]{2,1,0:T(8,128)(2,1)S(1)}, u32[]{:S(2)}, u32[]{:S(2)}) async-start(bf16[32,16,128]{2,1,0:T(8,128)(2,1)} %shard_map.105), calls=%async_computation.3 | async-start | bytes 262144 | tf_op jit(solution)/shard_map/all_to_all | solution.py:195
  66.7 3.5 %collective-permute-start.4 = (bf16[2,16,512]{2,1,0:T(8,128)(2,1)S(1)}, bf16[2,16,512]{2,1,0:T(8,128)(2,1)S(1)}, u32[]{:S(2)}, u32[]{:S(2)}) collective-permute-start(bf16[2,16,512]{2,1,0:T(8,128)(2,1)S(1)} %get-tuple-element.13.vec), channel_id=1, source_target_pairs={{1,2},{3,4},{5,6},{7,8},{9,10},{11,12},{13,14},{15,16},{17,18},{19... | collective-permute-start | bytes 98312 | tf_op jit(solution)/shard_map/ppermute | solution.py:212
  70.3 2.3 %near_terms.3.near = f32[2,16,512]{2,1,0:T(8,128)S(1)} custom-call(bf16[160,128]{1,0:T(8,128)(2,1)S(1)} %collective-permute-done.3.got, bf16[2,16,512]{2,1,0:T(8,128)(2,1)S(1)} %get-tuple-element.13.vec, bf16[3,2,512,512]{3,2,1,0:T(8,128)(2,1)} %blocks_hbm.7), custom_call_target="tpu_custom_call" | custom-call | tf_op jit(solution)/shard_map/near_terms/pallas_call | solution.py:216
  72.6 0.0 collective-permute-done.4.cross
  72.6 0.0 collective-permute-done.5.other
  72.6 2.4 %local_terms.3.local = f32[2,16,512]{2,1,0:T(8,128)S(1)} custom-call(f32[2,16,512]{2,1,0:T(8,128)S(1)} %near_terms.3.near, bf16[2,16,512]{2,1,0:T(8,128)(2,1)S(1)} %collective-permute-done.4.cross, bf16[16,32,128]{2,1,0:T(8,128)(2,1)S(1)} %all_to_all.21.recv, bf16[16,32,128]{2,1,0:T(8,128)(2,1)S(1)} %collective-permute-done.5.other, ...), custom_call_target="tpu_custom_call" | custom-call | tf_op jit(solution)/shard_map/local_terms/pallas_call | solution.py:229
  74.9 0.0 all-to-all-done.3.recv
  75.0 1.6 %shard_map.106 = f32[2,16,512]{2,1,0:T(8,128)} custom-call(bf16[32,16,128]{2,1,0:T(8,128)(2,1)S(1)} %all-to-all-done.3.recv, bf16[2,256,2048]{2,1,0:T(8,128)(2,1)S(1)} %copy-done, bf16[2,256,512]{2,1,0:T(8,128)(2,1)S(1)} %copy-done.1, f32[2,16,512]{2,1,0:T(8,128)S(1)} %local_terms.3.local), custom_call_target="tpu_custom_call" | custom-call | tf_op jit(solution)/shard_map/pallas_call | solution.py:185
  (2 shorter events, 0.0 us)
Async XLA Ops:
  2.1 4.2 %collective-permute-start = (bf16[160,128]{1,0:T(8,128)(2,1)S(1)}, bf16[160,128]{1,0:T(8,128)(2,1)S(1)}, u32[]{:S(2)}, u32[]{:S(2)}) collective-permute-start(bf16[160,128]{1,0:T(8,128)(2,1)S(1)} %get-tuple-element.8), channel_id=1, source_target_pairs={{0,1},{1,0},{2,3},{3,2},{4,5},{5,4},{6,7},{7,6},{8,9},{9,8},{10,11... | collective-permute-start | bytes 122888 | tf_op jit(solution)/shard_map/ppermute | solution.py:199
  22.2 16.4 %collective-permute-start.2 = (bf16[16,32,128]{2,1,0:T(8,128)(2,1)S(1)}, bf16[16,32,128]{2,1,0:T(8,128)(2,1)S(1)}, u32[]{:S(2)}, u32[]{:S(2)}) collective-permute-start(bf16[16,32,128]{2,1,0:T(8,128)(2,1)S(1)} %all_to_all.20.recv), channel_id=1, source_target_pairs={{0,1},{1,0},{2,3},{3,2},{4,5},{5,4},{6,7},{7,6},{8,9},{9,8},{10,11... | collective-permute-start | bytes 393224 | tf_op jit(solution)/shard_map/ppermute | solution.py:228
  24.9 16.0 %all-to-all-start.1 = ((bf16[32,16,128]{2,1,0:T(8,128)(2,1)}), bf16[32,16,128]{2,1,0:T(8,128)(2,1)S(1)}, u32[]{:S(2)}, u32[]{:S(2)}) async-start(bf16[32,16,128]{2,1,0:T(8,128)(2,1)} %shard_map.104), calls=%async_computation.1 | async-start | bytes 262144 | tf_op jit(solution)/shard_map/all_to_all | solution.py:195
  31.8 9.1 %copy-start = (bf16[2,256,2048]{2,1,0:T(8,128)(2,1)S(1)}, bf16[2,256,2048]{2,1,0:T(8,128)(2,1)}, u32[]{:S(2)}) copy-start(bf16[2,256,2048]{2,1,0:T(8,128)(2,1)} %coupling.3) | copy-start | bytes 6291460
  31.8 9.1 %copy-start.1 = (bf16[2,256,512]{2,1,0:T(8,128)(2,1)S(1)}, bf16[2,256,512]{2,1,0:T(8,128)(2,1)}, u32[]{:S(2)}) copy-start(bf16[2,256,512]{2,1,0:T(8,128)(2,1)} %expand.3) | copy-start | bytes 1572868
  31.9 6.7 %collective-permute-start.1 = (bf16[2,16,512]{2,1,0:T(8,128)(2,1)}, bf16[2,16,512]{2,1,0:T(8,128)(2,1)S(1)}, u32[]{:S(2)}, u32[]{:S(2)}) collective-permute-start(bf16[2,16,512]{2,1,0:T(8,128)(2,1)} %vec.1), channel_id=1, source_target_pairs={{1,2},{3,4},{5,6},{7,8},{9,10},{11,12},{13,14},{15,16},{17,18},{19... | collective-permute-start | bytes 98312 | tf_op jit(solution)/shard_map/ppermute | solution.py:212
  43.7 1.3 %collective-permute-start.3 = (bf16[160,128]{1,0:T(8,128)(2,1)S(1)}, bf16[160,128]{1,0:T(8,128)(2,1)S(1)}, u32[]{:S(2)}, u32[]{:S(2)}) collective-permute-start(bf16[160,128]{1,0:T(8,128)(2,1)S(1)} %get-tuple-element.11), channel_id=1, source_target_pairs={{0,1},{1,0},{2,3},{3,2},{4,5},{5,4},{6,7},{7,6},{8,9},{9,8},{10,11... | collective-permute-start | bytes 122888 | tf_op jit(solution)/shard_map/ppermute | solution.py:199
  57.4 15.1 %collective-permute-start.5 = (bf16[16,32,128]{2,1,0:T(8,128)(2,1)S(1)}, bf16[16,32,128]{2,1,0:T(8,128)(2,1)S(1)}, u32[]{:S(2)}, u32[]{:S(2)}) collective-permute-start(bf16[16,32,128]{2,1,0:T(8,128)(2,1)S(1)} %all_to_all.21.recv), channel_id=1, source_target_pairs={{0,1},{1,0},{2,3},{3,2},{4,5},{5,4},{6,7},{7,6},{8,9},{9,8},{10,11... | collective-permute-start | bytes 393224 | tf_op jit(solution)/shard_map/ppermute | solution.py:228
  60.0 14.9 %all-to-all-start.3 = ((bf16[32,16,128]{2,1,0:T(8,128)(2,1)}), bf16[32,16,128]{2,1,0:T(8,128)(2,1)S(1)}, u32[]{:S(2)}, u32[]{:S(2)}) async-start(bf16[32,16,128]{2,1,0:T(8,128)(2,1)} %shard_map.105), calls=%async_computation.3 | async-start | bytes 262144 | tf_op jit(solution)/shard_map/all_to_all | solution.py:195
  66.7 5.8 %collective-permute-start.4 = (bf16[2,16,512]{2,1,0:T(8,128)(2,1)S(1)}, bf16[2,16,512]{2,1,0:T(8,128)(2,1)S(1)}, u32[]{:S(2)}, u32[]{:S(2)}) collective-permute-start(bf16[2,16,512]{2,1,0:T(8,128)(2,1)S(1)} %get-tuple-element.13.vec), channel_id=1, source_target_pairs={{1,2},{3,4},{5,6},{7,8},{9,10},{11,12},{13,14},{15,16},{17,18},{19... | collective-permute-start | bytes 98312 | tf_op jit(solution)/shard_map/ppermute | solution.py:212

commit v5 on v4

--- a/solution.py
+++ b/solution.py
@@ -3,14 +3,15 @@
 from jax import lax
 from jax.experimental import pallas as pl
 from jax.experimental.pallas import tpu as pltpu
-from jax.sharding import Mesh
 from jax.sharding import PartitionSpec as P
 
-REGION = ("yh", "x")
-BLK = ("z", "yl", "c")
-CHIPS = ("z", "yl")
-PLANE = ("yh", "x", "yl", "c")
-ALL = REGION + BLK
+ALL = ("region", "blk")
+CHIP_ORDER = tuple(2 * z + y for z in (4, 5, 6, 7, 3, 2, 1, 0) for y in (1, 0))
+CHIPS = [[32 * r + 2 * i + c for i in CHIP_ORDER] for r in range(8) for c in range(2)]
+PLANE = [[32 * r + 4 * z + q for r in range(8) for q in range(4)] for z in range(8)]
+PARTNER = [(d, d ^ 1) for d in range(256)]
+CROSS = [(d, d + 1) for d in range(256) if d % 2 == 1 and d % 32 != 31]
+CROSS += [(d, d - 1) for d in range(256) if d % 2 == 0 and d % 32 != 0]
 NT = (((1,), (1,)), ((), ()))
 f32 = jnp.float32
 bf16 = jnp.bfloat16
@@ -42,7 +43,7 @@
 
 def fill_pair(vec, inner_basis, outer_basis, give, keep):
     real, imag = halves(nt(vec, outer_basis[...].reshape(512, 512)), 256)
-    core = lax.axis_index("c")
+    core = lax.rem(lax.axis_index("blk"), 2)
     wide = jnp.concatenate([real, imag], 0)
     low, high = wide[:, :128], wide[:, 128:]
     keep[:16] = paired(nt(vec, inner_basis[...].reshape(128, 512)))
@@ -62,7 +63,7 @@
     coeff = jnp.where(rank < ranks[0], keep[:16], 0.0).astype(bf16)
     quarters = (keep[16:] + got[:32].astype(f32)).astype(bf16)
     for d in range(16):
-        part = d % 2
+        part = CHIP_ORDER[d] % 2
         send[d, :16] = coeff
         send[d, 16:] = quarters[16 * part : 16 * part + 16]
 
@@ -77,7 +78,7 @@
 
 
 def near_kernel(got, vec, blocks_hbm, out, blocks, sems):
-    other = 2 - 2 * lax.axis_index("c")
+    other = 2 - 2 * lax.rem(lax.axis_index("blk"), 2)
     copies = [
         pltpu.make_async_copy(blocks_hbm.at[source], blocks.at[slot], sems.at[slot])
         for slot, source in enumerate((1, other))
@@ -93,7 +94,7 @@
 
 
 def terms_kernel(near, cross, recv, other, blocks_hbm, coupling_hbm, expand_hbm, out, block, coupling, expand, sems):
-    core = lax.axis_index("c")
+    core = lax.rem(lax.axis_index("blk"), 2)
     copies = [
         pltpu.make_async_copy(coupling_hbm, coupling, sems.at[0]),
         pltpu.make_async_copy(expand_hbm, expand, sems.at[1]),
@@ -102,10 +103,10 @@
     for copy in copies:
         copy.start()
     lane = lax.broadcasted_iota(jnp.int32, (16, 128), 1)
-    position = lax.axis_index(BLK)
+    position = lax.axis_index("blk")
     res, ims = [], []
     for j in range(16):
-        mine, theirs = (ref[j, :16].astype(f32) for ref in (recv, other))
+        mine, theirs = (ref[CHIP_ORDER.index(j), :16].astype(f32) for ref in (recv, other))
         first, second = jnp.where(core == 0, mine, theirs), jnp.where(core == 0, theirs, mine)
         first = jnp.where(jnp.abs(2 * j - position) > 1, first, 0.0)
         second = jnp.where(jnp.abs(2 * j + 1 - position) > 1, second, 0.0)
@@ -124,7 +125,7 @@
 
 
 def field_part(recv, coupling, expand):
-    region = lax.axis_index(REGION)
+    region = lax.axis_index("region")
     res, ims = [], []
     for s in range(8):
         tiles = [jnp.where(s != region, recv[4 * s + q], jnp.zeros((16, 128), bf16)) for q in range(4)]
@@ -166,8 +167,6 @@
     second[1] = local[1] + imag
 
 
-PARTNER = [(i, i ^ 1) for i in range(32)]
-CROSS = [(i, i + 1) for i in range(1, 31, 2)] + [(i, i - 1) for i in range(2, 32, 2)]
 ANY = pl.BlockSpec(memory_space=pl.ANY)
 RANKS = pl.BlockSpec(memory_space=pltpu.SMEM)
 PARAMS = pltpu.CompilerParams(vmem_limit_bytes=16 * 1024 * 1024)
@@ -183,20 +182,16 @@
 
 def call(kernel, outs, *args):
     return pl.pallas_call(
-        kernel,
-        in_specs=vmem(len(args)),
-        out_specs=vmem(len(outs)),
-        out_shape=outs,
-        compiler_params=PARAMS,
+        kernel, in_specs=vmem(len(args)), out_specs=vmem(len(outs)), out_shape=outs, compiler_params=PARAMS
     )(*args)
 
 
-def exchange(value, axes):
-    return lax.all_to_all(value, axes, split_axis=0, concat_axis=0, tiled=True)
+def exchange(value, groups):
+    return lax.all_to_all(value, ALL, split_axis=0, concat_axis=0, axis_index_groups=groups, tiled=True)
 
 
 def swapped(give, keep, ranks):
-    got = lax.ppermute(give, BLK, PARTNER)
+    got = lax.ppermute(give, ALL, PARTNER)
     send = pl.pallas_call(
         pair_kernel,
         in_specs=vmem(2) + [RANKS],
@@ -209,7 +204,7 @@
 
 
 def crossed(vec):
-    return lax.ppermute(vec, BLK, CROSS)
+    return lax.ppermute(vec, ALL, CROSS)
 
 
 def near_terms(got, vec, near_blocks):
@@ -225,7 +220,7 @@
 
 
 def local_terms(near, cross, recv, near_blocks, coupling, inner_expand):
-    other = lax.ppermute(recv, BLK, PARTNER)
+    other = lax.ppermute(recv, ALL, PARTNER)
     return pl.pallas_call(
         terms_kernel,
         in_specs=vmem(4) + [ANY] * 3,
@@ -291,22 +286,22 @@
 
 
 def solution(mesh):
-    fine = Mesh(mesh.devices.reshape(2, 4, 8, 2, 2), ALL)
+    last = P(None, None, ALL)
     placed = (
-        P(None, None, ALL),
+        last,
         P(None, None, ALL, None),
-        P(None, None, ALL),
+        last,
         P(None, ALL, None),
-        P(None, None, ALL),
-        P(None, None, ALL),
-        P(None, REGION, None),
-        P(None, None, ALL),
+        last,
+        last,
+        P(None, "region", None),
+        last,
         P(ALL),
     )
     return jax.shard_map(
         local,
-        mesh=fine,
+        mesh=mesh,
         in_specs=placed,
-        out_specs=(P(None, None, ALL), P(None, None, ALL)),
+        out_specs=(last, last),
         check_vma=False,
     )

time: 77.2 us -> 72.7 us (0.942)
  blocking collectives: 28.3 us -> 25.3 us
  starting transfers between devices: 28.1 us -> 26.7 us
    all_to_all x2, blocking collectives: 28.3 us -> 25.3 us  [exchange(): lax.all_to_all(value, ALL, split_axis=0, concat_axis=0, axis_index_groups...]
    ppermute x6, starting transfers between devices: 14.5 us -> 12.7 us  [the longest x2 7.21 us: crossed(): return lax.ppermute(vec, ALL, CROSS)]
  transfers between devices with their start and end apart: 8 -> 8, of which waited for: 2 -> 2; matrix products, arithmetic and copies ran while one was open for 0% -> 0% of each run, Pallas kernels for 15% -> 16%
where the time goes in v5:
time: 72.7 us; the launch traced here: 72.2 us
  starting transfers between devices  26.7 us (37%)
  blocking collectives  25.3 us (35%)
  Pallas kernels  17.2 us (24%)
  between operations  1.46 us (2%)
  waiting for transfers between devices  1.44 us (2%)
    all_to_all x2, blocking collectives, exchange(): lax.all_to_all(value, ALL, split_axis=0, concat_axis=0, axis_index_groups...  25.3 us
    all_to_all x2, starting transfers between devices, exchange(): lax.all_to_all(value, ALL, split_axis=0, concat_axis=0, axis_index_groups...  14 us
    ppermute x2, starting transfers between devices, crossed(): return lax.ppermute(vec, ALL, CROSS)  7.21 us
    pallas_call x2, Pallas kernels, near_terms(): pl.pallas_call(near_kernel, in_specs=vmem(2) + [ANY], out_specs=vmem(1)[0...  5.33 us
    pallas_call x2, Pallas kernels, local_terms(): pl.pallas_call(terms_kernel, in_specs=vmem(4) + [ANY] * 3, out_specs=vmem...  4.69 us
    ppermute x2, starting transfers between devices, swapped(): got = lax.ppermute(give, ALL, PARTNER)  3.38 us
    pallas_call x3, Pallas kernels, call(): pl.pallas_call(kernel, in_specs=vmem(len(args)), out_specs=vmem(len(outs)...  2.99 us
    pallas_call x1, Pallas kernels, local(): pl.pallas_call(middle_kernel, in_specs=vmem(4) + [ANY] * 2, out_specs=[AN...  2.73 us
  transfers between devices with their start and end apart: 8, of which 2 were waited for; matrix products, arithmetic and copies ran while one was open for 0% of the time, Pallas kernels for 16%

profile of v5, /device:TPU:1, one launch (start us, length us, event | category | flops | bytes accessed | tf_op | source)
XLA Modules:
  0.0 72.2 jit_solution(2598940166411250730)
XLA Ops:
  0.6 1.5 %start.1 = (bf16[160,128]{1,0:T(8,128)(2,1)S(1)}, f32[48,128]{1,0:T(8,128)S(1)}) custom-call(bf16[2,16,512]{2,1,0:T(8,128)(2,1)} %vec.1, bf16[2,64,512]{2,1,0:T(8,128)(2,1)} %inner_hbm.1, bf16[2,256,512]{2,1,0:T(8,128)(2,1)} %outer_hbm.1), custom_call_target="tpu_custom_call" | custom-call | tf_op jit(solution)/shard_map/start/pallas_call | solution.py:247
  2.1 3.3 %collective-permute-start = (bf16[160,128]{1,0:T(8,128)(2,1)S(1)}, bf16[160,128]{1,0:T(8,128)(2,1)S(1)}, u32[]{:S(2)}, u32[]{:S(2)}) collective-permute-start(bf16[160,128]{1,0:T(8,128)(2,1)S(1)} %get-tuple-element.8), channel_id=1, source_target_pairs={{0,1},{1,0},{2,3},{3,2},{4,5},{5,4},{6,7},{7,6},{8,9},{9,8},{10,11... | collective-permute-start | bytes 122888 | tf_op jit(solution)/shard_map/ppermute | solution.py:194
  6.0 0.2 collective-permute-done.got
  6.3 12.7 %all_to_all.20.recv = bf16[16,32,128]{2,1,0:T(8,128)(2,1)S(1)} all-to-all(bf16[16,32,128]{2,1,0:T(8,128)(2,1)S(1)} %pair_sums.2), channel_id=1, replica_groups={{18,16,22,20,26,24,30,28,14,12,10,8,6,4,2,0},{19,17,23,21,27,25,31,29,1..., dimensions={0} | all-to-all | bytes 262144 | tf_op jit(solution)/shard_map/all_to_all | solution.py:190
  19.0 1.2 %collective-permute-start.2 = (bf16[16,32,128]{2,1,0:T(8,128)(2,1)S(1)}, bf16[16,32,128]{2,1,0:T(8,128)(2,1)S(1)}, u32[]{:S(2)}, u32[]{:S(2)}) collective-permute-start(bf16[16,32,128]{2,1,0:T(8,128)(2,1)S(1)} %all_to_all.20.recv), channel_id=1, source_target_pairs={{0,1},{1,0},{2,3},{3,2},{4,5},{5,4},{6,7},{7,6},{8,9},{9,8},{10,11... | collective-permute-start | bytes 393224 | tf_op jit(solution)/shard_map/ppermute | solution.py:223
  20.2 0.7 shard_map.104
  20.8 7.1 %all-to-all-start.1 = ((bf16[32,16,128]{2,1,0:T(8,128)(2,1)}), bf16[32,16,128]{2,1,0:T(8,128)(2,1)S(1)}, u32[]{:S(2)}, u32[]{:S(2)}) async-start(bf16[32,16,128]{2,1,0:T(8,128)(2,1)} %shard_map.104), calls=%async_computation.1 | async-start | bytes 262144 | tf_op jit(solution)/shard_map/all_to_all | solution.py:190
  27.9 0.0 copy-start
  27.9 0.0 copy-start.1
  28.0 3.7 %collective-permute-start.1 = (bf16[2,16,512]{2,1,0:T(8,128)(2,1)}, bf16[2,16,512]{2,1,0:T(8,128)(2,1)S(1)}, u32[]{:S(2)}, u32[]{:S(2)}) collective-permute-start(bf16[2,16,512]{2,1,0:T(8,128)(2,1)} %vec.1), channel_id=1, source_target_pairs={{1,2},{3,4},{5,6},{7,8},{9,10},{11,12},{13,14},{15,16},{17,18},{19... | collective-permute-start | bytes 98312 | tf_op jit(solution)/shard_map/ppermute | solution.py:207
  31.6 3.0 %near_terms.2.near = f32[2,16,512]{2,1,0:T(8,128)S(1)} custom-call(bf16[160,128]{1,0:T(8,128)(2,1)S(1)} %collective-permute-done.got, bf16[2,16,512]{2,1,0:T(8,128)(2,1)} %vec.1, bf16[3,2,512,512]{3,2,1,0:T(8,128)(2,1)} %blocks_hbm.7), custom_call_target="tpu_custom_call" | custom-call | tf_op jit(solution)/shard_map/near_terms/pallas_call | solution.py:211
  34.7 0.0 collective-permute-done.1.cross
  34.7 0.0 collective-permute-done.2.other
  34.7 2.3 %local_terms.2.local = f32[2,16,512]{2,1,0:T(8,128)S(1)} custom-call(f32[2,16,512]{2,1,0:T(8,128)S(1)} %near_terms.2.near, bf16[2,16,512]{2,1,0:T(8,128)(2,1)S(1)} %collective-permute-done.1.cross, bf16[16,32,128]{2,1,0:T(8,128)(2,1)S(1)} %all_to_all.20.recv, bf16[16,32,128]{2,1,0:T(8,128)(2,1)S(1)} %collective-permute-done.2.other, ...), custom_call_target="tpu_custom_call" | custom-call | tf_op jit(solution)/shard_map/local_terms/pallas_call | solution.py:224
  37.1 0.0 all-to-all-done.1.recv
  37.1 0.0 copy-done
  37.1 0.0 copy-done.1
  37.1 2.7 %middle.1 = (f32[2,16,512]{2,1,0:T(8,128)}, bf16[2,16,512]{2,1,0:T(8,128)(2,1)S(1)}, bf16[160,128]{1,0:T(8,128)(2,1)S(1)}, f32[48,128]{1,0:T(8,128)S(1)}) custom-call(bf16[32,16,128]{2,1,0:T(8,128)(2,1)S(1)} %all-to-all-done.1.recv, bf16[2,256,2048]{2,1,0:T(8,128)(2,1)S(1)} %copy-done, bf16[2,256,512]{2,1,0:T(8,128)(2,1)S(1)} %copy-done.1, ...), custom_call_target="tpu_custom_call" | custom-call | tf_op jit(solution)/shard_map/middle/pallas_call | solution.py:263
  39.8 0.1 collective-permute-start.3
  39.9 1.2 %collective-permute-done.3.got = bf16[160,128]{1,0:T(8,128)(2,1)S(1)} collective-permute-done((bf16[160,128]{1,0:T(8,128)(2,1)S(1)}, bf16[160,128]{1,0:T(8,128)(2,1)S(1)}, u32[]{:S(2)}, u32[]{:S(2)}) %collective-permute-start.3) | collective-permute-done | bytes 40992 | tf_op jit(solution)/shard_map/ppermute | solution.py:194
  41.2 12.6 %all_to_all.21.recv = bf16[16,32,128]{2,1,0:T(8,128)(2,1)S(1)} all-to-all(bf16[16,32,128]{2,1,0:T(8,128)(2,1)S(1)} %pair_sums.3), channel_id=1, replica_groups={{18,16,22,20,26,24,30,28,14,12,10,8,6,4,2,0},{19,17,23,21,27,25,31,29,1..., dimensions={0} | all-to-all | bytes 262144 | tf_op jit(solution)/shard_map/all_to_all | solution.py:190
  53.8 1.0 %collective-permute-start.5 = (bf16[16,32,128]{2,1,0:T(8,128)(2,1)S(1)}, bf16[16,32,128]{2,1,0:T(8,128)(2,1)S(1)}, u32[]{:S(2)}, u32[]{:S(2)}) collective-permute-start(bf16[16,32,128]{2,1,0:T(8,128)(2,1)S(1)} %all_to_all.21.recv), channel_id=1, source_target_pairs={{0,1},{1,0},{2,3},{3,2},{4,5},{5,4},{6,7},{7,6},{8,9},{9,8},{10,11... | collective-permute-start | bytes 393224 | tf_op jit(solution)/shard_map/ppermute | solution.py:223
  54.8 0.7 shard_map.105
  55.4 6.9 %all-to-all-start.3 = ((bf16[32,16,128]{2,1,0:T(8,128)(2,1)}), bf16[32,16,128]{2,1,0:T(8,128)(2,1)S(1)}, u32[]{:S(2)}, u32[]{:S(2)}) async-start(bf16[32,16,128]{2,1,0:T(8,128)(2,1)} %shard_map.105), calls=%async_computation.3 | async-start | bytes 262144 | tf_op jit(solution)/shard_map/all_to_all | solution.py:190
  62.3 3.5 %collective-permute-start.4 = (bf16[2,16,512]{2,1,0:T(8,128)(2,1)S(1)}, bf16[2,16,512]{2,1,0:T(8,128)(2,1)S(1)}, u32[]{:S(2)}, u32[]{:S(2)}) collective-permute-start(bf16[2,16,512]{2,1,0:T(8,128)(2,1)S(1)} %get-tuple-element.13.vec), channel_id=1, source_target_pairs={{1,2},{3,4},{5,6},{7,8},{9,10},{11,12},{13,14},{15,16},{17,18},{19... | collective-permute-start | bytes 98312 | tf_op jit(solution)/shard_map/ppermute | solution.py:207
  65.9 2.3 %near_terms.3.near = f32[2,16,512]{2,1,0:T(8,128)S(1)} custom-call(bf16[160,128]{1,0:T(8,128)(2,1)S(1)} %collective-permute-done.3.got, bf16[2,16,512]{2,1,0:T(8,128)(2,1)S(1)} %get-tuple-element.13.vec, bf16[3,2,512,512]{3,2,1,0:T(8,128)(2,1)} %blocks_hbm.7), custom_call_target="tpu_custom_call" | custom-call | tf_op jit(solution)/shard_map/near_terms/pallas_call | solution.py:211
  68.1 0.0 collective-permute-done.4.cross
  68.2 0.0 collective-permute-done.5.other
  68.2 2.3 %local_terms.3.local = f32[2,16,512]{2,1,0:T(8,128)S(1)} custom-call(f32[2,16,512]{2,1,0:T(8,128)S(1)} %near_terms.3.near, bf16[2,16,512]{2,1,0:T(8,128)(2,1)S(1)} %collective-permute-done.4.cross, bf16[16,32,128]{2,1,0:T(8,128)(2,1)S(1)} %all_to_all.21.recv, bf16[16,32,128]{2,1,0:T(8,128)(2,1)S(1)} %collective-permute-done.5.other, ...), custom_call_target="tpu_custom_call" | custom-call | tf_op jit(solution)/shard_map/local_terms/pallas_call | solution.py:224
  70.5 0.0 all-to-all-done.3.recv
  70.5 1.6 %shard_map.106 = f32[2,16,512]{2,1,0:T(8,128)} custom-call(bf16[32,16,128]{2,1,0:T(8,128)(2,1)S(1)} %all-to-all-done.3.recv, bf16[2,256,2048]{2,1,0:T(8,128)(2,1)S(1)} %copy-done, bf16[2,256,512]{2,1,0:T(8,128)(2,1)S(1)} %copy-done.1, f32[2,16,512]{2,1,0:T(8,128)S(1)} %local_terms.3.local), custom_call_target="tpu_custom_call" | custom-call | tf_op jit(solution)/shard_map/pallas_call | solution.py:184
  (2 shorter events, 0.0 us)
Async XLA Ops:
  2.1 4.2 %collective-permute-start = (bf16[160,128]{1,0:T(8,128)(2,1)S(1)}, bf16[160,128]{1,0:T(8,128)(2,1)S(1)}, u32[]{:S(2)}, u32[]{:S(2)}) collective-permute-start(bf16[160,128]{1,0:T(8,128)(2,1)S(1)} %get-tuple-element.8), channel_id=1, source_target_pairs={{0,1},{1,0},{2,3},{3,2},{4,5},{5,4},{6,7},{7,6},{8,9},{9,8},{10,11... | collective-permute-start | bytes 122888 | tf_op jit(solution)/shard_map/ppermute | solution.py:194
  19.0 15.7 %collective-permute-start.2 = (bf16[16,32,128]{2,1,0:T(8,128)(2,1)S(1)}, bf16[16,32,128]{2,1,0:T(8,128)(2,1)S(1)}, u32[]{:S(2)}, u32[]{:S(2)}) collective-permute-start(bf16[16,32,128]{2,1,0:T(8,128)(2,1)S(1)} %all_to_all.20.recv), channel_id=1, source_target_pairs={{0,1},{1,0},{2,3},{3,2},{4,5},{5,4},{6,7},{7,6},{8,9},{9,8},{10,11... | collective-permute-start | bytes 393224 | tf_op jit(solution)/shard_map/ppermute | solution.py:223
  20.8 16.2 %all-to-all-start.1 = ((bf16[32,16,128]{2,1,0:T(8,128)(2,1)}), bf16[32,16,128]{2,1,0:T(8,128)(2,1)S(1)}, u32[]{:S(2)}, u32[]{:S(2)}) async-start(bf16[32,16,128]{2,1,0:T(8,128)(2,1)} %shard_map.104), calls=%async_computation.1 | async-start | bytes 262144 | tf_op jit(solution)/shard_map/all_to_all | solution.py:190
  27.9 9.1 %copy-start = (bf16[2,256,2048]{2,1,0:T(8,128)(2,1)S(1)}, bf16[2,256,2048]{2,1,0:T(8,128)(2,1)}, u32[]{:S(2)}) copy-start(bf16[2,256,2048]{2,1,0:T(8,128)(2,1)} %coupling.3) | copy-start | bytes 6291460
  27.9 9.1 %copy-start.1 = (bf16[2,256,512]{2,1,0:T(8,128)(2,1)S(1)}, bf16[2,256,512]{2,1,0:T(8,128)(2,1)}, u32[]{:S(2)}) copy-start(bf16[2,256,512]{2,1,0:T(8,128)(2,1)} %expand.3) | copy-start | bytes 1572868
  28.0 6.7 %collective-permute-start.1 = (bf16[2,16,512]{2,1,0:T(8,128)(2,1)}, bf16[2,16,512]{2,1,0:T(8,128)(2,1)S(1)}, u32[]{:S(2)}, u32[]{:S(2)}) collective-permute-start(bf16[2,16,512]{2,1,0:T(8,128)(2,1)} %vec.1), channel_id=1, source_target_pairs={{1,2},{3,4},{5,6},{7,8},{9,10},{11,12},{13,14},{15,16},{17,18},{19... | collective-permute-start | bytes 98312 | tf_op jit(solution)/shard_map/ppermute | solution.py:207
  39.8 1.3 %collective-permute-start.3 = (bf16[160,128]{1,0:T(8,128)(2,1)S(1)}, bf16[160,128]{1,0:T(8,128)(2,1)S(1)}, u32[]{:S(2)}, u32[]{:S(2)}) collective-permute-start(bf16[160,128]{1,0:T(8,128)(2,1)S(1)} %get-tuple-element.11), channel_id=1, source_target_pairs={{0,1},{1,0},{2,3},{3,2},{4,5},{5,4},{6,7},{7,6},{8,9},{9,8},{10,11... | collective-permute-start | bytes 122888 | tf_op jit(solution)/shard_map/ppermute | solution.py:194
  53.8 14.4 %collective-permute-start.5 = (bf16[16,32,128]{2,1,0:T(8,128)(2,1)S(1)}, bf16[16,32,128]{2,1,0:T(8,128)(2,1)S(1)}, u32[]{:S(2)}, u32[]{:S(2)}) collective-permute-start(bf16[16,32,128]{2,1,0:T(8,128)(2,1)S(1)} %all_to_all.21.recv), channel_id=1, source_target_pairs={{0,1},{1,0},{2,3},{3,2},{4,5},{5,4},{6,7},{7,6},{8,9},{9,8},{10,11... | collective-permute-start | bytes 393224 | tf_op jit(solution)/shard_map/ppermute | solution.py:223
  55.4 15.1 %all-to-all-start.3 = ((bf16[32,16,128]{2,1,0:T(8,128)(2,1)}), bf16[32,16,128]{2,1,0:T(8,128)(2,1)S(1)}, u32[]{:S(2)}, u32[]{:S(2)}) async-start(bf16[32,16,128]{2,1,0:T(8,128)(2,1)} %shard_map.105), calls=%async_computation.3 | async-start | bytes 262144 | tf_op jit(solution)/shard_map/all_to_all | solution.py:190
  62.3 5.8 %collective-permute-start.4 = (bf16[2,16,512]{2,1,0:T(8,128)(2,1)S(1)}, bf16[2,16,512]{2,1,0:T(8,128)(2,1)S(1)}, u32[]{:S(2)}, u32[]{:S(2)}) collective-permute-start(bf16[2,16,512]{2,1,0:T(8,128)(2,1)S(1)} %get-tuple-element.13.vec), channel_id=1, source_target_pairs={{1,2},{3,4},{5,6},{7,8},{9,10},{11,12},{13,14},{15,16},{17,18},{19... | collective-permute-start | bytes 98312 | tf_op jit(solution)/shard_map/ppermute | solution.py:207

commit v6 on v5

--- a/solution.py
+++ b/solution.py
@@ -41,7 +41,9 @@
     return acc[:16] + jnp.where(lane < 64, -crossed, crossed)
 
 
-def fill_pair(vec, inner_basis, outer_basis, give, keep):
+def start_kernel(probes, inner_basis, outer_basis, give, keep, held):
+    vec = probes[...].reshape(32, 512)
+    held[...] = probes[...]
     real, imag = halves(nt(vec, outer_basis[...].reshape(512, 512)), 256)
     core = lax.rem(lax.axis_index("blk"), 2)
     wide = jnp.concatenate([real, imag], 0)
@@ -53,19 +55,21 @@
         give[32 + 32 * k : 64 + 32 * k] = vec[:, 128 * k : 128 * k + 128]
 
 
-def start_kernel(probes, inner_basis, outer_basis, give, keep):
-    fill_pair(probes[...].reshape(32, 512), inner_basis, outer_basis, give, keep)
-
-
-def pair_kernel(got, keep, ranks, send):
+def masked(coeff, ranks):
     lane = lax.broadcasted_iota(jnp.int32, (16, 128), 1)
     rank = jnp.where(lane < 64, lane, lane - 64)
-    coeff = jnp.where(rank < ranks[0], keep[:16], 0.0).astype(bf16)
+    return jnp.where(rank < ranks[0], coeff, 0.0).astype(bf16)
+
+
+def fill_sends(coeff, quarters, send):
+    for d in range(16):
+        send[d, :16] = coeff
+        send[d, 16:] = quarters[CHIP_ORDER[d] % 2]
+
+
+def pair_kernel(got, keep, ranks, send):
     quarters = (keep[16:] + got[:32].astype(f32)).astype(bf16)
-    for d in range(16):
-        part = CHIP_ORDER[d] % 2
-        send[d, :16] = coeff
-        send[d, 16:] = quarters[16 * part : 16 * part + 16]
+    fill_sends(masked(keep[:16], ranks), (quarters[:16], quarters[16:]), send)
 
 
 def sum_kernel(recv, send):
@@ -85,7 +89,10 @@
     ]
     for copy in copies:
         copy.start()
-    partner = jnp.concatenate([got[32 + 32 * k : 64 + 32 * k] for k in range(4)], 1)
+    if got.shape[1] == 128:
+        partner = jnp.concatenate([got[32 + 32 * k : 64 + 32 * k] for k in range(4)], 1)
+    else:
+        partner = got[...]
     copies[0].wait()
     acc = nt(vec[...].reshape(32, 512), blocks[0].reshape(1024, 512))
     copies[1].wait()
@@ -124,7 +131,7 @@
     out[1] = near[1] + imag + (a[16:] + b[:16])
 
 
-def field_part(recv, coupling, expand):
+def field_rows(recv, coupling):
     region = lax.axis_index("region")
     res, ims = [], []
     for s in range(8):
@@ -133,36 +140,52 @@
         ims += tiles[2:]
     rows = jnp.concatenate([jnp.concatenate(res, 1), jnp.concatenate(ims, 1)], 0)
     real, imag = halves(nt(rows, coupling[...].reshape(512, 2048)), 256)
-    rows = jnp.concatenate([real, imag], 0).astype(bf16)
+    return jnp.concatenate([real, imag], 0).astype(bf16)
+
+
+def expanded(rows, expand):
     a, b = nn(rows, expand[0]), nn(rows, expand[1])
     return a[:16] - b[16:], a[16:] + b[:16]
 
 
-def middle_kernel(recv, coupling, expand, local, inner_hbm, outer_hbm, first_hbm, vec, give, keep, *scratch):
-    inner_basis, outer_basis, first, sems = scratch
+def middle_kernel(recv, coupling, expand, local, mate, ranks, *refs):
+    inner_hbm, outer_hbm, mate_outer_hbm, mate_expand_hbm = refs[:4]
+    first_hbm, vec, mate_vec, send = refs[4:8]
+    inner_basis, outer_basis, mate_expand, first, sems = refs[8:]
+    core = lax.rem(lax.axis_index("blk"), 2)
+    half = pl.ds(pl.multiple_of(128 * core, 128), 128)
     copies = [
-        pltpu.make_async_copy(inner_hbm, inner_basis, sems.at[0]),
-        pltpu.make_async_copy(outer_hbm, outer_basis, sems.at[1]),
+        pltpu.make_async_copy(mate_expand_hbm, mate_expand, sems.at[0]),
+        pltpu.make_async_copy(outer_hbm.at[:, half], outer_basis.at[0], sems.at[1]),
+        pltpu.make_async_copy(mate_outer_hbm.at[:, half], outer_basis.at[1], sems.at[2]),
+        pltpu.make_async_copy(inner_hbm, inner_basis, sems.at[3]),
     ]
     for copy in copies:
         copy.start()
-    real, imag = field_part(recv, coupling, expand)
+    field = field_rows(recv, coupling)
+    real, imag = expanded(field, expand)
     real, imag = local[0] + real, local[1] + imag
     first[0] = real
     first[1] = imag
-    result = pltpu.make_async_copy(first, first_hbm, sems.at[2])
+    result = pltpu.make_async_copy(first, first_hbm, sems.at[4])
     result.start()
     rows = jnp.concatenate([real, imag], 0).astype(bf16)
     vec[0] = rows[:16]
     vec[1] = rows[16:]
-    for copy in copies:
+    copies[0].wait()
+    real, imag = expanded(field, mate_expand)
+    mate_rows = jnp.concatenate([mate[0] + real, mate[1] + imag], 0).astype(bf16)
+    mate_vec[...] = mate_rows
+    for copy in copies[1:]:
         copy.wait()
-    fill_pair(rows, inner_basis, outer_basis, give, keep)
+    wide = nt(rows, outer_basis[0].reshape(256, 512)) + nt(mate_rows, outer_basis[1].reshape(256, 512))
+    quarters = [part.astype(bf16) for part in halves(wide, 128)]
+    fill_sends(masked(paired(nt(rows, inner_basis[...].reshape(128, 512))), ranks), quarters, send)
     result.wait()
 
 
 def last_kernel(recv, coupling, expand, local, second):
-    real, imag = field_part(recv, coupling, expand)
+    real, imag = expanded(field_rows(recv, coupling), expand)
     second[0] = local[0] + real
     second[1] = local[1] + imag
 
@@ -243,11 +266,11 @@
 
 
 def local(probes, near_blocks, inner_basis, coupling, inner_expand, outer_basis, group_coupling, outer_expand, ranks):
-    pair = [pltpu.VMEM((160, 128), bf16), pltpu.VMEM((48, 128), f32)]
-    give, keep = pl.pallas_call(
+    pair = [pltpu.VMEM((160, 128), bf16), pltpu.VMEM((48, 128), f32), pltpu.VMEM((2, 16, 512), bf16)]
+    give, keep, held = pl.pallas_call(
         start_kernel,
         in_specs=vmem(3),
-        out_specs=vmem(2),
+        out_specs=vmem(3),
         out_shape=pair,
         compiler_params=PARAMS,
         name="start",
@@ -255,30 +278,36 @@
     got, send = swapped(give, keep, ranks)
     recv = exchange(send, CHIPS)
     cross = crossed(probes)
+    mate_outer, mate_expand = (lax.ppermute(w, ALL, PARTNER) for w in (outer_basis, outer_expand))
     sums = group_sums(recv)
-    near = near_terms(got, *in_hbm(probes), near_blocks)
+    near = near_terms(got, *in_vmem(held), near_blocks)
     near = local_terms(near, cross, recv, near_blocks, coupling, inner_expand)
-    outs = [jax.ShapeDtypeStruct((2, 16, 512), f32), pltpu.VMEM((2, 16, 512), bf16)] + pair
+    mate = lax.ppermute(near, ALL, PARTNER)
     weights = in_vmem(group_coupling, outer_expand)
-    first, vec, give, keep = pl.pallas_call(
+    first, vec, mate_vec, send = pl.pallas_call(
         middle_kernel,
-        in_specs=vmem(4) + [ANY] * 2,
+        in_specs=vmem(5) + [RANKS] + [ANY] * 4,
         out_specs=[ANY] + vmem(3),
-        out_shape=outs,
+        out_shape=[
+            jax.ShapeDtypeStruct((2, 16, 512), f32),
+            pltpu.VMEM((2, 16, 512), bf16),
+            pltpu.VMEM((32, 512), bf16),
+            pltpu.VMEM((16, 32, 128), bf16),
+        ],
         scratch_shapes=[
             pltpu.VMEM(inner_basis.shape, bf16),
-            pltpu.VMEM(outer_basis.shape, bf16),
+            pltpu.VMEM((2, 2, 128, 512), bf16),
+            pltpu.VMEM(outer_expand.shape, bf16),
             pltpu.VMEM((2, 16, 512), f32),
-            pltpu.SemaphoreType.DMA((3,)),
+            pltpu.SemaphoreType.DMA((5,)),
         ],
         compiler_params=PARAMS,
         name="middle",
-    )(*in_vmem(sums), *weights, *in_vmem(near), *in_hbm(inner_basis, outer_basis))
-    got, send = swapped(give, keep, ranks)
+    )(*in_vmem(sums), *weights, *in_vmem(near, mate), ranks, *in_hbm(inner_basis, outer_basis, mate_outer, mate_expand))
     recv = exchange(send, CHIPS)
     cross = crossed(vec)
     sums = group_sums(recv)
-    near = near_terms(got, *in_vmem(vec), near_blocks)
+    near = near_terms(mate_vec, *in_vmem(vec), near_blocks)
     near = local_terms(near, cross, recv, near_blocks, coupling, inner_expand)
     args = in_vmem(sums) + weights + in_vmem(near)
     second = call(last_kernel, [jax.ShapeDtypeStruct((2, 16, 512), f32)], *args)[0]

time: 72.7 us -> 73 us (level)
    ppermute x0 -> x3, starting transfers between devices: none -> 3.48 us  [the longest x2 3.39 us: local(): lax.ppermute(w, ALL, PARTNER)]
    ppermute x2 -> x1, starting transfers between devices: 3.38 us -> 0.49 us  [swapped(): got = lax.ppermute(give, ALL, PARTNER)]
    ppermute x0 -> x3, waiting for transfers between devices: none -> 1.24 us  [the longest x1 1.23 us: local(): mate = lax.ppermute(near, ALL, PARTNER)]
    ppermute x2 -> x1, waiting for transfers between devices: 1.42 us -> 0.22 us  [swapped(): got = lax.ppermute(give, ALL, PARTNER)]
  transfers between devices with their start and end apart: 8 -> 10, of which waited for: 2 -> 3; matrix products, arithmetic and copies ran while one was open for 0% -> 0% of each run, Pallas kernels for 16% -> 17%
where the time goes in v6:
time: 73 us; the launch traced here: 72.5 us
  starting transfers between devices  27.1 us (37%)
  blocking collectives  25.8 us (35%)
  Pallas kernels  16.6 us (23%)
  waiting for transfers between devices  1.59 us (2%)
  between operations  1.44 us (2%)
    all_to_all x2, blocking collectives, exchange(): lax.all_to_all(value, ALL, split_axis=0, concat_axis=0, axis_index_groups...  25.8 us
    all_to_all x2, starting transfers between devices, exchange(): lax.all_to_all(value, ALL, split_axis=0, concat_axis=0, axis_index_groups...  13.9 us
    ppermute x2, starting transfers between devices, crossed(): return lax.ppermute(vec, ALL, CROSS)  7.08 us
    pallas_call x2, Pallas kernels, near_terms(): pl.pallas_call(near_kernel, in_specs=vmem(2) + [ANY], out_specs=vmem(1)[0...  4.72 us
    pallas_call x2, Pallas kernels, local_terms(): pl.pallas_call(terms_kernel, in_specs=vmem(4) + [ANY] * 3, out_specs=vmem...  4.68 us
    ppermute x2, starting transfers between devices, local(): lax.ppermute(w, ALL, PARTNER)  3.39 us
    pallas_call x3, Pallas kernels, call(): pl.pallas_call(kernel, in_specs=vmem(len(args)), out_specs=vmem(len(outs)...  2.99 us
    pallas_call x1, Pallas kernels, local(): pl.pallas_call(middle_kernel, in_specs=vmem(5) + [RANKS] + [ANY] * 4, out...  2.69 us
  transfers between devices with their start and end apart: 10, of which 3 were waited for; matrix products, arithmetic and copies ran while one was open for 0% of the time, Pallas kernels for 17%

profile of v6, /device:TPU:1, one launch (start us, length us, event | category | flops | bytes accessed | tf_op | source)
XLA Modules:
  0.0 72.5 jit_solution(11271621442525004301)
XLA Ops:
  0.6 3.3 %collective-permute-start.4 = (bf16[2,256,512]{2,1,0:T(8,128)(2,1)}, bf16[2,256,512]{2,1,0:T(8,128)(2,1)}, u32[]{:S(2)}, u32[]{:S(2)}) collective-permute-start(bf16[2,256,512]{2,1,0:T(8,128)(2,1)} %refs_1_.1), channel_id=1, source_target_pairs={{0,1},{1,0},{2,3},{3,2},{4,5},{5,4},{6,7},{7,6},{8,9},{9,8},{10,11... | collective-permute-start | bytes 1572872 | tf_op jit(solution)/shard_map/ppermute | solution.py:281
  3.9 0.1 collective-permute-start.5
  4.0 1.5 %start.1 = (bf16[160,128]{1,0:T(8,128)(2,1)S(1)}, f32[48,128]{1,0:T(8,128)S(1)}, bf16[2,16,512]{2,1,0:T(8,128)(2,1)S(1)}) custom-call(bf16[2,16,512]{2,1,0:T(8,128)(2,1)} %probes.1, bf16[2,64,512]{2,1,0:T(8,128)(2,1)} %refs_0_.1, bf16[2,256,512]{2,1,0:T(8,128)(2,1)} %refs_1_.1), custom_call_target="tpu_custom_call" | custom-call | tf_op jit(solution)/shard_map/start/pallas_call | solution.py:270
  5.5 0.5 collective-permute-start
  6.6 0.2 collective-permute-done.got
  6.9 12.7 %all_to_all.20.recv = bf16[16,32,128]{2,1,0:T(8,128)(2,1)S(1)} all-to-all(bf16[16,32,128]{2,1,0:T(8,128)(2,1)S(1)} %pair_sums.1), channel_id=1, replica_groups={{18,16,22,20,26,24,30,28,14,12,10,8,6,4,2,0},{19,17,23,21,27,25,31,29,1..., dimensions={0} | all-to-all | bytes 262144 | tf_op jit(solution)/shard_map/all_to_all | solution.py:213
  19.6 1.2 %collective-permute-start.2 = (bf16[16,32,128]{2,1,0:T(8,128)(2,1)S(1)}, bf16[16,32,128]{2,1,0:T(8,128)(2,1)S(1)}, u32[]{:S(2)}, u32[]{:S(2)}) collective-permute-start(bf16[16,32,128]{2,1,0:T(8,128)(2,1)S(1)} %all_to_all.20.recv), channel_id=1, source_target_pairs={{0,1},{1,0},{2,3},{3,2},{4,5},{5,4},{6,7},{7,6},{8,9},{9,8},{10,11... | collective-permute-start | bytes 393224 | tf_op jit(solution)/shard_map/ppermute | solution.py:246
  20.8 0.7 shard_map.104
  21.4 7.1 %all-to-all-start.1 = ((bf16[32,16,128]{2,1,0:T(8,128)(2,1)}), bf16[32,16,128]{2,1,0:T(8,128)(2,1)S(1)}, u32[]{:S(2)}, u32[]{:S(2)}) async-start(bf16[32,16,128]{2,1,0:T(8,128)(2,1)} %shard_map.104), calls=%async_computation.1 | async-start | bytes 262144 | tf_op jit(solution)/shard_map/all_to_all | solution.py:213
  28.5 3.5 %collective-permute-start.1 = (bf16[2,16,512]{2,1,0:T(8,128)(2,1)}, bf16[2,16,512]{2,1,0:T(8,128)(2,1)S(1)}, u32[]{:S(2)}, u32[]{:S(2)}) collective-permute-start(bf16[2,16,512]{2,1,0:T(8,128)(2,1)} %probes.1), channel_id=1, source_target_pairs={{1,2},{3,4},{5,6},{7,8},{9,10},{11,12},{13,14},{15,16},{17,18},{19... | collective-permute-start | bytes 98312 | tf_op jit(solution)/shard_map/ppermute | solution.py:230
  32.1 0.0 copy-start
  32.1 0.0 copy-start.1
  32.1 2.4 %near_terms.2.near = f32[2,16,512]{2,1,0:T(8,128)S(1)} custom-call(bf16[160,128]{1,0:T(8,128)(2,1)S(1)} %collective-permute-done.got, bf16[2,16,512]{2,1,0:T(8,128)(2,1)S(1)} %get-tuple-element.11.vec, bf16[3,2,512,512]{3,2,1,0:T(8,128)(2,1)} %blocks_hbm.7), custom_call_target="tpu_custom_call" | custom-call | tf_op jit(solution)/shard_map/near_terms/pallas_call | solution.py:234
  34.5 0.1 collective-permute-done.1.cross
  34.7 0.0 collective-permute-done.2.other
  34.7 2.3 %local_terms.2.local = f32[2,16,512]{2,1,0:T(8,128)S(1)} custom-call(f32[2,16,512]{2,1,0:T(8,128)S(1)} %near_terms.2.near, bf16[2,16,512]{2,1,0:T(8,128)(2,1)S(1)} %collective-permute-done.1.cross, bf16[16,32,128]{2,1,0:T(8,128)(2,1)S(1)} %all_to_all.20.recv, bf16[16,32,128]{2,1,0:T(8,128)(2,1)S(1)} %collective-permute-done.2.other, ...), custom_call_target="tpu_custom_call" | custom-call | tf_op jit(solution)/shard_map/local_terms/pallas_call | solution.py:247
  37.0 0.1 collective-permute-start.3
  37.1 0.0 all-to-all-done.1.recv
  37.1 1.2 %collective-permute-done.3.mate = f32[2,16,512]{2,1,0:T(8,128)S(1)} collective-permute-done((f32[2,16,512]{2,1,0:T(8,128)S(1)}, f32[2,16,512]{2,1,0:T(8,128)S(1)}, u32[]{:S(2)}, u32[]{:S(2)}) %collective-permute-start.3) | collective-permute-done | bytes 65568 | tf_op jit(solution)/shard_map/ppermute | solution.py:285
  38.3 0.0 collective-permute-done.4.refs_2_
  38.4 0.0 collective-permute-done.5.refs_3_
  38.4 2.7 %middle.1 = (f32[2,16,512]{2,1,0:T(8,128)}, bf16[2,16,512]{2,1,0:T(8,128)(2,1)S(1)}, bf16[32,512]{1,0:T(8,128)(2,1)S(1)}, bf16[16,32,128]{2,1,0:T(8,128)(2,1)S(1)}) custom-call(bf16[32,16,128]{2,1,0:T(8,128)(2,1)S(1)} %all-to-all-done.1.recv, bf16[2,256,2048]{2,1,0:T(8,128)(2,1)S(1)} %copy-done, bf16[2,256,512]{2,1,0:T(8,128)(2,1)S(1)} %copy-done.1, ...), custom_call_target="tpu_custom_call" | custom-call | tf_op jit(solution)/shard_map/middle/pallas_call | solution.py:287
  41.1 13.1 %all_to_all.21.recv = bf16[16,32,128]{2,1,0:T(8,128)(2,1)S(1)} all-to-all(bf16[16,32,128]{2,1,0:T(8,128)(2,1)S(1)} %get-tuple-element.13), channel_id=1, replica_groups={{18,16,22,20,26,24,30,28,14,12,10,8,6,4,2,0},{19,17,23,21,27,25,31,29,1..., dimensions={0} | all-to-all | bytes 262144 | tf_op jit(solution)/shard_map/all_to_all | solution.py:213
  54.2 0.9 %collective-permute-start.7 = (bf16[16,32,128]{2,1,0:T(8,128)(2,1)S(1)}, bf16[16,32,128]{2,1,0:T(8,128)(2,1)S(1)}, u32[]{:S(2)}, u32[]{:S(2)}) collective-permute-start(bf16[16,32,128]{2,1,0:T(8,128)(2,1)S(1)} %all_to_all.21.recv), channel_id=1, source_target_pairs={{0,1},{1,0},{2,3},{3,2},{4,5},{5,4},{6,7},{7,6},{8,9},{9,8},{10,11... | collective-permute-start | bytes 393224 | tf_op jit(solution)/shard_map/ppermute | solution.py:246
  55.2 0.7 shard_map.105
  55.8 6.8 %all-to-all-start.3 = ((bf16[32,16,128]{2,1,0:T(8,128)(2,1)}), bf16[32,16,128]{2,1,0:T(8,128)(2,1)S(1)}, u32[]{:S(2)}, u32[]{:S(2)}) async-start(bf16[32,16,128]{2,1,0:T(8,128)(2,1)} %shard_map.105), calls=%async_computation.3 | async-start | bytes 262144 | tf_op jit(solution)/shard_map/all_to_all | solution.py:213
  62.6 3.5 %collective-permute-start.6 = (bf16[2,16,512]{2,1,0:T(8,128)(2,1)S(1)}, bf16[2,16,512]{2,1,0:T(8,128)(2,1)S(1)}, u32[]{:S(2)}, u32[]{:S(2)}) collective-permute-start(bf16[2,16,512]{2,1,0:T(8,128)(2,1)S(1)} %get-tuple-element.15.vec), channel_id=1, source_target_pairs={{1,2},{3,4},{5,6},{7,8},{9,10},{11,12},{13,14},{15,16},{17,18},{19... | collective-permute-start | bytes 98312 | tf_op jit(solution)/shard_map/ppermute | solution.py:230
  66.2 2.3 %near_terms.3.near = f32[2,16,512]{2,1,0:T(8,128)S(1)} custom-call(bf16[32,512]{1,0:T(8,128)(2,1)S(1)} %get-tuple-element.14.got, bf16[2,16,512]{2,1,0:T(8,128)(2,1)S(1)} %get-tuple-element.15.vec, bf16[3,2,512,512]{3,2,1,0:T(8,128)(2,1)} %blocks_hbm.7), custom_call_target="tpu_custom_call" | custom-call | tf_op jit(solution)/shard_map/near_terms/pallas_call | solution.py:234
  68.5 0.0 collective-permute-done.6.cross
  68.5 0.0 collective-permute-done.7.other
  68.5 2.3 %local_terms.3.local = f32[2,16,512]{2,1,0:T(8,128)S(1)} custom-call(f32[2,16,512]{2,1,0:T(8,128)S(1)} %near_terms.3.near, bf16[2,16,512]{2,1,0:T(8,128)(2,1)S(1)} %collective-permute-done.6.cross, bf16[16,32,128]{2,1,0:T(8,128)(2,1)S(1)} %all_to_all.21.recv, bf16[16,32,128]{2,1,0:T(8,128)(2,1)S(1)} %collective-permute-done.7.other, ...), custom_call_target="tpu_custom_call" | custom-call | tf_op jit(solution)/shard_map/local_terms/pallas_call | solution.py:247
  70.9 1.6 %shard_map.106 = f32[2,16,512]{2,1,0:T(8,128)} custom-call(bf16[32,16,128]{2,1,0:T(8,128)(2,1)S(1)} %all-to-all-done.3.recv, bf16[2,256,2048]{2,1,0:T(8,128)(2,1)S(1)} %copy-done, bf16[2,256,512]{2,1,0:T(8,128)(2,1)S(1)} %copy-done.1, f32[2,16,512]{2,1,0:T(8,128)S(1)} %local_terms.3.local), custom_call_target="tpu_custom_call" | custom-call | tf_op jit(solution)/shard_map/pallas_call | solution.py:207
  (4 shorter events, 0.0 us)
Async XLA Ops:
  0.6 37.7 %collective-permute-start.4 = (bf16[2,256,512]{2,1,0:T(8,128)(2,1)}, bf16[2,256,512]{2,1,0:T(8,128)(2,1)}, u32[]{:S(2)}, u32[]{:S(2)}) collective-permute-start(bf16[2,256,512]{2,1,0:T(8,128)(2,1)} %refs_1_.1), channel_id=1, source_target_pairs={{0,1},{1,0},{2,3},{3,2},{4,5},{5,4},{6,7},{7,6},{8,9},{9,8},{10,11... | collective-permute-start | bytes 1572872 | tf_op jit(solution)/shard_map/ppermute | solution.py:281
  3.9 34.4 %collective-permute-start.5 = (bf16[2,256,512]{2,1,0:T(8,128)(2,1)}, bf16[2,256,512]{2,1,0:T(8,128)(2,1)}, u32[]{:S(2)}, u32[]{:S(2)}) collective-permute-start(bf16[2,256,512]{2,1,0:T(8,128)(2,1)} %expand.3), channel_id=1, source_target_pairs={{0,1},{1,0},{2,3},{3,2},{4,5},{5,4},{6,7},{7,6},{8,9},{9,8},{10,11... | collective-permute-start | bytes 1572872 | tf_op jit(solution)/shard_map/ppermute | solution.py:281
  5.5 1.4 %collective-permute-start = (bf16[160,128]{1,0:T(8,128)(2,1)S(1)}, bf16[160,128]{1,0:T(8,128)(2,1)S(1)}, u32[]{:S(2)}, u32[]{:S(2)}) collective-permute-start(bf16[160,128]{1,0:T(8,128)(2,1)S(1)} %get-tuple-element.9), channel_id=1, source_target_pairs={{0,1},{1,0},{2,3},{3,2},{4,5},{5,4},{6,7},{7,6},{8,9},{9,8},{10,11... | collective-permute-start | bytes 122888 | tf_op jit(solution)/shard_map/ppermute | solution.py:217
  19.6 15.1 %collective-permute-start.2 = (bf16[16,32,128]{2,1,0:T(8,128)(2,1)S(1)}, bf16[16,32,128]{2,1,0:T(8,128)(2,1)S(1)}, u32[]{:S(2)}, u32[]{:S(2)}) collective-permute-start(bf16[16,32,128]{2,1,0:T(8,128)(2,1)S(1)} %all_to_all.20.recv), channel_id=1, source_target_pairs={{0,1},{1,0},{2,3},{3,2},{4,5},{5,4},{6,7},{7,6},{8,9},{9,8},{10,11... | collective-permute-start | bytes 393224 | tf_op jit(solution)/shard_map/ppermute | solution.py:246
  21.4 15.7 %all-to-all-start.1 = ((bf16[32,16,128]{2,1,0:T(8,128)(2,1)}), bf16[32,16,128]{2,1,0:T(8,128)(2,1)S(1)}, u32[]{:S(2)}, u32[]{:S(2)}) async-start(bf16[32,16,128]{2,1,0:T(8,128)(2,1)} %shard_map.104), calls=%async_computation.1 | async-start | bytes 262144 | tf_op jit(solution)/shard_map/all_to_all | solution.py:213
  28.5 6.1 %collective-permute-start.1 = (bf16[2,16,512]{2,1,0:T(8,128)(2,1)}, bf16[2,16,512]{2,1,0:T(8,128)(2,1)S(1)}, u32[]{:S(2)}, u32[]{:S(2)}) collective-permute-start(bf16[2,16,512]{2,1,0:T(8,128)(2,1)} %probes.1), channel_id=1, source_target_pairs={{1,2},{3,4},{5,6},{7,8},{9,10},{11,12},{13,14},{15,16},{17,18},{19... | collective-permute-start | bytes 98312 | tf_op jit(solution)/shard_map/ppermute | solution.py:230
  32.1 6.3 %copy-start = (bf16[2,256,2048]{2,1,0:T(8,128)(2,1)S(1)}, bf16[2,256,2048]{2,1,0:T(8,128)(2,1)}, u32[]{:S(2)}) copy-start(bf16[2,256,2048]{2,1,0:T(8,128)(2,1)} %coupling.3) | copy-start | bytes 6291460
  32.1 6.3 %copy-start.1 = (bf16[2,256,512]{2,1,0:T(8,128)(2,1)S(1)}, bf16[2,256,512]{2,1,0:T(8,128)(2,1)}, u32[]{:S(2)}) copy-start(bf16[2,256,512]{2,1,0:T(8,128)(2,1)} %expand.3) | copy-start | bytes 1572868
  37.0 1.3 %collective-permute-start.3 = (f32[2,16,512]{2,1,0:T(8,128)S(1)}, f32[2,16,512]{2,1,0:T(8,128)S(1)}, u32[]{:S(2)}, u32[]{:S(2)}) collective-permute-start(f32[2,16,512]{2,1,0:T(8,128)S(1)} %local_terms.2.local), channel_id=1, source_target_pairs={{0,1},{1,0},{2,3},{3,2},{4,5},{5,4},{6,7},{7,6},{8,9},{9,8},{10,11... | collective-permute-start | bytes 196616 | tf_op jit(solution)/shard_map/ppermute | solution.py:285
  54.2 14.3 %collective-permute-start.7 = (bf16[16,32,128]{2,1,0:T(8,128)(2,1)S(1)}, bf16[16,32,128]{2,1,0:T(8,128)(2,1)S(1)}, u32[]{:S(2)}, u32[]{:S(2)}) collective-permute-start(bf16[16,32,128]{2,1,0:T(8,128)(2,1)S(1)} %all_to_all.21.recv), channel_id=1, source_target_pairs={{0,1},{1,0},{2,3},{3,2},{4,5},{5,4},{6,7},{7,6},{8,9},{9,8},{10,11... | collective-permute-start | bytes 393224 | tf_op jit(solution)/shard_map/ppermute | solution.py:246
  55.8 15.0 %all-to-all-start.3 = ((bf16[32,16,128]{2,1,0:T(8,128)(2,1)}), bf16[32,16,128]{2,1,0:T(8,128)(2,1)S(1)}, u32[]{:S(2)}, u32[]{:S(2)}) async-start(bf16[32,16,128]{2,1,0:T(8,128)(2,1)} %shard_map.105), calls=%async_computation.3 | async-start | bytes 262144 | tf_op jit(solution)/shard_map/all_to_all | solution.py:213
  62.6 5.8 %collective-permute-start.6 = (bf16[2,16,512]{2,1,0:T(8,128)(2,1)S(1)}, bf16[2,16,512]{2,1,0:T(8,128)(2,1)S(1)}, u32[]{:S(2)}, u32[]{:S(2)}) collective-permute-start(bf16[2,16,512]{2,1,0:T(8,128)(2,1)S(1)} %get-tuple-element.15.vec), channel_id=1, source_target_pairs={{1,2},{3,4},{5,6},{7,8},{9,10},{11,12},{13,14},{15,16},{17,18},{19... | collective-permute-start | bytes 98312 | tf_op jit(solution)/shard_map/ppermute | solution.py:230

commit v7 on v6

--- a/solution.py
+++ b/solution.py
@@ -8,7 +8,8 @@
 ALL = ("region", "blk")
 CHIP_ORDER = tuple(2 * z + y for z in (4, 5, 6, 7, 3, 2, 1, 0) for y in (1, 0))
 CHIPS = [[32 * r + 2 * i + c for i in CHIP_ORDER] for r in range(8) for c in range(2)]
-PLANE = [[32 * r + 4 * z + q for r in range(8) for q in range(4)] for z in range(8)]
+PLANE_ORDER = tuple(4 * (4 * h + x) + 2 * y + c for x in (2, 3, 1, 0) for h, y in ((1, 0), (1, 1), (0, 1), (0, 0)) for c in (1, 0))
+PLANE = [[32 * (k // 4) + 4 * z + k % 4 for k in PLANE_ORDER] for z in range(8)]
 PARTNER = [(d, d ^ 1) for d in range(256)]
 CROSS = [(d, d + 1) for d in range(256) if d % 2 == 1 and d % 32 != 31]
 CROSS += [(d, d - 1) for d in range(256) if d % 2 == 0 and d % 32 != 0]
@@ -135,7 +136,7 @@
     region = lax.axis_index("region")
     res, ims = [], []
     for s in range(8):
-        tiles = [jnp.where(s != region, recv[4 * s + q], jnp.zeros((16, 128), bf16)) for q in range(4)]
+        tiles = [jnp.where(s != region, recv[PLANE_ORDER.index(4 * s + q)], jnp.zeros((16, 128), bf16)) for q in range(4)]
         res += tiles[:2]
         ims += tiles[2:]
     rows = jnp.concatenate([jnp.concatenate(res, 1), jnp.concatenate(ims, 1)], 0)

time: 73 us -> 74 us (1.014)
  the two profiles are of different devices: /device:TPU:1 before, /device:TPU:32 now
where the time goes in v7:
time: 74 us; the launch traced here: 72.8 us
  blocking collectives  27.8 us (38%)
  starting transfers between devices  21.4 us (29%)
  Pallas kernels  16.5 us (22%)
  waiting for transfers between devices  5.57 us (8%)
  between operations  1.43 us (2%)
    all_to_all x2, blocking collectives, exchange(): lax.all_to_all(value, ALL, split_axis=0, concat_axis=0, axis_index_groups...  27.8 us
    all_to_all x2, starting transfers between devices, exchange(): lax.all_to_all(value, ALL, split_axis=0, concat_axis=0, axis_index_groups...  16.6 us
    pallas_call x2, Pallas kernels, near_terms(): pl.pallas_call(near_kernel, in_specs=vmem(2) + [ANY], out_specs=vmem(1)[0...  4.72 us
    pallas_call x2, Pallas kernels, local_terms(): pl.pallas_call(terms_kernel, in_specs=vmem(4) + [ANY] * 3, out_specs=vmem...  4.67 us
    ppermute x2, waiting for transfers between devices, crossed(): return lax.ppermute(vec, ALL, CROSS)  3.86 us
    ppermute x2, starting transfers between devices, crossed(): return lax.ppermute(vec, ALL, CROSS)  3.84 us
    pallas_call x3, Pallas kernels, call(): pl.pallas_call(kernel, in_specs=vmem(len(args)), out_specs=vmem(len(outs)...  2.99 us
    pallas_call x1, Pallas kernels, local(): pl.pallas_call(middle_kernel, in_specs=vmem(5) + [RANKS] + [ANY] * 4, out...  2.69 us
  transfers between devices with their start and end apart: 10, of which 4 were waited for; matrix products, arithmetic and copies ran while one was open for 0% of the time, Pallas kernels for 17%

profile of v7, /device:TPU:32, one launch (start us, length us, event | category | flops | bytes accessed | tf_op | source)
XLA Modules:
  0.0 72.8 jit_solution(18195425431373680550)
XLA Ops:
  0.6 0.1 collective-permute-start.4
  0.7 0.5 collective-permute-start.5
  1.2 1.5 %start.1 = (bf16[160,128]{1,0:T(8,128)(2,1)S(1)}, f32[48,128]{1,0:T(8,128)S(1)}, bf16[2,16,512]{2,1,0:T(8,128)(2,1)S(1)}) custom-call(bf16[2,16,512]{2,1,0:T(8,128)(2,1)} %probes.1, bf16[2,64,512]{2,1,0:T(8,128)(2,1)} %refs_0_.1, bf16[2,256,512]{2,1,0:T(8,128)(2,1)} %refs_1_.1), custom_call_target="tpu_custom_call" | custom-call | tf_op jit(solution)/shard_map/start/pallas_call | solution.py:271
  2.7 0.2 collective-permute-start
  3.5 0.5 collective-permute-done.got
  4.0 14.7 %all_to_all.20.recv = bf16[16,32,128]{2,1,0:T(8,128)(2,1)S(1)} all-to-all(bf16[16,32,128]{2,1,0:T(8,128)(2,1)S(1)} %pair_sums.1), channel_id=1, replica_groups={{18,16,22,20,26,24,30,28,14,12,10,8,6,4,2,0},{19,17,23,21,27,25,31,29,1..., dimensions={0} | all-to-all | bytes 262144 | tf_op jit(solution)/shard_map/all_to_all | solution.py:214
  18.7 0.0 collective-permute-start.2
  18.7 0.7 shard_map.104
  19.4 9.4 %all-to-all-start.1 = ((bf16[32,16,128]{2,1,0:T(8,128)(2,1)}), bf16[32,16,128]{2,1,0:T(8,128)(2,1)S(1)}, u32[]{:S(2)}, u32[]{:S(2)}) async-start(bf16[32,16,128]{2,1,0:T(8,128)(2,1)} %shard_map.104), calls=%async_computation.1 | async-start | bytes 262144 | tf_op jit(solution)/shard_map/all_to_all | solution.py:214
  28.8 1.9 %collective-permute-start.1 = (bf16[2,16,512]{2,1,0:T(8,128)(2,1)}, bf16[2,16,512]{2,1,0:T(8,128)(2,1)S(1)}, u32[]{:S(2)}, u32[]{:S(2)}) collective-permute-start(bf16[2,16,512]{2,1,0:T(8,128)(2,1)} %probes.1), channel_id=1, source_target_pairs={{1,2},{3,4},{5,6},{7,8},{9,10},{11,12},{13,14},{15,16},{17,18},{19... | collective-permute-start | bytes 98312 | tf_op jit(solution)/shard_map/ppermute | solution.py:231
  30.7 0.0 copy-start
  30.7 0.0 copy-start.1
  30.7 2.4 %near_terms.2.near = f32[2,16,512]{2,1,0:T(8,128)S(1)} custom-call(bf16[160,128]{1,0:T(8,128)(2,1)S(1)} %collective-permute-done.got, bf16[2,16,512]{2,1,0:T(8,128)(2,1)S(1)} %get-tuple-element.11.vec, bf16[3,2,512,512]{3,2,1,0:T(8,128)(2,1)} %blocks_hbm.7), custom_call_target="tpu_custom_call" | custom-call | tf_op jit(solution)/shard_map/near_terms/pallas_call | solution.py:235
  33.2 2.0 %collective-permute-done.1.cross = bf16[2,16,512]{2,1,0:T(8,128)(2,1)S(1)} collective-permute-done((bf16[2,16,512]{2,1,0:T(8,128)(2,1)}, bf16[2,16,512]{2,1,0:T(8,128)(2,1)S(1)}, u32[]{:S(2)}, u32[]{:S(2)}) %collective-permute-start.1) | collective-permute-done | bytes 32800 | tf_op jit(solution)/shard_map/ppermute | solution.py:231
  35.1 0.0 collective-permute-done.2.other
  35.1 2.3 %local_terms.2.local = f32[2,16,512]{2,1,0:T(8,128)S(1)} custom-call(f32[2,16,512]{2,1,0:T(8,128)S(1)} %near_terms.2.near, bf16[2,16,512]{2,1,0:T(8,128)(2,1)S(1)} %collective-permute-done.1.cross, bf16[16,32,128]{2,1,0:T(8,128)(2,1)S(1)} %all_to_all.20.recv, bf16[16,32,128]{2,1,0:T(8,128)(2,1)S(1)} %collective-permute-done.2.other, ...), custom_call_target="tpu_custom_call" | custom-call | tf_op jit(solution)/shard_map/local_terms/pallas_call | solution.py:248
  37.5 0.1 collective-permute-start.3
  37.6 0.0 all-to-all-done.1.recv
  37.6 1.2 %collective-permute-done.3.mate = f32[2,16,512]{2,1,0:T(8,128)S(1)} collective-permute-done((f32[2,16,512]{2,1,0:T(8,128)S(1)}, f32[2,16,512]{2,1,0:T(8,128)S(1)}, u32[]{:S(2)}, u32[]{:S(2)}) %collective-permute-start.3) | collective-permute-done | bytes 65568 | tf_op jit(solution)/shard_map/ppermute | solution.py:286
  38.8 0.0 collective-permute-done.4.refs_2_
  38.8 0.0 collective-permute-done.5.refs_3_
  38.8 2.7 %middle.1 = (f32[2,16,512]{2,1,0:T(8,128)}, bf16[2,16,512]{2,1,0:T(8,128)(2,1)S(1)}, bf16[32,512]{1,0:T(8,128)(2,1)S(1)}, bf16[16,32,128]{2,1,0:T(8,128)(2,1)S(1)}) custom-call(bf16[32,16,128]{2,1,0:T(8,128)(2,1)S(1)} %all-to-all-done.1.recv, bf16[2,256,2048]{2,1,0:T(8,128)(2,1)S(1)} %copy-done, bf16[2,256,512]{2,1,0:T(8,128)(2,1)S(1)} %copy-done.1, ...), custom_call_target="tpu_custom_call" | custom-call | tf_op jit(solution)/shard_map/middle/pallas_call | solution.py:288
  41.5 13.1 %all_to_all.21.recv = bf16[16,32,128]{2,1,0:T(8,128)(2,1)S(1)} all-to-all(bf16[16,32,128]{2,1,0:T(8,128)(2,1)S(1)} %get-tuple-element.13), channel_id=1, replica_groups={{18,16,22,20,26,24,30,28,14,12,10,8,6,4,2,0},{19,17,23,21,27,25,31,29,1..., dimensions={0} | all-to-all | bytes 262144 | tf_op jit(solution)/shard_map/all_to_all | solution.py:214
  54.7 0.0 collective-permute-start.7
  54.7 0.7 shard_map.105
  55.4 7.3 %all-to-all-start.3 = ((bf16[32,16,128]{2,1,0:T(8,128)(2,1)}), bf16[32,16,128]{2,1,0:T(8,128)(2,1)S(1)}, u32[]{:S(2)}, u32[]{:S(2)}) async-start(bf16[32,16,128]{2,1,0:T(8,128)(2,1)} %shard_map.105), calls=%async_computation.3 | async-start | bytes 262144 | tf_op jit(solution)/shard_map/all_to_all | solution.py:214
  62.6 1.9 %collective-permute-start.6 = (bf16[2,16,512]{2,1,0:T(8,128)(2,1)S(1)}, bf16[2,16,512]{2,1,0:T(8,128)(2,1)S(1)}, u32[]{:S(2)}, u32[]{:S(2)}) collective-permute-start(bf16[2,16,512]{2,1,0:T(8,128)(2,1)S(1)} %get-tuple-element.15.vec), channel_id=1, source_target_pairs={{1,2},{3,4},{5,6},{7,8},{9,10},{11,12},{13,14},{15,16},{17,18},{19... | collective-permute-start | bytes 98312 | tf_op jit(solution)/shard_map/ppermute | solution.py:231
  64.6 2.3 %near_terms.3.near = f32[2,16,512]{2,1,0:T(8,128)S(1)} custom-call(bf16[32,512]{1,0:T(8,128)(2,1)S(1)} %get-tuple-element.14.got, bf16[2,16,512]{2,1,0:T(8,128)(2,1)S(1)} %get-tuple-element.15.vec, bf16[3,2,512,512]{3,2,1,0:T(8,128)(2,1)} %blocks_hbm.7), custom_call_target="tpu_custom_call" | custom-call | tf_op jit(solution)/shard_map/near_terms/pallas_call | solution.py:235
  66.9 1.9 %collective-permute-done.6.cross = bf16[2,16,512]{2,1,0:T(8,128)(2,1)S(1)} collective-permute-done((bf16[2,16,512]{2,1,0:T(8,128)(2,1)S(1)}, bf16[2,16,512]{2,1,0:T(8,128)(2,1)S(1)}, u32[]{:S(2)}, u32[]{:S(2)}) %collective-permute-start.6) | collective-permute-done | bytes 32800 | tf_op jit(solution)/shard_map/ppermute | solution.py:231
  68.8 0.0 collective-permute-done.7.other
  68.8 2.3 %local_terms.3.local = f32[2,16,512]{2,1,0:T(8,128)S(1)} custom-call(f32[2,16,512]{2,1,0:T(8,128)S(1)} %near_terms.3.near, bf16[2,16,512]{2,1,0:T(8,128)(2,1)S(1)} %collective-permute-done.6.cross, bf16[16,32,128]{2,1,0:T(8,128)(2,1)S(1)} %all_to_all.21.recv, bf16[16,32,128]{2,1,0:T(8,128)(2,1)S(1)} %collective-permute-done.7.other, ...), custom_call_target="tpu_custom_call" | custom-call | tf_op jit(solution)/shard_map/local_terms/pallas_call | solution.py:248
  71.1 1.6 %shard_map.106 = f32[2,16,512]{2,1,0:T(8,128)} custom-call(bf16[32,16,128]{2,1,0:T(8,128)(2,1)S(1)} %all-to-all-done.3.recv, bf16[2,256,2048]{2,1,0:T(8,128)(2,1)S(1)} %copy-done, bf16[2,256,512]{2,1,0:T(8,128)(2,1)S(1)} %copy-done.1, f32[2,16,512]{2,1,0:T(8,128)S(1)} %local_terms.3.local), custom_call_target="tpu_custom_call" | custom-call | tf_op jit(solution)/shard_map/pallas_call | solution.py:208
  (4 shorter events, 0.0 us)
Async XLA Ops:
  0.6 38.2 %collective-permute-start.4 = (bf16[2,256,512]{2,1,0:T(8,128)(2,1)}, bf16[2,256,512]{2,1,0:T(8,128)(2,1)}, u32[]{:S(2)}, u32[]{:S(2)}) collective-permute-start(bf16[2,256,512]{2,1,0:T(8,128)(2,1)} %refs_1_.1), channel_id=1, source_target_pairs={{0,1},{1,0},{2,3},{3,2},{4,5},{5,4},{6,7},{7,6},{8,9},{9,8},{10,11... | collective-permute-start | bytes 1572872 | tf_op jit(solution)/shard_map/ppermute | solution.py:282
  0.7 38.1 %collective-permute-start.5 = (bf16[2,256,512]{2,1,0:T(8,128)(2,1)}, bf16[2,256,512]{2,1,0:T(8,128)(2,1)}, u32[]{:S(2)}, u32[]{:S(2)}) collective-permute-start(bf16[2,256,512]{2,1,0:T(8,128)(2,1)} %expand.3), channel_id=1, source_target_pairs={{0,1},{1,0},{2,3},{3,2},{4,5},{5,4},{6,7},{7,6},{8,9},{9,8},{10,11... | collective-permute-start | bytes 1572872 | tf_op jit(solution)/shard_map/ppermute | solution.py:282
  2.7 1.3 %collective-permute-start = (bf16[160,128]{1,0:T(8,128)(2,1)S(1)}, bf16[160,128]{1,0:T(8,128)(2,1)S(1)}, u32[]{:S(2)}, u32[]{:S(2)}) collective-permute-start(bf16[160,128]{1,0:T(8,128)(2,1)S(1)} %get-tuple-element.9), channel_id=1, source_target_pairs={{0,1},{1,0},{2,3},{3,2},{4,5},{5,4},{6,7},{7,6},{8,9},{9,8},{10,11... | collective-permute-start | bytes 122888 | tf_op jit(solution)/shard_map/ppermute | solution.py:218
  18.7 16.4 %collective-permute-start.2 = (bf16[16,32,128]{2,1,0:T(8,128)(2,1)S(1)}, bf16[16,32,128]{2,1,0:T(8,128)(2,1)S(1)}, u32[]{:S(2)}, u32[]{:S(2)}) collective-permute-start(bf16[16,32,128]{2,1,0:T(8,128)(2,1)S(1)} %all_to_all.20.recv), channel_id=1, source_target_pairs={{0,1},{1,0},{2,3},{3,2},{4,5},{5,4},{6,7},{7,6},{8,9},{9,8},{10,11... | collective-permute-start | bytes 393224 | tf_op jit(solution)/shard_map/ppermute | solution.py:247
  19.4 18.2 %all-to-all-start.1 = ((bf16[32,16,128]{2,1,0:T(8,128)(2,1)}), bf16[32,16,128]{2,1,0:T(8,128)(2,1)S(1)}, u32[]{:S(2)}, u32[]{:S(2)}) async-start(bf16[32,16,128]{2,1,0:T(8,128)(2,1)} %shard_map.104), calls=%async_computation.1 | async-start | bytes 262144 | tf_op jit(solution)/shard_map/all_to_all | solution.py:214
  28.8 6.3 %collective-permute-start.1 = (bf16[2,16,512]{2,1,0:T(8,128)(2,1)}, bf16[2,16,512]{2,1,0:T(8,128)(2,1)S(1)}, u32[]{:S(2)}, u32[]{:S(2)}) collective-permute-start(bf16[2,16,512]{2,1,0:T(8,128)(2,1)} %probes.1), channel_id=1, source_target_pairs={{1,2},{3,4},{5,6},{7,8},{9,10},{11,12},{13,14},{15,16},{17,18},{19... | collective-permute-start | bytes 98312 | tf_op jit(solution)/shard_map/ppermute | solution.py:231
  30.7 8.1 %copy-start = (bf16[2,256,2048]{2,1,0:T(8,128)(2,1)S(1)}, bf16[2,256,2048]{2,1,0:T(8,128)(2,1)}, u32[]{:S(2)}) copy-start(bf16[2,256,2048]{2,1,0:T(8,128)(2,1)} %coupling.3) | copy-start | bytes 6291460
  30.7 8.1 %copy-start.1 = (bf16[2,256,512]{2,1,0:T(8,128)(2,1)S(1)}, bf16[2,256,512]{2,1,0:T(8,128)(2,1)}, u32[]{:S(2)}) copy-start(bf16[2,256,512]{2,1,0:T(8,128)(2,1)} %expand.3) | copy-start | bytes 1572868
  37.5 1.3 %collective-permute-start.3 = (f32[2,16,512]{2,1,0:T(8,128)S(1)}, f32[2,16,512]{2,1,0:T(8,128)S(1)}, u32[]{:S(2)}, u32[]{:S(2)}) collective-permute-start(f32[2,16,512]{2,1,0:T(8,128)S(1)} %local_terms.2.local), channel_id=1, source_target_pairs={{0,1},{1,0},{2,3},{3,2},{4,5},{5,4},{6,7},{7,6},{8,9},{9,8},{10,11... | collective-permute-start | bytes 196616 | tf_op jit(solution)/shard_map/ppermute | solution.py:286
  54.7 14.1 %collective-permute-start.7 = (bf16[16,32,128]{2,1,0:T(8,128)(2,1)S(1)}, bf16[16,32,128]{2,1,0:T(8,128)(2,1)S(1)}, u32[]{:S(2)}, u32[]{:S(2)}) collective-permute-start(bf16[16,32,128]{2,1,0:T(8,128)(2,1)S(1)} %all_to_all.21.recv), channel_id=1, source_target_pairs={{0,1},{1,0},{2,3},{3,2},{4,5},{5,4},{6,7},{7,6},{8,9},{9,8},{10,11... | collective-permute-start | bytes 393224 | tf_op jit(solution)/shard_map/ppermute | solution.py:247
  55.4 15.8 %all-to-all-start.3 = ((bf16[32,16,128]{2,1,0:T(8,128)(2,1)}), bf16[32,16,128]{2,1,0:T(8,128)(2,1)S(1)}, u32[]{:S(2)}, u32[]{:S(2)}) async-start(bf16[32,16,128]{2,1,0:T(8,128)(2,1)} %shard_map.105), calls=%async_computation.3 | async-start | bytes 262144 | tf_op jit(solution)/shard_map/all_to_all | solution.py:214
  62.6 6.1 %collective-permute-start.6 = (bf16[2,16,512]{2,1,0:T(8,128)(2,1)S(1)}, bf16[2,16,512]{2,1,0:T(8,128)(2,1)S(1)}, u32[]{:S(2)}, u32[]{:S(2)}) collective-permute-start(bf16[2,16,512]{2,1,0:T(8,128)(2,1)S(1)} %get-tuple-element.15.vec), channel_id=1, source_target_pairs={{1,2},{3,4},{5,6},{7,8},{9,10},{11,12},{13,14},{15,16},{17,18},{19... | collective-permute-start | bytes 98312 | tf_op jit(solution)/shard_map/ppermute | solution.py:231
